TPU v7x, 32 devices: a whole 2x2x4 slice. The times are simulated.
32 devices in a mesh: group: 4 (over x, core), dev: 8 (over z, y).
Axes of the slice: x: 2, y: 2, z: 4, core: 2. Of those that a mesh axis runs over, the one named last changes fastest.
Arguments:
- adjoint_seed: bfloat16 [64, 3, 48, 16, 128], P(('group', 'dev')), may hold values from -6 to 6
- stiffness: float32 [64, 48, 16, 128], P(('group', 'dev')), may hold values from 0.1 to 0.4
- lengths: int32 [64], P(('group', 'dev')), may hold values from 24 to 48, as said below
- conn_lower: int32 [64, 3], P(('group', 'dev')), may hold values from -1 to 7, as said below
- conn_upper: int32 [64, 3], P(('group', 'dev')), may hold values from -1 to 7, as said below
- coord_x: float32 [64, 48], P(('group', 'dev')), may hold values from 0 to 95
- coord_y: float32 [64, 16], P(('group', 'dev')), may hold values from 0 to 63
- coord_z: float32 [64, 128], P(('group', 'dev')), may hold values from 0 to 31
Outputs:
- adjoint_field: float32 [64, 3, 48, 16, 128], P(('group', 'dev'))
- lattice_grad: float32 [96, 6144], P('dev')
Inputs may be any that keep to these rules, and one draw needn't show every extreme that they name: `conn_lower`: each row names, within the same cluster of 16 blocks, the device index along dev and the slot of the block whose upper face meets this block's lower face (first entry -1 for a wall, then 0 and 0), and 1 in the third entry where that face is reversed along the second grid dimension. A cluster's links form one chain through all its blocks; each link appears mirrored in conn_upper with the same orientation. `conn_upper`: likewise for the block across the upper face, whose lower face it meets. `lengths`: in every cluster some block has 48 active rows and some 48 // 2.
All inputs are finite; a program needn't handle non-finite values.
Results may differ from a plain program's by a relative error of at most 0.0003.
Values sent between devices are 32-bit elements; how exact they have to be, the bound alone decides.
No kernel may reach another device: no remote copies, remote signals or barrier semaphores. Data moves between devices by JAX's collectives and lax.ppermute only.
A program may use at most 64 MiB of HBM per device.

v0:
```python
import math

import jax
import jax.numpy as jnp
from jax import lax
from jax.sharding import PartitionSpec as P

CX = 48
CY = 16
CZ = 128
LX = 96
LY = 64
LZ = 32
SWEEPS = 2


TAPS = [
    (shift_x, shift_y, shift_z, 1.0 / (shift_x * shift_x + shift_y * shift_y + shift_z * shift_z))
    for shift_x in (-1, 0, 1)
    for shift_y in (-1, 0, 1)
    for shift_z in (-1, 0, 1)
    if (shift_x, shift_y, shift_z) != (0, 0, 0)
]
DOMINANCE = 1.25


def stencil(padded, count_x, count_y, count_z):
    running = None
    for shift_x, shift_y, shift_z, factor in TAPS:
        window = padded[
            :,
            1 + shift_x : 1 + shift_x + count_x,
            1 + shift_y : 1 + shift_y + count_y,
            1 + shift_z : 1 + shift_z + count_z,
        ]
        running = factor * window if running is None else running + factor * window
    return running


def extend(values, lower_halo, upper_halo, length):
    zero_row = jnp.zeros_like(lower_halo)[:, None]
    joined = jnp.concatenate([lower_halo[:, None], values, zero_row], axis=1)
    joined = lax.dynamic_update_slice(
        joined, upper_halo[:, None], (jnp.int32(0), length + 1, jnp.int32(0), jnp.int32(0))
    )
    return jnp.pad(joined, ((0, 0), (0, 0), (1, 1), (1, 1)))


def end_faces(values, lengths):
    lower_face = values[:, :, 0]
    upper_face = jax.vmap(
        lambda block_values, length: lax.dynamic_index_in_dim(
            block_values, length - 1, axis=1, keepdims=False
        )
    )(values, lengths)
    return jnp.stack([lower_face, upper_face], axis=1)


def partner_tiles(face_tiles, links, side, slots):
    partner = jnp.maximum(links[:, 0], 0) * slots + links[:, 1]
    chosen = face_tiles[partner, side]
    mirrored = chosen[..., ::-1, :]
    turned = jnp.where((links[:, 2] == 1)[:, None, None, None], mirrored, chosen)
    return jnp.where((links[:, 0] >= 0)[:, None, None, None], turned, jnp.zeros_like(turned))


def hat(coords, points):
    grid_points = jnp.arange(points, dtype=jnp.float32)[None, :, None]
    return jnp.maximum(0.0, 1.0 - jnp.abs(grid_points - coords[:, None, :]))


def on_device(adjoint_seed, stiffness, lengths, conn_lower, conn_upper, coord_x, coord_y, coord_z):
    slots = stiffness.shape[0]
    active = (jnp.arange(CX, dtype=jnp.int32)[None, :] < lengths[:, None]).astype(jnp.float32)[
        :, :, None, None
    ]
    stiff_masked = stiffness * active
    stiff_tiles = lax.all_gather(
        end_faces(stiff_masked[:, None], lengths), "dev", axis=0, tiled=True
    )
    stiff_lower = partner_tiles(stiff_tiles, conn_lower, 1, slots)
    stiff_upper = partner_tiles(stiff_tiles, conn_upper, 0, slots)

    def diagonal_one(stiff_block, lower_halo, upper_halo, length):
        near = stencil(extend(stiff_block[None], lower_halo, upper_halo, length), CX, CY, CZ)[0]
        return DOMINANCE * stiff_block * near

    diagonal = jax.vmap(diagonal_one)(stiff_masked, stiff_lower, stiff_upper, lengths)
    safe = jnp.where(active > 0, diagonal, jnp.ones_like(diagonal))
    source = adjoint_seed.astype(jnp.float32) * active[:, None]
    adjoint = source / safe[:, None]

    def sweep_one(values, low_tile, high_tile, length, stiff_block, source_block, safe_block):
        near = stencil(extend(values, low_tile, high_tile, length), CX, CY, CZ)
        return (source_block + stiff_block[None] * near) / safe_block[None]

    for sweep_index in range(SWEEPS):
        weighted = stiff_masked[:, None] * adjoint
        weighted_tiles = lax.all_gather(end_faces(weighted, lengths), "dev", axis=0, tiled=True)
        lower_halo = partner_tiles(weighted_tiles, conn_lower, 1, slots)
        upper_halo = partner_tiles(weighted_tiles, conn_upper, 0, slots)
        adjoint = jax.vmap(sweep_one)(
            weighted, lower_halo, upper_halo, lengths, stiff_masked, source, safe
        )
    hat_x = hat(coord_x, LX)
    hat_y = hat(coord_y, LY)
    hat_z = hat(coord_z, LZ)
    first = jnp.einsum("bcxyz,bnz->bcxyn", adjoint, hat_z, precision=lax.Precision.HIGHEST)
    second = jnp.einsum("bcxyn,bmy->bxcmn", first, hat_y, precision=lax.Precision.HIGHEST)
    contracted = second.reshape(slots * CX, 3 * LY * LZ)
    hat_rows = jnp.transpose(hat_x, (1, 0, 2)).reshape(LX, slots * CX)
    scale = math.sqrt(
        LX * LY * LZ / (lax.axis_size("group") * lax.axis_size("dev") * slots * CX * CY * CZ)
    )
    partial_value = lax.psum_scatter(
        jnp.dot(
            hat_rows,
            contracted,
            precision=lax.Precision.HIGHEST,
            preferred_element_type=jnp.float32,
        ),
        "dev",
        scatter_dimension=0,
        tiled=True,
    )
    owned = lax.psum(partial_value, "group")
    return (adjoint, owned * scale)


def solution(mesh):
    in_specs = (
        P(("group", "dev"), None, None, None, None),
        P(("group", "dev"), None, None, None),
        P(("group", "dev")),
        P(("group", "dev"), None),
        P(("group", "dev"), None),
        P(("group", "dev"), None),
        P(("group", "dev"), None),
        P(("group", "dev"), None),
    )
    out_specs = (P(("group", "dev"), None, None, None, None), P("dev", None))
    return jax.shard_map(
        on_device, mesh=mesh, in_specs=in_specs, out_specs=out_specs, check_vma=False
    )
```

profile of v0, /device:TPU:0, one launch (start us, length us, event | category | flops | bytes accessed | tf_op | source)
XLA Modules:
  0.0 348.4 jit_solution(1823001275424142487)
XLA Ops:
  7.3 0.7 broadcast_compare_fusion
  8.0 0.7 fusion.188
  8.6 1.3 fusion.204
  11.1 32.6 %all_gather.9 = f32[16,2,1,16,128]{4,3,0,2,1:T(8,128)S(1)} all-gather(f32[2,2,1,16,128]{4,3,0,2,1:T(8,128)S(1)} %pad_maximum_fusion.2), channel_id=1, replica_groups=mesh['group'=4,'dev'=8] {'dev'}, dimensions={0}, use_global_device_ids=true | all-gather | bytes 294912 | tf_op jit(solution)/shard_map/all_gather | solution.py:78
  46.1 15.4 %while.3 = (s32[]{:T(128)}, f32[2,1,50,16,128]{4,3,0,2,1:T(8,128)S(1)}, s32[2,5]{1,0:T(2,128)S(1)}, f32[2,1,1,16,128]{4,3,2,1,0:T(8,128)S(1)}, s32[]{:T(128)}, /*index=5*/s32[5]{0:T(128)S(1)}) while((s32[]{:T(128)}, f32[2,1,50,16,128]{4,3,0,2,1:T(8,128)S(1)}, s32[2,5]{1,0:T(2,128)S(1)}, f32[2,1,1,16,128]{4,3,2,1,0:T(8,128)S(1)}, s32[]{:T(128)}, ...), condition=%wide.while_cond, body=%wide.while_body.sunk | while | flops 2069 | bytes 41215 | solution.py:43
  46.2 0.7 fusion.208
  46.8 3.2 concatenate.70
  50.0 0.7 and_reduce_fusion.6
  50.7 1.3 constant_dynamic-slice_fusion.14
  51.9 1.9 bitcast_dynamic-update-slice_fusion.6
  53.9 0.7 fusion.208
  54.5 3.2 concatenate.70
  57.7 0.7 and_reduce_fusion.6
  58.4 1.3 constant_dynamic-slice_fusion.14
  59.7 1.9 bitcast_dynamic-update-slice_fusion.6
  61.6 4.2 %fusion.142 = f32[2,48,16,128]{3,2,0,1:T(8,128)S(1)} fusion(f32[2,1,50,16,128]{4,3,0,2,1:T(8,128)S(1)} %get-tuple-element.7, pred[2,48]{0,1:T(8,128)(4,1)S(1)} %get-tuple-element.113, f32[2,48]{0,1:T(8,128)S(1)} %get-tuple-element.114, f32[2,48,16,128]{3,2,1,0:T(8,128)S(1)} %copy-done.4), kind=kLoop, calls=%fused_computation.243 | loop fusion | flops 9633792 | bytes 3995648 | tf_op jit(solution)/shard_map/jit(_where)/select_n | solution.py:89
  65.7 1.9 divide_multiply_fusion
  67.7 1.7 copy.85
  69.9 2.2 gather_fusion.7
  72.1 31.7 %all_gather.10 = f32[16,2,3,16,128]{4,3,2,0,1:T(8,128)S(1)} all-gather(f32[2,2,3,16,128]{4,3,2,0,1:T(8,128)S(1)} %pad_maximum_fusion), channel_id=1, replica_groups=mesh['group'=4,'dev'=8] {'dev'}, dimensions={0}, use_global_device_ids=true | all-gather | bytes 884736 | tf_op jit(solution)/shard_map/all_gather | solution.py:99
  105.2 1.9 maximum_maximum_fusion
  107.1 15.0 %while.4 = (s32[]{:T(128)}, f32[2,3,50,16,128]{4,3,1,0,2:T(8,128)S(1)}, s32[2,5]{1,0:T(2,128)S(1)}, f32[2,3,1,16,128]{4,3,2,1,0:T(8,128)S(1)}, s32[]{:T(128)}, /*index=5*/s32[5]{0:T(128)S(1)}) while((s32[]{:T(128)}, f32[2,3,50,16,128]{4,3,1,0,2:T(8,128)S(1)}, s32[2,5]{1,0:T(2,128)S(1)}, f32[2,3,1,16,128]{4,3,2,1,0:T(8,128)S(1)}, s32[]{:T(128)}, ...), condition=%wide.while_cond.1, body=%wide.while_body.1.sunk | while | flops 6165 | bytes 123135 | solution.py:43
  107.1 0.7 fusion.209
  107.8 3.2 concatenate.71
  110.9 0.6 and_reduce_fusion.7
  111.6 1.2 constant_dynamic-slice_fusion.16
  112.7 1.8 bitcast_dynamic-update-slice_fusion.7
  114.6 0.7 fusion.209
  115.2 3.2 concatenate.71
  118.4 0.6 and_reduce_fusion.7
  119.0 1.2 constant_dynamic-slice_fusion.16
  120.2 1.8 bitcast_dynamic-update-slice_fusion.7
  122.1 13.0 %fusion.97 = f32[2,3,48,16,128]{4,3,1,0,2:T(8,128)S(1)} fusion(f32[2,3,50,16,128]{4,3,1,0,2:T(8,128)S(1)} %get-tuple-element.15, f32[2,48,16,128]{3,2,0,1:T(8,128)} %copy-done.2, f32[2,48,16,128]{3,2,0,1:T(8,128)S(1)} %copy_multiply_fusion, f32[2,48]{0,1:T(8,128)S(1)} %get-tuple-element.114, bf16[2,3,48,16,128]{4,3,2,1,0:T(8,128)(2,1)} %param.8), kind=kLoop, calls=%fused_computation.196 | loop fusion | flops 30081024 | bytes 12312576 | tf_op jit(solution)/shard_map/mul | solution.py:98
  135.2 1.2 copy-done.1
  137.0 32.2 %all_gather.11 = f32[16,2,3,16,128]{4,3,2,0,1:T(8,128)S(1)} all-gather(f32[2,2,3,16,128]{4,3,2,0,1:T(8,128)S(1)} %pad_maximum_fusion.1), channel_id=1, replica_groups=mesh['group'=4,'dev'=8] {'dev'}, dimensions={0}, use_global_device_ids=true | all-gather | bytes 884736 | tf_op jit(solution)/shard_map/all_gather | solution.py:99
  170.5 1.9 maximum_maximum_fusion.1
  172.4 15.0 %while.5 = (s32[]{:T(128)}, f32[2,3,50,16,128]{4,3,1,0,2:T(8,128)S(1)}, s32[2,5]{1,0:T(2,128)S(1)}, f32[2,3,1,16,128]{4,3,2,1,0:T(8,128)S(1)}, s32[]{:T(128)}, /*index=5*/s32[5]{0:T(128)S(1)}) while((s32[]{:T(128)}, f32[2,3,50,16,128]{4,3,1,0,2:T(8,128)S(1)}, s32[2,5]{1,0:T(2,128)S(1)}, f32[2,3,1,16,128]{4,3,2,1,0:T(8,128)S(1)}, s32[]{:T(128)}, ...), condition=%wide.while_cond.2, body=%wide.while_body.2.sunk | while | flops 6165 | bytes 123135 | solution.py:43
  172.5 0.7 fusion.210
  173.1 3.2 concatenate.72
  176.3 0.6 and_reduce_fusion.8
  176.9 1.2 constant_dynamic-slice_fusion.18
  178.1 1.8 bitcast_dynamic-update-slice_fusion.8
  179.9 0.7 fusion.210
  180.6 3.2 concatenate.72
  183.8 0.6 and_reduce_fusion.8
  184.4 1.2 constant_dynamic-slice_fusion.18
  185.6 1.8 bitcast_dynamic-update-slice_fusion.8
  187.4 13.0 %fusion.93 = f32[2,3,48,16,128]{4,3,1,0,2:T(8,128)S(1)} fusion(f32[2,3,50,16,128]{4,3,1,0,2:T(8,128)S(1)} %get-tuple-element.23, f32[2,48,16,128]{3,2,0,1:T(8,128)} %copy-done.2, f32[2,48,16,128]{3,2,0,1:T(8,128)S(1)} %copy_multiply_fusion, f32[2,48]{0,1:T(8,128)S(1)} %get-tuple-element.114, bf16[2,3,48,16,128]{4,3,2,1,0:T(8,128)(2,1)} %param.8), kind=kLoop, calls=%fused_computation.190 | loop fusion | flops 29491200 | bytes 12312576 | tf_op jit(solution)/shard_map/vmap()/div | solution.py:95
  200.7 1.4 copy-done.3
  202.1 2.1 fusion.152
  204.2 2.3 copy.98
  206.5 10.4 %convolution_bitcast_fusion = f32[2,48,3,64,32]{3,1,4,2,0:T(8,128)} fusion(f32[2,3,48,16,32]{2,3,4,1,0:T(8,128)} %copy.98, f32[2,16]{1,0:T(2,128)S(1)} %copy-done.5), kind=kOutput, calls=%fused_computation.197 | convolution fusion | flops 113254400 | bytes 2949248 | tf_op jit(solution)/shard_map/bcxyn,bmy->bxcmn/dot_general | solution.py:109
  216.9 9.6 %copy.99 = f32[2,48,3,64,32]{1,0,4,3,2:T(2,128)} copy(f32[2,48,3,64,32]{3,1,4,2,0:T(8,128)} %convolution_bitcast_fusion) | data formatting | bytes 4718592 | tf_op jit(solution)/shard_map/bcxyn,bmy->bxcmn/transpose | solution.py:109
  226.5 6.1 %reshape.97 = f32[96,6144]{0,1:T(8,128)S(1)} reshape(f32[2,48,3,64,32]{1,0,4,3,2:T(2,128)} %copy.99) | data formatting | bytes 4718592 | tf_op jit(solution)/shard_map/reshape | solution.py:110
  232.6 4.7 %fusion.146 = f32[96,6144]{1,0:T(8,128)} fusion(f32[96,6144]{0,1:T(8,128)S(1)} %reshape.97, f32[96]{0:T(128)S(1)} %sub.71), kind=kOutput, calls=%fused_computation.253 | convolution fusion | flops 679514112 | bytes 4718976 | tf_op jit(solution)/shard_map/dot_general | solution.py:116
  237.3 50.6 %fusion = f32[16,6144]{1,0:T(8,128)S(1)} fusion(f32[96,6144]{1,0:T(8,128)} %fusion.146), kind=kCustom, calls=%all-reduce-scatter | all-reduce-scatter fusion | flops 786433 | bytes 2753024
  287.9 4.4 %collective-permute-start = (f32[16,6144]{1,0:T(8,128)S(1)}, f32[16,6144]{1,0:T(8,128)S(1)}, u32[]{:S(2)}, u32[]{:S(2)}) collective-permute-start(f32[16,6144]{1,0:T(8,128)S(1)} %fusion), channel_id=1, source_target_pairs={{0,1},{1,2},{2,3},{3,4},{4,5},{5,6},{6,7},{8,9},{9,10},{10,11},{11... | collective-permute-start | bytes 1179656
  292.4 6.3 %collective-permute-start.1 = (f32[12,6144]{1,0:T(8,128)S(1)}, f32[12,6144]{1,0:T(8,128)S(1)}, u32[]{:S(2)}, u32[]{:S(2)}) collective-permute-start(f32[12,6144]{1,0:T(8,128)S(1)} %slice.489), channel_id=1, source_target_pairs={{0,2},{1,3},{2,4},{3,5},{4,6},{5,7},{8,10},{9,11},{10,12},{11,13},... | collective-permute-start | bytes 884744
  298.7 0.6 dynamic-slice.22
  300.0 4.0 %collective-permute-done.1 = f32[12,6144]{1,0:T(8,128)S(1)} collective-permute-done((f32[12,6144]{1,0:T(8,128)S(1)}, f32[12,6144]{1,0:T(8,128)S(1)}, u32[]{:S(2)}, u32[]{:S(2)}) %collective-permute-start.1) | collective-permute-done | bytes 294944
  304.0 1.0 concatenate.66
  305.0 0.8 constant_dynamic-slice_fusion.6
  305.8 33.9 %all-reduce.9.cloned.1.call-done = f32[12,6144]{1,0:T(8,128)} async-done(((f32[12,6144]{1,0:T(8,128)}), f32[12,6144]{1,0:T(8,128)}) %all-reduce.9.cloned.1.call-update) | async-done | bytes 294928 | tf_op jit(solution)/shard_map/psum | solution.py:126
  339.8 1.8 broadcast_multiply_fusion
  (91 shorter events, 7.7 us)
Async XLA Ops:
  7.2 3.2 copy-start.9
  7.2 3.2 copy-start.4
  7.2 2.9 copy-start.6
  7.2 3.0 copy-start.7
  7.2 332.6 %all-reduce.9.cloned.1.call-start = ((), (), s32[]{:S(2)}) async-start(), calls=%async_computation | async-start | bytes 786432 | tf_op jit(solution)/shard_map/psum | solution.py:126
  9.9 36.0 %copy-start.11 = (s32[4]{0:T(128)S(1)}, s32[4]{0:T(128)}, u32[]{:S(2)}) copy-start(s32[4]{0:T(128)} %constant.25.clone.1) | copy-start | bytes 52
  10.0 36.1 %copy-start.13 = (s32[5]{0:T(128)S(1)}, s32[5]{0:T(128)}, u32[]{:S(2)}) copy-start(s32[5]{0:T(128)} %constant.656) | copy-start | bytes 64
  65.7 2.0 copy-start.2
  67.7 2.2 copy-start
  135.0 1.4 copy-start.1
  200.4 1.6 copy-start.8
  200.7 1.4 copy-start.3
  204.1 2.3 copy-start.5
  226.5 6.1 %copy-start.12 = (f32[2,48]{1,0:T(2,128)S(1)}, f32[2,48]{1,0:T(2,128)}, u32[]{:S(2)}) copy-start(f32[2,48]{1,0:T(2,128)} %param.13) | copy-start | bytes 1156
  237.3 61.4 %copy-start.10 = (u32[32]{0:T(128)S(1)}, u32[32]{0:T(128)}, u32[]{:S(2)}) copy-start(u32[32]{0:T(128)} %constant.342) | copy-start | bytes 388
  287.9 16.0 %collective-permute-start = (f32[16,6144]{1,0:T(8,128)S(1)}, f32[16,6144]{1,0:T(8,128)S(1)}, u32[]{:S(2)}, u32[]{:S(2)}) collective-permute-start(f32[16,6144]{1,0:T(8,128)S(1)} %fusion), channel_id=1, source_target_pairs={{0,1},{1,2},{2,3},{3,4},{4,5},{5,6},{6,7},{8,9},{9,10},{10,11},{11... | collective-permute-start | bytes 1179656
  292.4 11.6 %collective-permute-start.1 = (f32[12,6144]{1,0:T(8,128)S(1)}, f32[12,6144]{1,0:T(8,128)S(1)}, u32[]{:S(2)}, u32[]{:S(2)}) collective-permute-start(f32[12,6144]{1,0:T(8,128)S(1)} %slice.489), channel_id=1, source_target_pairs={{0,2},{1,3},{2,4},{3,5},{4,6},{5,7},{8,10},{9,11},{10,12},{11,13},... | collective-permute-start | bytes 884744
Sparse Core Ops, SparseCore 0:
  306.0 33.7 all-reduce.8
where the time goes:
time: 350 us; the launch traced here: 348 us
  blocking collectives  147 us (42%)
  local copies, waits for them, and re-layouts  63.7 us (18%)
  other arithmetic  56.4 us (16%)
  waiting for transfers between devices  38 us (11%)
  matrix products  17.1 us (5%)
  between operations  15.1 us (4%)
  starting transfers between devices  10.8 us (3%)
    all_gather x2, blocking collectives, on_device(): lax.all_gather(end_faces(weighted, lengths), 'dev', axis=0, tiled=True)  63.9 us
    unnamed x1, blocking collectives  50.6 us
    psum x1, waiting for transfers between devices, on_device(): owned = lax.psum(partial_value, 'group')  33.9 us
    all_gather x1, blocking collectives, on_device(): lax.all_gather(end_faces(stiff_masked[:, None], lengths), 'dev', axis=0,...  32.6 us
    scatter x24, local copies, waits for them, and re-layouts  30.2 us
    scatter x12, other arithmetic  14.9 us
    mul x2, other arithmetic, on_device(): weighted = stiff_masked[:, None] * adjoint  14.9 us
    div x1, other arithmetic, sweep_one(): return (source_block + stiff_block[None] * near) / safe_block[None]  13 us
  transfers between devices with their start and end apart: 3, of which 2 were waited for; matrix products, arithmetic and copies ran while one was open for 0% of the time, Pallas kernels for 0%

commit v1 on v0

v1 whole, which is shorter than its diff:
```python
import functools
import math

import jax
import jax.numpy as jnp
from jax import lax
from jax.experimental import pallas as pl
from jax.experimental.pallas import tpu as pltpu
from jax.sharding import PartitionSpec as P

LX = 96
LY = 64
LZ = 32
DOMINANCE = 1.25
PLANES = 8
STEP = 4

F32 = jnp.float32
BF16 = jnp.bfloat16
SMEM = pl.BlockSpec(memory_space=pltpu.SMEM)
VMEM = pl.BlockSpec(memory_space=pltpu.VMEM)


def params():
    return pltpu.CompilerParams(vmem_limit_bytes=60 * 1024 * 1024)


def neighbours(v, axis):
    extent = v.shape[axis]
    place = lax.broadcasted_iota(jnp.int32, v.shape, axis)
    up = jnp.where(place == 0, 0.0, pltpu.roll(v, 1, axis))
    down = jnp.where(place == extent - 1, 0.0, pltpu.roll(v, extent - 1, axis))
    return up + down


def plane_parts(v):
    along_z = neighbours(v, v.ndim - 1)
    first = v + 0.5 * along_z
    second = 0.5 * v + (1.0 / 3.0) * along_z
    beside = first + neighbours(second, v.ndim - 2)
    own = along_z + neighbours(first, v.ndim - 2)
    return beside, own


def split(v):
    high = v.astype(BF16)
    return high, (v - high.astype(F32)).astype(BF16)


def dot3(a, b, contract_b=0):
    numbers = (((1,), (contract_b,)), ((), ()))
    mul = lambda p, q: lax.dot_general(p, q, numbers, preferred_element_type=F32)
    return mul(a[0], b[0]) + (mul(a[0], b[1]) + mul(a[1], b[0]))


def pack_kernel(devs, len_ref, low_ref, up_ref, seed_ref, stiff_ref, out_ref, packet):
    slots, _, cy, cz = stiff_ref.shape
    rows = PLANES * cy
    chunk = rows // devs
    for s in range(slots):
        length = len_ref[s]
        for side in range(2):
            at = [k if side == 0 else length - 1 - k for k in range(3)]
            stiff = [stiff_ref[s, i] for i in at]
            parts = [plane_parts(v) for v in stiff]
            inner = parts[0][1] + parts[1][0]
            next_near = parts[1][1] + parts[0][0] + parts[2][0]
            scale = 1.0 / (DOMINANCE * next_near)
            planes = [stiff[0], inner]
            planes += [seed_ref[s, c, at[0]].astype(F32) for c in range(3)]
            for c in range(3):
                planes.append(plane_parts(seed_ref[s, c, at[1]].astype(F32) * scale)[0])
            for k, plane in enumerate(planes):
                packet[2 * s + side, k * cy : (k + 1) * cy] = plane
    wanted = []
    for s in range(slots):
        for side, ref in ((0, low_ref), (1, up_ref)):
            number = jnp.maximum(ref[s, 0], 0) * (2 * slots) + ref[s, 1] * 2 + (1 - side)
            wanted.append(number.astype(F32))
    row = lax.broadcasted_iota(jnp.int32, (8, cz), 0)
    note = jnp.zeros((8, cz), F32)
    for f, number in enumerate(wanted):
        note = jnp.where(row == f, number, note)
    for j in range(devs):
        for f in range(2 * slots):
            out_ref[j, f * chunk : (f + 1) * chunk] = packet[f, j * chunk : (j + 1) * chunk]
        out_ref[j, 2 * slots * chunk :] = note


def route_kernel(in_ref, out_ref):
    devs, rows, _ = out_ref.shape
    faces = 4
    chunk = rows // faces
    for e in range(devs):
        for f in range(faces):
            cell = in_ref[e, rows + f : rows + f + 1, 0:1]
            number = cell[0, 0].astype(jnp.int32)
            source = number // faces
            start = (number % faces) * chunk
            if chunk % 8 == 0:
                start = pl.multiple_of(start, 8)
            out_ref[e, f * chunk : (f + 1) * chunk] = in_ref[source, pl.ds(start, chunk)]


def main_kernel(
    per,
    dest_ref,
    len_ref,
    low_ref,
    up_ref,
    seed_ref,
    stiff_ref,
    halo_ref,
    cx_ref,
    cy_ref,
    cz_ref,
    out_ref,
    keep_ref,
    send_ref,
    pack,
    s_ext,
    w_ext,
    v_ext,
    inv_ref,
    fac_ref,
    zdone,
    xdone,
):
    slots, nx, ny, nz = stiff_ref.shape
    devs = halo_ref.shape[0]
    chunk = halo_ref.shape[1] // (2 * slots)
    zero_plane = jnp.zeros((ny, nz), F32)

    for s in range(slots):
        for side, ref in ((0, low_ref), (1, up_ref)):
            f = 2 * s + side
            wall = ref[s, 0] < 0
            turned = ref[s, 2] == 1

            def place(reverse, f=f):
                for k in range(PLANES):
                    for r in range(ny):
                        at = k * ny + r
                        to = ny - 1 - r if reverse else r
                        j, o = at // chunk, at % chunk
                        pack[f, k, to : to + 1] = halo_ref[j, f * chunk + o : f * chunk + o + 1]

            @pl.when(wall)
            def _(f=f):
                for k in range(PLANES):
                    pack[f, k] = zero_plane

            @pl.when(jnp.logical_and(jnp.logical_not(wall), turned))
            def _(place=place):
                place(True)

            @pl.when(jnp.logical_and(jnp.logical_not(wall), jnp.logical_not(turned)))
            def _(place=place):
                place(False)

    def sweep(get, finish):
        before, _ = plane_parts(get(0, 1))
        here, own = plane_parts(get(1, 1))

        def body(step, carry):
            before, here, own = carry
            i = step * STEP
            beside, mine = plane_parts(get(i + 2, STEP))
            all_beside = jnp.concatenate([before, here, beside], axis=0)
            all_own = jnp.concatenate([own, mine], axis=0)
            near = all_own[:STEP] + all_beside[:STEP] + all_beside[2:]
            finish(i, near)
            return all_beside[STEP : STEP + 1], all_beside[STEP + 1 :], all_own[STEP:]

        lax.fori_loop(0, nx // STEP, body, (before, here, own))

    for b in range(slots):
        length = len_ref[b]
        lower, upper = 2 * b, 2 * b + 1

        def fill(step, _, b=b, length=length):
            i = step * STEP
            at = i + lax.broadcasted_iota(jnp.int32, (STEP, ny, nz), 0)
            s_ext[pl.ds(i + 1, STEP)] = jnp.where(at < length, stiff_ref[b, pl.ds(i, STEP)], 0.0)
            return 0

        lax.fori_loop(0, nx // STEP, fill, 0)
        s_ext[nx + 1] = zero_plane
        s_ext[0] = pack[lower, 0]
        s_ext[length + 1] = pack[upper, 0]

        def first(i, near, b=b, length=length):
            at = i + lax.broadcasted_iota(jnp.int32, (STEP, ny, nz), 0)
            active = at < length
            stiff = jnp.where(active, stiff_ref[b, pl.ds(i, STEP)], 0.0)
            safe = jnp.where(active, DOMINANCE * stiff * near, 1.0)
            inv = jnp.where(active, 1.0 / safe, 0.0)
            fac = stiff * inv
            inv_ref[pl.ds(i, STEP)] = inv
            fac_ref[pl.ds(i, STEP)] = fac
            for c in range(3):
                w_ext[c, pl.ds(i + 1, STEP)] = seed_ref[b, c, pl.ds(i, STEP)].astype(F32) * fac

        sweep(lambda i, n: s_ext[pl.ds(i, n)], first)

        ends = ((lower, 1, 0), (upper, length, length + 1))
        for f, mine, there in ends:
            near = pack[f, 1] + plane_parts(stiff_ref[b, mine - 1])[0]
            fac = 1.0 / (DOMINANCE * near)
            for c in range(3):
                weighted = pack[f, 2 + c] * fac
                beside, own = plane_parts(weighted)
                total = own + pack[f, 5 + c] + plane_parts(w_ext[c, mine])[0]
                v_ext[c, there] = (pack[f, 2 + c] + pack[f, 0] * total) * fac
                pack[f, 5 + c] = weighted
        for c in range(3):
            w_ext[c, nx + 1] = zero_plane
        for f, mine, there in ends:
            for c in range(3):
                w_ext[c, there] = pack[f, 5 + c]
        keep_ends = [[v_ext[c, there] for c in range(3)] for f, mine, there in ends]

        for c in range(3):

            def second(i, near, b=b, c=c):
                seed = seed_ref[b, c, pl.ds(i, STEP)].astype(F32)
                stiff = stiff_ref[b, pl.ds(i, STEP)]
                v_ext[c, pl.ds(i + 1, STEP)] = (seed + stiff * near) * fac_ref[pl.ds(i, STEP)]

            sweep(lambda i, n, c=c: w_ext[c, pl.ds(i, n)], second)
            v_ext[c, nx + 1] = zero_plane
            v_ext[c, 0] = keep_ends[0][c]
            v_ext[c, length + 1] = keep_ends[1][c]

            def third(i, near, b=b, c=c):
                seed = seed_ref[b, c, pl.ds(i, STEP)].astype(F32)
                stiff = stiff_ref[b, pl.ds(i, STEP)]
                out_ref[b, c, pl.ds(i, STEP)] = (seed + stiff * near) * inv_ref[pl.ds(i, STEP)]

            sweep(lambda i, n, c=c: v_ext[c, pl.ds(i, n)], third)

    group = 16
    row = lax.broadcasted_iota(jnp.int32, (128, 3 * nz), 0)
    lane = lax.broadcasted_iota(jnp.int32, (128, 3 * nz), 1)
    same = (row // LZ) == (lane // nz)
    point = (row % LZ).astype(F32)
    for b in range(slots):
        cz = cz_ref[b : b + 1, :]
        hat_z = jnp.maximum(0.0, 1.0 - jnp.abs(point - jnp.concatenate([cz, cz, cz], axis=1)))
        hat_z = split(jnp.where(same, hat_z, 0.0))
        for x in range(0, nx, group):
            rows = [out_ref[b, c, x : x + group].reshape(group * ny, nz) for c in range(3)]
            done = dot3(split(jnp.concatenate(rows, axis=1)), hat_z, 1)
            zdone[pl.ds((b * nx + x) * ny, group * ny)] = done
        line = lax.broadcasted_iota(jnp.int32, (LX, nx), 0).astype(F32)
        hat_x = split(jnp.maximum(0.0, 1.0 - jnp.abs(line - cx_ref[b : b + 1, :])))
        for y in range(ny):
            part = zdone[pl.ds(b * nx * ny + y, nx, stride=ny), :]
            xdone[pl.ds(b * ny + y, LX, stride=slots * ny), :] = dot3(hat_x, split(part))

    depth = per * slots * ny
    row = lax.broadcasted_iota(jnp.int32, (LY * per, depth), 0).astype(F32)
    lane = lax.broadcasted_iota(jnp.int32, (LY * per, depth), 1).astype(F32)
    which = jnp.floor((row + 0.5) * (1.0 / per))
    inside = row - which * per
    owner = jnp.floor((lane + 0.5) * (1.0 / (slots * ny)))
    hat_y = jnp.maximum(0.0, 1.0 - jnp.abs(which - cy_ref[...]))
    hat_y = split(jnp.where(inside == owner, hat_y, 0.0))
    third_rows = LY // 4 * per
    pieces = keep_ref.shape[3]
    tail = lax.broadcasted_iota(jnp.int32, (third_rows, 128), 1) >= 3 * LZ

    def close(number, _):
        start = number * depth
        if depth % 8 == 0:
            start = pl.multiple_of(start, 8)
        done = dot3(hat_y, split(xdone[pl.ds(start, depth), :]))
        last = done[3 * third_rows :]
        dense = []
        for q in range(3):
            moved = pltpu.roll(last, 3 * LZ - q * LZ, 1)
            dense.append(jnp.where(tail, moved, done[q * third_rows : (q + 1) * third_rows]))
        dense = jnp.concatenate(dense, axis=0)
        size = 3 * third_rows // 8
        d, t = number // pieces, number % pieces
        for core in range(2):

            @pl.when(dest_ref[0] == core)
            def _(core=core):
                for g in range(8):
                    ref = keep_ref if g // 4 == core else send_ref
                    ref[d, g // 2 % 2, g % 2, t] = dense[g * size : (g + 1) * size]

        return 0

    lax.fori_loop(0, LX // per, close, 0)


def core_kernel(dest_ref, keep_ref, got_ref, keep_y, send_y, keep_x, send_x):
    y, x = dest_ref[2], dest_ref[1]
    keep_y[...] = keep_ref[:, y, 0] + got_ref[:, y, 0]
    send_y[...] = keep_ref[:, 1 - y, 0] + got_ref[:, 1 - y, 0]
    keep_x[...] = keep_ref[:, :, 1, x] + got_ref[:, :, 1, x]
    send_x[...] = keep_ref[:, :, 1, 1 - x] + got_ref[:, :, 1, 1 - x]


def plane_kernel(dest_ref, keep_y, got_y, keep_x, got_x, keep_0, send_0, keep_1, send_1):
    y, x = dest_ref[2], dest_ref[1]
    keep_0[...] = keep_y[:, x] + got_y[:, x]
    send_0[...] = keep_y[:, 1 - x] + got_y[:, 1 - x]
    keep_1[...] = keep_x[:, y] + got_x[:, y]
    send_1[...] = keep_x[:, 1 - y] + got_x[:, 1 - y]


def line_kernel(dest_ref, keep_0, got_0, keep_1, got_1, *outs):
    z = dest_ref[3]
    count = len(outs)
    for k, out in enumerate(outs):
        at = lax.rem(z + k, count)
        out[0] = keep_0[at] + got_0[at]
        out[1] = keep_1[at] + got_1[at]


def sum_kernel(scale, *refs):
    total = refs[0][...]
    for ref in refs[1:-1]:
        total = total + ref[...]
    refs[-1][...] = total * scale


def unpack_kernel(per, dest_ref, own, got_c, got_x, got_xc, out_ref, pieces):
    core, x = dest_ref[0], dest_ref[1]
    pieces[core, x] = own[...]
    pieces[1 - core, x] = got_c[...]
    pieces[core, 1 - x] = got_x[...]
    pieces[1 - core, 1 - x] = got_xc[...]
    count = own.shape[1]
    quarter = LY // 4
    size = 3 * quarter // 8
    lane = lax.broadcasted_iota(jnp.int32, (per, 128), 1) // LZ
    for t in range(count):

        def strip(r):
            g, at = r // size, r % size
            return pieces[g // 4, g % 2, g // 2 % 2, t, at * per : (at + 1) * per]

        for c in range(3):
            for m4 in range(LY // 4):
                tile = None
                for k in range(4):
                    m = 4 * m4 + k
                    if m < 3 * quarter:
                        value, lies = strip(m), c
                    else:
                        value, lies = strip(c * quarter + m - 3 * quarter), 3
                    shift = ((k - lies) * LZ) % 128
                    value = pltpu.roll(value, shift, 1) if shift else value
                    tile = value if tile is None else jnp.where(lane == k, value, tile)
                at = c * LY * LZ + m4 * 128
                out_ref[t * per : (t + 1) * per, at : at + 128] = tile


def on_device(groups, devs, seed, stiff, lengths, low, up, coord_x, coord_y, coord_z):
    slots, nx, ny, nz = stiff.shape
    faces = 2 * slots
    chunk = PLANES * ny // devs
    rows = faces * chunk
    mine = LX // devs
    per = 4 if mine % 4 == 0 else mine
    pieces = mine // per
    size = 3 * LY // 4 // 8 * per
    group_at = lax.axis_index("group")
    dev_at = lax.axis_index("dev")
    fast = groups == 4 and devs % 2 == 0 and size % 8 == 0
    if fast:
        dest = jnp.stack([group_at % 2, group_at // 2, dev_at % 2, dev_at // 2]).astype(jnp.int32)
    else:
        dest = jnp.zeros((4,), jnp.int32)
    shape = lambda *dims: jax.ShapeDtypeStruct(dims, F32)

    packed = pl.pallas_call(
        functools.partial(pack_kernel, devs),
        out_shape=shape(devs, rows + 8, nz),
        in_specs=[SMEM, SMEM, SMEM, VMEM, VMEM],
        out_specs=VMEM,
        scratch_shapes=[pltpu.VMEM((faces, PLANES * ny, nz), F32)],
        compiler_params=params(),
        name="pack",
    )(lengths, low, up, seed, stiff)
    spread = lax.all_to_all(packed, "dev", 0, 0)
    routed = pl.pallas_call(
        route_kernel,
        out_shape=shape(devs, rows, nz),
        in_specs=[VMEM],
        out_specs=VMEM,
        compiler_params=params(),
        name="route",
    )(spread)
    halos = lax.all_to_all(routed, "dev", 0, 0)

    ext = pltpu.VMEM((nx + 2, ny, nz), F32)
    ext3 = pltpu.VMEM((3, nx + 2, ny, nz), F32)
    plain = pltpu.VMEM((nx, ny, nz), F32)
    half = shape(devs, 2, 2, pieces, size, 128)
    adjoint, keep, send = pl.pallas_call(
        functools.partial(main_kernel, per),
        out_shape=(shape(slots, 3, nx, ny, nz), half, half),
        in_specs=[SMEM] * 4 + [VMEM] * 6,
        out_specs=(VMEM,) * 3,
        scratch_shapes=[
            pltpu.VMEM((faces, PLANES, ny, nz), F32),
            ext,
            ext3,
            ext3,
            plain,
            plain,
            pltpu.VMEM((slots * nx * ny, 128), F32),
            pltpu.VMEM((LX * slots * ny, 128), F32),
        ],
        compiler_params=params(),
        name="main",
    )(
        dest,
        lengths,
        low,
        up,
        seed,
        stiff,
        halos,
        coord_x,
        jnp.tile(coord_y.reshape(1, slots * ny), (1, per)),
        coord_z,
    )

    scale = math.sqrt(LX * LY * LZ / (groups * devs * slots * nx * ny * nz))

    def small(kernel, outs, args, scratch=()):
        return pl.pallas_call(
            kernel,
            out_shape=outs,
            in_specs=[SMEM if a is dest else VMEM for a in args],
            out_specs=jax.tree.map(lambda _: VMEM, outs),
            scratch_shapes=scratch,
            compiler_params=params(),
        )(*args)

    piece = (2, pieces, size, 128)
    if fast:
        lines = devs // 2
        body = pieces * size

        def move(value, to):
            links = []
            for g in range(groups):
                for d in range(devs):
                    c2, x2, y2, z2 = to(g % 2, g // 2, d % 2, d // 2)
                    links.append((g * devs + d, (x2 * 2 + c2) * devs + z2 * 2 + y2))
            return lax.ppermute(value, ("group", "dev"), links)

        flip_c = lambda c, x, y, z: (1 - c, x, y, z)
        flip_x = lambda c, x, y, z: (c, 1 - x, y, z)
        flip_y = lambda c, x, y, z: (c, x, 1 - y, z)
        flip_xc = lambda c, x, y, z: (1 - c, 1 - x, y, z)
        got = move(send, flip_c)
        view = (lines, 2, 2, 2, body, 128)
        part = shape(lines, 2, body, 128)
        keep_y, send_y, keep_x, send_x = small(
            core_kernel, (part,) * 4, (dest, keep.reshape(view), got.reshape(view))
        )
        got_y, got_x = move(send_y, flip_y), move(send_x, flip_x)
        part = shape(lines, body, 128)
        keep_0, send_0, keep_1, send_1 = small(
            plane_kernel, (part,) * 4, (dest, keep_y, got_y, keep_x, got_x)
        )
        got_0, got_1 = move(send_0, flip_x), move(send_1, flip_y)
        part = shape(2, body, 128)
        sums = small(line_kernel, (part,) * lines, (dest, keep_0, got_0, keep_1, got_1))
        terms = [sums[0]]
        for k in range(1, lines):
            terms.append(move(sums[k], lambda c, x, y, z, k=k: (c, x, y, (z + k) % lines)))
        own = small(functools.partial(sum_kernel, scale), part, tuple(terms))
        others = [move(own, to) for to in (flip_c, flip_x, flip_xc)]
        quarters = [v.reshape(piece) for v in (own, *others)]
    else:
        whole = jnp.stack([keep, send], axis=1).reshape(devs, -1, 128)
        owned = lax.psum_scatter(whole, "dev", scatter_dimension=0, tiled=True)
        owned = lax.psum(owned, "group") * scale
        owned = owned.reshape(2, 2, 2, pieces, size, 128)
        quarters = [owned[c, :, x] for x in range(2) for c in range(2)]
    lattice = small(
        functools.partial(unpack_kernel, per),
        shape(mine, 3 * LY * LZ),
        (dest, *quarters),
        [pltpu.VMEM((2, 2, *piece), F32)],
    )
    return adjoint, lattice


def solution(mesh):
    both = ("group", "dev")
    in_specs = (
        P(both, None, None, None, None),
        P(both, None, None, None),
        P(both),
        P(both, None),
        P(both, None),
        P(both, None),
        P(both, None),
        P(both, None),
    )
    out_specs = (P(both, None, None, None, None), P("dev", None))
    body = functools.partial(on_device, mesh.shape["group"], mesh.shape["dev"])
    return jax.shard_map(
        body, mesh=mesh, in_specs=in_specs, out_specs=out_specs, check_vma=False
    )
```

time: 350 us -> 117 us (0.33)
  blocking collectives: 147 us -> 17.9 us
  local copies, waits for them, and re-layouts: 63.7 us -> 5.03 us
  other arithmetic: 56.4 us -> 0.65 us
  Pallas kernels: 0 us -> 49.2 us
  matrix products: 17.1 us -> 0 us
  between operations: 15.1 us -> 0.71 us
  waiting for transfers between devices: 38 us -> 29 us
    all_gather x3 -> x0, blocking collectives: 96.5 us -> none  [the longest x2 63.9 us: on_device(): lax.all_gather(end_faces(weighted, lengths), 'dev', axis=0, tiled=True)]
    unnamed x1 -> x0, blocking collectives: 50.6 us -> none
    pallas_call x0 -> x8, Pallas kernels: none -> 49.2 us  [the longest x1 34.1 us: on_device(): pl.pallas_call(functools.partial(main_kernel, per), out_shape=(shape(slot...]
    psum x1 -> x0, waiting for transfers between devices: 33.9 us -> none  [on_device(): owned = lax.psum(partial_value, 'group')]
    scatter x24 -> x0, local copies, waits for them, and re-layouts: 30.2 us -> none
    ppermute x0 -> x11, waiting for transfers between devices: none -> 22 us  [move(): return lax.ppermute(value, ('group', 'dev'), links)]
    all_to_all x0 -> x1, blocking collectives: none -> 17.9 us  [on_device(): spread = lax.all_to_all(packed, 'dev', 0, 0)]
    dot_general x3 -> x0, matrix products: 17.1 us -> none  [the longest x1 10.4 us: on_device(): jnp.einsum('bcxyn,bmy->bxcmn', first, hat_y, precision=lax.Precision.HIGH...]
  transfers between devices with their start and end apart: 3 -> 12, of which waited for: 2 -> 10; matrix products, arithmetic and copies ran while one was open for 0% -> 1% of each run, Pallas kernels for 0% -> 0%
where the time goes in v1:
time: 117 us
  Pallas kernels  49.2 us (42%)
  waiting for transfers between devices  29 us (25%)
  blocking collectives  17.9 us (15%)
  starting transfers between devices  14.1 us (12%)
  local copies, waits for them, and re-layouts  5.03 us (4%)
    pallas_call x1, Pallas kernels, on_device(): pl.pallas_call(functools.partial(main_kernel, per), out_shape=(shape(slot...  34.1 us
    ppermute x11, waiting for transfers between devices, move(): return lax.ppermute(value, ('group', 'dev'), links)  22 us
    all_to_all x1, blocking collectives, on_device(): spread = lax.all_to_all(packed, 'dev', 0, 0)  17.9 us
    pallas_call x5, Pallas kernels, small(): pl.pallas_call(kernel, out_shape=outs, in_specs=[SMEM if a is dest else V...  10.7 us
    ppermute x11, starting transfers between devices, move(): return lax.ppermute(value, ('group', 'dev'), links)  10.7 us
    all_to_all x1, waiting for transfers between devices, on_device(): halos = lax.all_to_all(routed, 'dev', 0, 0)  7.05 us
    unnamed x26, local copies, waits for them, and re-layouts  4.38 us
    all_to_all x1, starting transfers between devices, on_device(): halos = lax.all_to_all(routed, 'dev', 0, 0)  3.41 us
  transfers between devices with their start and end apart: 12, of which 10 were waited for; matrix products, arithmetic and copies ran while one was open for 1% of the time, Pallas kernels for 0%

profile of v1, /device:TPU:0, one launch (start us, length us, event | category | flops | bytes accessed | tf_op | source)
XLA Modules:
  0.0 116.6 jit_solution(10351084694103536588)
XLA Ops:
  0.6 2.5 %pack.1 = f32[8,72,128]{2,1,0:T(8,128)} custom-call(s32[2]{0:T(128)} %len_ref.3, s32[2,3]{1,0:T(2,128)} %low_ref.3, s32[2,3]{1,0:T(2,128)} %up_ref.3, bf16[2,3,48,16,128]{4,3,2,1,0:T(8,128)(2,1)} %seed_ref.3, f32[2,48,16,128]{3,2,1,0:T(8,128)} %stiff_ref.3), custom_call_target="tpu_custom_call" | custom-call | tf_op jit(solution)/shard_map/pack/pallas_call | solution.py:381
  3.1 0.0 copy-start.12
  3.1 17.9 %all_to_all.10.in_ref = f32[8,72,128]{2,1,0:T(8,128)} all-to-all(f32[8,72,128]{2,1,0:T(8,128)} %pack.1), channel_id=1, replica_groups=mesh['group'=4,'dev'=8] {'dev'}, dimensions={0} | all-to-all | bytes 589824 | tf_op jit(solution)/shard_map/all_to_all | solution.py:390
  21.0 1.9 %route.1 = f32[8,64,128]{2,1,0:T(8,128)} custom-call(f32[8,72,128]{2,1,0:T(8,128)} %all_to_all.10.in_ref), custom_call_target="tpu_custom_call" | custom-call | tf_op jit(solution)/shard_map/route/pallas_call | solution.py:391
  22.9 3.4 %all-to-all-start.1 = ((f32[8,64,128]{2,1,0:T(8,128)}), f32[8,64,128]{2,1,0:T(8,128)S(1)}, u32[]{:S(2)}, u32[]{:S(2)}) async-start(f32[8,64,128]{2,1,0:T(8,128)} %route.1), calls=%async_computation.1 | async-start | bytes 524288 | tf_op jit(solution)/shard_map/all_to_all | solution.py:399
  26.4 0.0 copy-done.12
  26.4 0.1 tile.10
  26.5 0.6 tile.12.cy_ref
  27.1 0.7 pad_add_fusion.dest_ref
  27.7 7.0 %all-to-all-done.1.halo_ref = f32[8,64,128]{2,1,0:T(8,128)S(1)} async-done(((f32[8,64,128]{2,1,0:T(8,128)}), f32[8,64,128]{2,1,0:T(8,128)S(1)}, u32[]{:S(2)}, u32[]{:S(2)}) %all-to-all-start.1) | async-done | bytes 262176 | tf_op jit(solution)/shard_map/all_to_all | solution.py:399
  34.8 0.0 copy-start.1
  34.8 0.7 copy-done.1
  35.5 34.1 %main.1 = (f32[2,3,48,16,128]{4,3,2,1,0:T(8,128)}, f32[8,2,2,3,24,128]{5,4,3,2,1,0:T(8,128)}, f32[8,2,2,3,24,128]{5,4,3,2,1,0:T(8,128)}) custom-call(s32[4]{0:T(128)} %pad_add_fusion.dest_ref, s32[2]{0:T(128)} %len_ref.3, s32[2,3]{1,0:T(2,128)} %low_ref.3, s32[2,3]{1,0:T(2,128)} %up_ref.3, bf16[2,3,48,16,128]{4,3,2,1,0:T(8,128)(2,1)} %seed_ref.3, ...), custom_call_target="tpu_custom_call" | custom-call | tf_op jit(solution)/shard_map/main/pallas_call | solution.py:405
  69.5 0.0 collective-permute-start
  69.5 3.1 %collective-permute-done = f32[8,2,2,3,24,128]{5,4,3,2,1,0:T(8,128)S(1)} collective-permute-done((f32[8,2,2,3,24,128]{5,4,3,2,1,0:T(8,128)}, f32[8,2,2,3,24,128]{5,4,3,2,1,0:T(8,128)S(1)}, u32[]{:S(2)}, u32[]{:S(2)}) %collective-permute-start) | collective-permute-done | bytes 1179680 | tf_op jit(solution)/shard_map/ppermute | solution.py:458
  72.6 0.0 copy-start
  72.6 1.0 copy-done
  73.6 2.8 %shard_map.95 = (f32[4,2,72,128]{3,2,1,0:T(8,128)}, f32[4,2,72,128]{3,2,1,0:T(8,128)}, f32[4,2,72,128]{3,2,1,0:T(8,128)}, f32[4,2,72,128]{3,2,1,0:T(8,128)}) custom-call(s32[4]{0:T(128)} %pad_add_fusion.dest_ref, f32[4,2,2,2,72,128]{5,4,3,2,1,0:T(8,128)} %bitcast.10, f32[4,2,2,2,72,128]{5,4,3,2,1,0:T(8,128)} %bitcast.11), custom_call_target="tpu_custom_call" | custom-call | tf_op jit(solution)/shard_map/pallas_call | solution.py:438
  76.4 1.2 %collective-permute-start.1 = (f32[4,2,72,128]{3,2,1,0:T(8,128)}, f32[4,2,72,128]{3,2,1,0:T(8,128)S(1)}, u32[]{:S(2)}, u32[]{:S(2)}) collective-permute-start(f32[4,2,72,128]{3,2,1,0:T(8,128)} %get-tuple-element.21), channel_id=1, source_target_pairs={{0,1},{1,0},{2,3},{3,2},{4,5},{5,4},{6,7},{7,6},{8,9},{9,8},{10,11... | collective-permute-start | bytes 884744 | tf_op jit(solution)/shard_map/ppermute | solution.py:458
  77.6 1.6 %collective-permute-start.2 = (f32[4,2,72,128]{3,2,1,0:T(8,128)}, f32[4,2,72,128]{3,2,1,0:T(8,128)S(1)}, u32[]{:S(2)}, u32[]{:S(2)}) collective-permute-start(f32[4,2,72,128]{3,2,1,0:T(8,128)} %get-tuple-element.23), channel_id=1, source_target_pairs={{0,16},{1,17},{2,18},{3,19},{4,20},{5,21},{6,22},{7,23},{8,24},{9,... | collective-permute-start | bytes 884744 | tf_op jit(solution)/shard_map/ppermute | solution.py:458
  79.1 6.5 %collective-permute-done.1.got_y = f32[4,2,72,128]{3,2,1,0:T(8,128)S(1)} collective-permute-done((f32[4,2,72,128]{3,2,1,0:T(8,128)}, f32[4,2,72,128]{3,2,1,0:T(8,128)S(1)}, u32[]{:S(2)}, u32[]{:S(2)}) %collective-permute-start.1) | collective-permute-done | bytes 294944 | tf_op jit(solution)/shard_map/ppermute | solution.py:458
  85.6 0.0 copy-start.2
  85.7 0.9 collective-permute-done.2.got_x
  86.6 0.0 copy-start.3
  86.6 0.0 copy-done.2
  86.6 0.7 copy-done.3
  87.3 2.1 %shard_map.96 = (f32[4,72,128]{2,1,0:T(8,128)}, f32[4,72,128]{2,1,0:T(8,128)}, f32[4,72,128]{2,1,0:T(8,128)}, f32[4,72,128]{2,1,0:T(8,128)}) custom-call(s32[4]{0:T(128)} %pad_add_fusion.dest_ref, f32[4,2,72,128]{3,2,1,0:T(8,128)} %get-tuple-element.20.keep_y, f32[4,2,72,128]{3,2,1,0:T(8,128)} %copy-done.2, f32[4,2,72,128]{3,2,1,0:T(8,128)} %get-tuple-element.22.keep_x, ...), custom_call_target="tpu_custom_call" | custom-call | tf_op jit(solution)/shard_map/pallas_call | solution.py:438
  89.4 1.6 %collective-permute-start.3 = (f32[4,72,128]{2,1,0:T(8,128)}, f32[4,72,128]{2,1,0:T(8,128)S(1)}, u32[]{:S(2)}, u32[]{:S(2)}) collective-permute-start(f32[4,72,128]{2,1,0:T(8,128)} %get-tuple-element.25), channel_id=1, source_target_pairs={{0,16},{1,17},{2,18},{3,19},{4,20},{5,21},{6,22},{7,23},{8,24},{9,... | collective-permute-start | bytes 442376 | tf_op jit(solution)/shard_map/ppermute | solution.py:458
  90.9 0.7 collective-permute-start.4
  91.6 3.1 %collective-permute-done.3.got_0 = f32[4,72,128]{2,1,0:T(8,128)S(1)} collective-permute-done((f32[4,72,128]{2,1,0:T(8,128)}, f32[4,72,128]{2,1,0:T(8,128)S(1)}, u32[]{:S(2)}, u32[]{:S(2)}) %collective-permute-start.3) | collective-permute-done | bytes 147488 | tf_op jit(solution)/shard_map/ppermute | solution.py:458
  94.7 0.0 copy-start.4
  94.7 1.6 %collective-permute-done.4.got_1 = f32[4,72,128]{2,1,0:T(8,128)S(1)} collective-permute-done((f32[4,72,128]{2,1,0:T(8,128)}, f32[4,72,128]{2,1,0:T(8,128)S(1)}, u32[]{:S(2)}, u32[]{:S(2)}) %collective-permute-start.4) | collective-permute-done | bytes 147488 | tf_op jit(solution)/shard_map/ppermute | solution.py:458
  96.3 0.0 copy-start.5
  96.3 0.0 copy-done.4
  96.3 0.7 copy-done.5
  97.0 1.9 %shard_map.97 = (f32[2,72,128]{2,1,0:T(8,128)}, f32[2,72,128]{2,1,0:T(8,128)}, f32[2,72,128]{2,1,0:T(8,128)}, f32[2,72,128]{2,1,0:T(8,128)}) custom-call(s32[4]{0:T(128)} %pad_add_fusion.dest_ref, f32[4,72,128]{2,1,0:T(8,128)} %get-tuple-element.24.keep_0, f32[4,72,128]{2,1,0:T(8,128)} %copy-done.4, f32[4,72,128]{2,1,0:T(8,128)} %get-tuple-element.26.keep_1, ...), custom_call_target="tpu_custom_call" | custom-call | tf_op jit(solution)/shard_map/pallas_call | solution.py:438
  98.8 0.0 collective-permute-start.5
  98.9 1.9 %collective-permute-start.6 = (f32[2,72,128]{2,1,0:T(8,128)}, f32[2,72,128]{2,1,0:T(8,128)S(1)}, u32[]{:S(2)}, u32[]{:S(2)}) collective-permute-start(f32[2,72,128]{2,1,0:T(8,128)} %get-tuple-element.30), channel_id=1, source_target_pairs={{0,4},{1,5},{2,6},{3,7},{4,0},{5,1},{6,2},{7,3},{8,12},{9,13},{10,... | collective-permute-start | bytes 221192 | tf_op jit(solution)/shard_map/ppermute | solution.py:458
  100.8 1.9 %collective-permute-start.7 = (f32[2,72,128]{2,1,0:T(8,128)}, f32[2,72,128]{2,1,0:T(8,128)S(1)}, u32[]{:S(2)}, u32[]{:S(2)}) collective-permute-start(f32[2,72,128]{2,1,0:T(8,128)} %get-tuple-element.31), channel_id=1, source_target_pairs={{0,6},{1,7},{2,0},{3,1},{4,2},{5,3},{6,4},{7,5},{8,14},{9,15},{10,... | collective-permute-start | bytes 221192 | tf_op jit(solution)/shard_map/ppermute | solution.py:458
  102.7 2.6 %collective-permute-done.5.refs_1_ = f32[2,72,128]{2,1,0:T(8,128)S(1)} collective-permute-done((f32[2,72,128]{2,1,0:T(8,128)}, f32[2,72,128]{2,1,0:T(8,128)S(1)}, u32[]{:S(2)}, u32[]{:S(2)}) %collective-permute-start.5) | collective-permute-done | bytes 73760 | tf_op jit(solution)/shard_map/ppermute | solution.py:458
  105.3 0.0 copy-start.9
  105.3 0.0 collective-permute-done.6.refs_2_
  105.3 0.0 copy-start.10
  105.3 0.8 collective-permute-done.7.refs_3_
  106.0 0.0 copy-start.11
  106.0 0.0 copy-done.9
  106.0 0.0 copy-done.10
  106.0 0.6 copy-done.11
  106.7 1.6 %shard_map.98 = f32[2,72,128]{2,1,0:T(8,128)} custom-call(f32[2,72,128]{2,1,0:T(8,128)} %get-tuple-element.28.refs_0_, f32[2,72,128]{2,1,0:T(8,128)} %copy-done.9, f32[2,72,128]{2,1,0:T(8,128)} %copy-done.10, f32[2,72,128]{2,1,0:T(8,128)} %copy-done.11), custom_call_target="tpu_custom_call" | custom-call | tf_op jit(solution)/shard_map/pallas_call | solution.py:438
  108.3 0.0 collective-permute-start.10
  108.3 0.5 collective-permute-start.9
  108.8 1.4 %collective-permute-start.8 = (f32[2,72,128]{2,1,0:T(8,128)}, f32[2,72,128]{2,1,0:T(8,128)S(1)}, u32[]{:S(2)}, u32[]{:S(2)}) collective-permute-start(f32[2,72,128]{2,1,0:T(8,128)} %shard_map.98), channel_id=1, source_target_pairs={{0,8},{1,9},{2,10},{3,11},{4,12},{5,13},{6,14},{7,15},{8,0},{9,1},... | collective-permute-start | bytes 221192 | tf_op jit(solution)/shard_map/ppermute | solution.py:458
  110.2 2.3 %collective-permute-done.10 = f32[2,72,128]{2,1,0:T(8,128)S(1)} collective-permute-done((f32[2,72,128]{2,1,0:T(8,128)}, f32[2,72,128]{2,1,0:T(8,128)S(1)}, u32[]{:S(2)}, u32[]{:S(2)}) %collective-permute-start.10) | collective-permute-done | bytes 73760 | tf_op jit(solution)/shard_map/ppermute | solution.py:458
  112.5 0.0 copy-start.6
  112.5 1.2 collective-permute-done.9
  113.7 0.0 copy-start.7
  113.7 0.0 collective-permute-done.8
  113.7 0.0 copy-start.8
  113.7 0.0 copy-done.6
  113.7 0.6 copy-done.7
  114.3 0.0 copy-done.8
  114.3 2.3 %shard_map.99 = f32[12,6144]{1,0:T(8,128)} custom-call(s32[4]{0:T(128)} %pad_add_fusion.dest_ref, f32[2,3,24,128]{3,2,1,0:T(8,128)} %bitcast.12, f32[2,3,24,128]{3,2,1,0:T(8,128)} %bitcast.15, f32[2,3,24,128]{3,2,1,0:T(8,128)} %bitcast.14, f32[2,3,24,128]{3,2,1,0:T(8,128)} %bitcast.13), custom_call_target="tpu_custom_call" | custom-call | tf_op jit(solution)/shard_map/pallas_call | solution.py:438
  (1 shorter events, 0.0 us)
Async XLA Ops:
  3.1 23.3 %copy-start.12 = (f32[2,16]{1,0:T(2,128)S(1)}, f32[2,16]{1,0:T(2,128)}, u32[]{:S(2)}) copy-start(f32[2,16]{1,0:T(2,128)} %param.14) | copy-start | bytes 388
  22.9 11.8 %all-to-all-start.1 = ((f32[8,64,128]{2,1,0:T(8,128)}), f32[8,64,128]{2,1,0:T(8,128)S(1)}, u32[]{:S(2)}, u32[]{:S(2)}) async-start(f32[8,64,128]{2,1,0:T(8,128)} %route.1), calls=%async_computation.1 | async-start | bytes 524288 | tf_op jit(solution)/shard_map/all_to_all | solution.py:399
  34.8 0.7 copy-start.1
  69.5 3.1 %collective-permute-start = (f32[8,2,2,3,24,128]{5,4,3,2,1,0:T(8,128)}, f32[8,2,2,3,24,128]{5,4,3,2,1,0:T(8,128)S(1)}, u32[]{:S(2)}, u32[]{:S(2)}) collective-permute-start(f32[8,2,2,3,24,128]{5,4,3,2,1,0:T(8,128)} %get-tuple-element.19), channel_id=1, source_target_pairs={{0,8},{1,9},{2,10},{3,11},{4,12},{5,13},{6,14},{7,15},{8,0},{9,1},... | collective-permute-start | bytes 3538952 | tf_op jit(solution)/shard_map/ppermute | solution.py:458
  72.6 1.0 copy-start
  76.4 9.3 %collective-permute-start.1 = (f32[4,2,72,128]{3,2,1,0:T(8,128)}, f32[4,2,72,128]{3,2,1,0:T(8,128)S(1)}, u32[]{:S(2)}, u32[]{:S(2)}) collective-permute-start(f32[4,2,72,128]{3,2,1,0:T(8,128)} %get-tuple-element.21), channel_id=1, source_target_pairs={{0,1},{1,0},{2,3},{3,2},{4,5},{5,4},{6,7},{7,6},{8,9},{9,8},{10,11... | collective-permute-start | bytes 884744 | tf_op jit(solution)/shard_map/ppermute | solution.py:458
  77.6 9.0 %collective-permute-start.2 = (f32[4,2,72,128]{3,2,1,0:T(8,128)}, f32[4,2,72,128]{3,2,1,0:T(8,128)S(1)}, u32[]{:S(2)}, u32[]{:S(2)}) collective-permute-start(f32[4,2,72,128]{3,2,1,0:T(8,128)} %get-tuple-element.23), channel_id=1, source_target_pairs={{0,16},{1,17},{2,18},{3,19},{4,20},{5,21},{6,22},{7,23},{8,24},{9,... | collective-permute-start | bytes 884744 | tf_op jit(solution)/shard_map/ppermute | solution.py:458
  85.6 0.9 copy-start.2
  86.6 0.7 copy-start.3
  89.4 5.4 %collective-permute-start.3 = (f32[4,72,128]{2,1,0:T(8,128)}, f32[4,72,128]{2,1,0:T(8,128)S(1)}, u32[]{:S(2)}, u32[]{:S(2)}) collective-permute-start(f32[4,72,128]{2,1,0:T(8,128)} %get-tuple-element.25), channel_id=1, source_target_pairs={{0,16},{1,17},{2,18},{3,19},{4,20},{5,21},{6,22},{7,23},{8,24},{9,... | collective-permute-start | bytes 442376 | tf_op jit(solution)/shard_map/ppermute | solution.py:458
  90.9 5.4 %collective-permute-start.4 = (f32[4,72,128]{2,1,0:T(8,128)}, f32[4,72,128]{2,1,0:T(8,128)S(1)}, u32[]{:S(2)}, u32[]{:S(2)}) collective-permute-start(f32[4,72,128]{2,1,0:T(8,128)} %get-tuple-element.27), channel_id=1, source_target_pairs={{0,1},{1,0},{2,3},{3,2},{4,5},{5,4},{6,7},{7,6},{8,9},{9,8},{10,11... | collective-permute-start | bytes 442376 | tf_op jit(solution)/shard_map/ppermute | solution.py:458
  94.7 1.6 %copy-start.4 = (f32[4,72,128]{2,1,0:T(8,128)}, f32[4,72,128]{2,1,0:T(8,128)S(1)}, u32[]{:S(2)}) copy-start(f32[4,72,128]{2,1,0:T(8,128)S(1)} %collective-permute-done.3.got_0) | copy-start | bytes 442372
  96.3 0.7 copy-start.5
  98.8 6.4 %collective-permute-start.5 = (f32[2,72,128]{2,1,0:T(8,128)}, f32[2,72,128]{2,1,0:T(8,128)S(1)}, u32[]{:S(2)}, u32[]{:S(2)}) collective-permute-start(f32[2,72,128]{2,1,0:T(8,128)} %get-tuple-element.29), channel_id=1, source_target_pairs={{0,2},{1,3},{2,4},{3,5},{4,6},{5,7},{6,0},{7,1},{8,10},{9,11},{10,... | collective-permute-start | bytes 221192 | tf_op jit(solution)/shard_map/ppermute | solution.py:458
  98.9 6.4 %collective-permute-start.6 = (f32[2,72,128]{2,1,0:T(8,128)}, f32[2,72,128]{2,1,0:T(8,128)S(1)}, u32[]{:S(2)}, u32[]{:S(2)}) collective-permute-start(f32[2,72,128]{2,1,0:T(8,128)} %get-tuple-element.30), channel_id=1, source_target_pairs={{0,4},{1,5},{2,6},{3,7},{4,0},{5,1},{6,2},{7,3},{8,12},{9,13},{10,... | collective-permute-start | bytes 221192 | tf_op jit(solution)/shard_map/ppermute | solution.py:458
  100.8 5.3 %collective-permute-start.7 = (f32[2,72,128]{2,1,0:T(8,128)}, f32[2,72,128]{2,1,0:T(8,128)S(1)}, u32[]{:S(2)}, u32[]{:S(2)}) collective-permute-start(f32[2,72,128]{2,1,0:T(8,128)} %get-tuple-element.31), channel_id=1, source_target_pairs={{0,6},{1,7},{2,0},{3,1},{4,2},{5,3},{6,4},{7,5},{8,14},{9,15},{10,... | collective-permute-start | bytes 221192 | tf_op jit(solution)/shard_map/ppermute | solution.py:458
  105.3 0.8 copy-start.9
  105.3 0.8 copy-start.10
  106.0 0.6 copy-start.11
  108.3 4.2 %collective-permute-start.10 = (f32[2,72,128]{2,1,0:T(8,128)}, f32[2,72,128]{2,1,0:T(8,128)S(1)}, u32[]{:S(2)}, u32[]{:S(2)}) collective-permute-start(f32[2,72,128]{2,1,0:T(8,128)} %shard_map.98), channel_id=1, source_target_pairs={{0,24},{1,25},{2,26},{3,27},{4,28},{5,29},{6,30},{7,31},{8,16},{9,... | collective-permute-start | bytes 221192 | tf_op jit(solution)/shard_map/ppermute | solution.py:458
  108.3 5.4 %collective-permute-start.9 = (f32[2,72,128]{2,1,0:T(8,128)}, f32[2,72,128]{2,1,0:T(8,128)S(1)}, u32[]{:S(2)}, u32[]{:S(2)}) collective-permute-start(f32[2,72,128]{2,1,0:T(8,128)} %shard_map.98), channel_id=1, source_target_pairs={{0,16},{1,17},{2,18},{3,19},{4,20},{5,21},{6,22},{7,23},{8,24},{9,... | collective-permute-start | bytes 221192 | tf_op jit(solution)/shard_map/ppermute | solution.py:458
  108.8 4.9 %collective-permute-start.8 = (f32[2,72,128]{2,1,0:T(8,128)}, f32[2,72,128]{2,1,0:T(8,128)S(1)}, u32[]{:S(2)}, u32[]{:S(2)}) collective-permute-start(f32[2,72,128]{2,1,0:T(8,128)} %shard_map.98), channel_id=1, source_target_pairs={{0,8},{1,9},{2,10},{3,11},{4,12},{5,13},{6,14},{7,15},{8,0},{9,1},... | collective-permute-start | bytes 221192 | tf_op jit(solution)/shard_map/ppermute | solution.py:458
  112.5 1.2 %copy-start.6 = (f32[2,72,128]{2,1,0:T(8,128)}, f32[2,72,128]{2,1,0:T(8,128)S(1)}, u32[]{:S(2)}) copy-start(f32[2,72,128]{2,1,0:T(8,128)S(1)} %collective-permute-done.10) | copy-start | bytes 221188
  113.7 0.6 copy-start.7
  113.7 0.7 copy-start.8

commit v2 on v1

--- a/solution.py
+++ b/solution.py
@@ -14,15 +14,18 @@
 DOMINANCE = 1.25
 PLANES = 8
 STEP = 4
+ENDS = 3
+EDGES = 20
 
 F32 = jnp.float32
 BF16 = jnp.bfloat16
 SMEM = pl.BlockSpec(memory_space=pltpu.SMEM)
 VMEM = pl.BlockSpec(memory_space=pltpu.VMEM)
-
-
-def params():
-    return pltpu.CompilerParams(vmem_limit_bytes=60 * 1024 * 1024)
+ANY = pl.BlockSpec(memory_space=pl.ANY)
+
+
+def params(mib):
+    return pltpu.CompilerParams(vmem_limit_bytes=mib * 1024 * 1024)
 
 
 def neighbours(v, axis):
@@ -42,15 +45,31 @@
     return beside, own
 
 
+def padded_stencil(ref, lead, i, count):
+    rows = ref.shape[-2] - 16
+    planes = pl.ds(i, count + 2)
+    v = ref[(*lead, planes, slice(8, 8 + rows))]
+    t = ref[(*lead, planes, slice(7, 7 + rows))] + ref[(*lead, planes, slice(9, 9 + rows))]
+    t_beside = t[:-2] + t[2:]
+    near = t[1:-1] + (v[:-2] + v[2:])
+    mixed = v[1:-1] + 0.5 * near + (1.0 / 3.0) * t_beside
+    return v[1:-1], near + 0.5 * t_beside + neighbours(mixed, mixed.ndim - 1)
+
+
 def split(v):
     high = v.astype(BF16)
     return high, (v - high.astype(F32)).astype(BF16)
 
 
-def dot3(a, b, contract_b=0):
+def thrice(v, axis, data):
+    high, low = split(v)
+    parts = [high, low, high] if data else [high, high, low]
+    return jnp.concatenate(parts, axis=axis)
+
+
+def dot(a, b, contract_b=0):
     numbers = (((1,), (contract_b,)), ((), ()))
-    mul = lambda p, q: lax.dot_general(p, q, numbers, preferred_element_type=F32)
-    return mul(a[0], b[0]) + (mul(a[0], b[1]) + mul(a[1], b[0]))
+    return lax.dot_general(a, b, numbers, preferred_element_type=F32)
 
 
 def pack_kernel(devs, len_ref, low_ref, up_ref, seed_ref, stiff_ref, out_ref, packet):
@@ -102,33 +121,150 @@
             out_ref[e, f * chunk : (f + 1) * chunk] = in_ref[source, pl.ds(start, chunk)]
 
 
-def main_kernel(
+def inner_kernel(len_ref, seed_ref, stiff_ref, out_ref, edge_ref, s_ext, w_ext, v_ext, fac_ref, mul_ref):
+    slots, nx, ny, nz = stiff_ref.shape
+    last = 8 + ny
+    zeros = jnp.zeros((nx + 2, 8, nz), F32)
+    for ref, lead in ((s_ext, ()), *((r, (c,)) for r in (w_ext, v_ext) for c in range(3))):
+        ref[(*lead, slice(None), slice(0, 8))] = zeros
+        ref[(*lead, slice(None), slice(last, last + 8))] = zeros
+        for i in (0, nx + 1):
+            ref[(*lead, i, slice(8, last))] = jnp.zeros((ny, nz), F32)
+
+    def loop(body):
+        def step(k, _):
+            body(k * STEP)
+            return 0
+
+        lax.fori_loop(0, nx // STEP, step, 0)
+
+    for b in range(slots):
+        length = len_ref[b]
+
+        def active_at(i, length=length):
+            return i + lax.broadcasted_iota(jnp.int32, (STEP, ny, nz), 0) < length
+
+        def fill(i, b=b, active_at=active_at):
+            s_ext[pl.ds(i + 1, STEP), 8:last] = jnp.where(
+                active_at(i), stiff_ref[b, pl.ds(i, STEP)], 0.0
+            )
+
+        loop(fill)
+
+        def first(i, b=b, active_at=active_at):
+            stiff, near = padded_stencil(s_ext, (), i, STEP)
+            active = active_at(i)
+            safe = jnp.where(active, DOMINANCE * stiff * near, 1.0)
+            inv = jnp.where(active, 1.0 / safe, 0.0)
+            fac = stiff * inv
+            fac_ref[pl.ds(i, STEP)] = fac
+            mul_ref[pl.ds(i, STEP)] = stiff * fac
+            for c in range(3):
+                seed = seed_ref[b, c, pl.ds(i, STEP)].astype(F32)
+                w_ext[c, pl.ds(i + 1, STEP), 8:last] = seed * fac
+                out_ref[b, c, pl.ds(i, STEP)] = seed * inv
+
+        loop(first)
+
+        for c in range(3):
+            for side in range(2):
+                f = 2 * b + side
+                for k, at in ((11 + c, 1), (14 + c, 2)):
+                    row = at if side == 0 else length - 1 - at
+                    edge_ref[f, k] = out_ref[b, c, row]
+
+        for c in range(3):
+
+            def second(i, c=c):
+                here, near = padded_stencil(w_ext, (c,), i, STEP)
+                v_ext[c, pl.ds(i + 1, STEP), 8:last] = here + mul_ref[pl.ds(i, STEP)] * near
+
+            loop(second)
+
+            def third(i, b=b, c=c):
+                _, near = padded_stencil(v_ext, (c,), i, STEP)
+                out_ref[b, c, pl.ds(i, STEP)] += fac_ref[pl.ds(i, STEP)] * near
+
+            loop(third)
+
+        for side in range(2):
+            f = 2 * b + side
+            at = [k if side == 0 else length - 1 - k for k in range(4)]
+            stiff = [stiff_ref[b, at[k]] for k in range(2)]
+            edge_ref[f, 0] = stiff[0]
+            edge_ref[f, 1] = plane_parts(stiff[0])[1] + plane_parts(stiff[1])[0]
+            mul_1, fac_1, fac_2 = mul_ref[at[1]], fac_ref[at[1]], fac_ref[at[2]]
+            edge_ref[f, 17], edge_ref[f, 18], edge_ref[f, 19] = mul_1, fac_1, fac_2
+            for c in range(3):
+                edge_ref[f, 2 + c] = seed_ref[b, c, at[0]].astype(F32)
+                w_1, w_2 = w_ext[c, at[1] + 1, 8:last], w_ext[c, at[2] + 1, 8:last]
+                v_2, v_3 = v_ext[c, at[2] + 1, 8:last], v_ext[c, at[3] + 1, 8:last]
+                beside, own = plane_parts(w_1)
+                edge_ref[f, 5 + c] = beside
+                edge_ref[f, 8 + c] = w_1 + mul_1 * (own + plane_parts(w_2)[0])
+                beside, own = plane_parts(v_2)
+                edge_ref[f, 11 + c] += fac_1 * beside
+                edge_ref[f, 14 + c] += fac_2 * (own + plane_parts(v_3)[0])
+
+
+def hat_along_z(coord, nz):
+    row = lax.broadcasted_iota(jnp.int32, (128, 3 * nz), 0)
+    lane = lax.broadcasted_iota(jnp.int32, (128, 3 * nz), 1)
+    point = (row % LZ).astype(F32)
+    hat = jnp.maximum(0.0, 1.0 - jnp.abs(point - jnp.concatenate([coord] * 3, axis=1)))
+    return thrice(jnp.where((row // LZ) == (lane // nz), hat, 0.0), 1, False)
+
+
+def lattice_kernel(len_ref, adj_ref, cx_ref, cz_ref, out_ref, zdone):
+    slots, _, nx, ny, nz = adj_ref.shape
+    group = 16
+    for b in range(slots):
+        hat_z = hat_along_z(cz_ref[b : b + 1, :], nz)
+        for x in range(0, nx, group):
+            rows = [adj_ref[b, c, x : x + group].reshape(group * ny, nz) for c in range(3)]
+            done = dot(thrice(jnp.concatenate(rows, axis=1), 1, True), hat_z, 1)
+            zdone[pl.ds((b * nx + x) * ny, group * ny)] = done
+        line = lax.broadcasted_iota(jnp.int32, (LX, 3 * nx), 0).astype(F32)
+        lane = lax.broadcasted_iota(jnp.int32, (LX, 3 * nx), 1)
+        x = lane % nx
+        hat = jnp.maximum(0.0, 1.0 - jnp.abs(line - cx_ref[b : b + 1, :]))
+        hat = jnp.where(jnp.logical_and(x >= ENDS, x < len_ref[b] - ENDS), hat, 0.0)
+        high, low = split(hat)
+        hat_x = jnp.where(lane < 2 * nx, high.astype(F32), low.astype(F32)).astype(BF16)
+        for y in range(0, ny, 2):
+            part = [zdone[pl.ds(b * nx * ny + y + k, nx, stride=ny), :] for k in range(2)]
+            done = dot(hat_x, thrice(jnp.concatenate(part, axis=1), 0, True))
+            for k in range(2):
+                at = pl.ds(b * ny + y + k, LX, stride=slots * ny)
+                out_ref[at, :] = done[:, 128 * k : 128 * (k + 1)]
+
+
+def outer_kernel(
     per,
     dest_ref,
     len_ref,
     low_ref,
     up_ref,
-    seed_ref,
-    stiff_ref,
+    cx_ref,
     halo_ref,
-    cx_ref,
+    edge_ref,
+    part_ref,
     cy_ref,
     cz_ref,
-    out_ref,
+    adj_in,
+    adj_out,
     keep_ref,
     send_ref,
     pack,
-    s_ext,
-    w_ext,
-    v_ext,
-    inv_ref,
-    fac_ref,
+    ends,
     zdone,
     xdone,
+    sems,
 ):
-    slots, nx, ny, nz = stiff_ref.shape
-    devs = halo_ref.shape[0]
-    chunk = halo_ref.shape[1] // (2 * slots)
+    del adj_in
+    faces, _, ny, nz = edge_ref.shape
+    slots = faces // 2
+    chunk = halo_ref.shape[1] // faces
     zero_plane = jnp.zeros((ny, nz), F32)
 
     for s in range(slots):
@@ -158,105 +294,68 @@
             def _(place=place):
                 place(False)
 
-    def sweep(get, finish):
-        before, _ = plane_parts(get(0, 1))
-        here, own = plane_parts(get(1, 1))
-
-        def body(step, carry):
-            before, here, own = carry
-            i = step * STEP
-            beside, mine = plane_parts(get(i + 2, STEP))
-            all_beside = jnp.concatenate([before, here, beside], axis=0)
-            all_own = jnp.concatenate([own, mine], axis=0)
-            near = all_own[:STEP] + all_beside[:STEP] + all_beside[2:]
-            finish(i, near)
-            return all_beside[STEP : STEP + 1], all_beside[STEP + 1 :], all_own[STEP:]
-
-        lax.fori_loop(0, nx // STEP, body, (before, here, own))
-
+    copies = []
+    for f in range(faces):
+        b, side = f // 2, f % 2
+        stiff, inside = edge_ref[f, 0], edge_ref[f, 1]
+        beside = plane_parts(stiff)[0]
+        there = 1.0 / (DOMINANCE * (pack[f, 1] + beside))
+        inv = 1.0 / (DOMINANCE * stiff * (inside + plane_parts(pack[f, 0])[0]))
+        fac = stiff * inv
+        mul_1, fac_1, fac_2 = edge_ref[f, 17], edge_ref[f, 18], edge_ref[f, 19]
+        for c in range(3):
+            seed = edge_ref[f, 2 + c]
+            w_n = pack[f, 2 + c] * there
+            w_0 = seed * fac
+            beside_n, own_n = plane_parts(w_n)
+            beside_0, own_0 = plane_parts(w_0)
+            v_n = w_n + pack[f, 0] * there * (own_n + pack[f, 5 + c] + beside_0)
+            v_0 = w_0 + stiff * fac * (own_0 + edge_ref[f, 5 + c] + beside_n)
+            v_1 = edge_ref[f, 8 + c] + mul_1 * beside_0
+            beside_n = plane_parts(v_n)[0]
+            beside_0, own_0 = plane_parts(v_0)
+            beside_1, own_1 = plane_parts(v_1)
+            rows = [
+                seed * inv + fac * (own_0 + beside_1 + beside_n),
+                edge_ref[f, 11 + c] + fac_1 * (own_1 + beside_0),
+                edge_ref[f, 14 + c] + fac_2 * beside_1,
+            ]
+            for k, row in enumerate(rows):
+                ends[b, c, k if side == 0 else 2 * ENDS - 1 - k] = row
+            start = 0 if side == 0 else len_ref[b] - ENDS
+            copy = pltpu.make_async_copy(
+                ends.at[b, c, pl.ds(side * ENDS, ENDS)],
+                adj_out.at[b, c, pl.ds(start, ENDS)],
+                sems.at[f, c],
+            )
+            copy.start()
+            copies.append(copy)
+
+    eight = 8
+    line = lax.broadcasted_iota(jnp.int32, (LX, 4 * eight), 0).astype(F32)
+    lane = lax.broadcasted_iota(jnp.int32, (LX, 4 * eight), 1)
     for b in range(slots):
-        length = len_ref[b]
-        lower, upper = 2 * b, 2 * b + 1
-
-        def fill(step, _, b=b, length=length):
-            i = step * STEP
-            at = i + lax.broadcasted_iota(jnp.int32, (STEP, ny, nz), 0)
-            s_ext[pl.ds(i + 1, STEP)] = jnp.where(at < length, stiff_ref[b, pl.ds(i, STEP)], 0.0)
-            return 0
-
-        lax.fori_loop(0, nx // STEP, fill, 0)
-        s_ext[nx + 1] = zero_plane
-        s_ext[0] = pack[lower, 0]
-        s_ext[length + 1] = pack[upper, 0]
-
-        def first(i, near, b=b, length=length):
-            at = i + lax.broadcasted_iota(jnp.int32, (STEP, ny, nz), 0)
-            active = at < length
-            stiff = jnp.where(active, stiff_ref[b, pl.ds(i, STEP)], 0.0)
-            safe = jnp.where(active, DOMINANCE * stiff * near, 1.0)
-            inv = jnp.where(active, 1.0 / safe, 0.0)
-            fac = stiff * inv
-            inv_ref[pl.ds(i, STEP)] = inv
-            fac_ref[pl.ds(i, STEP)] = fac
-            for c in range(3):
-                w_ext[c, pl.ds(i + 1, STEP)] = seed_ref[b, c, pl.ds(i, STEP)].astype(F32) * fac
-
-        sweep(lambda i, n: s_ext[pl.ds(i, n)], first)
-
-        ends = ((lower, 1, 0), (upper, length, length + 1))
-        for f, mine, there in ends:
-            near = pack[f, 1] + plane_parts(stiff_ref[b, mine - 1])[0]
-            fac = 1.0 / (DOMINANCE * near)
-            for c in range(3):
-                weighted = pack[f, 2 + c] * fac
-                beside, own = plane_parts(weighted)
-                total = own + pack[f, 5 + c] + plane_parts(w_ext[c, mine])[0]
-                v_ext[c, there] = (pack[f, 2 + c] + pack[f, 0] * total) * fac
-                pack[f, 5 + c] = weighted
-        for c in range(3):
-            w_ext[c, nx + 1] = zero_plane
-        for f, mine, there in ends:
-            for c in range(3):
-                w_ext[c, there] = pack[f, 5 + c]
-        keep_ends = [[v_ext[c, there] for c in range(3)] for f, mine, there in ends]
-
-        for c in range(3):
-
-            def second(i, near, b=b, c=c):
-                seed = seed_ref[b, c, pl.ds(i, STEP)].astype(F32)
-                stiff = stiff_ref[b, pl.ds(i, STEP)]
-                v_ext[c, pl.ds(i + 1, STEP)] = (seed + stiff * near) * fac_ref[pl.ds(i, STEP)]
-
-            sweep(lambda i, n, c=c: w_ext[c, pl.ds(i, n)], second)
-            v_ext[c, nx + 1] = zero_plane
-            v_ext[c, 0] = keep_ends[0][c]
-            v_ext[c, length + 1] = keep_ends[1][c]
-
-            def third(i, near, b=b, c=c):
-                seed = seed_ref[b, c, pl.ds(i, STEP)].astype(F32)
-                stiff = stiff_ref[b, pl.ds(i, STEP)]
-                out_ref[b, c, pl.ds(i, STEP)] = (seed + stiff * near) * inv_ref[pl.ds(i, STEP)]
-
-            sweep(lambda i, n, c=c: v_ext[c, pl.ds(i, n)], third)
-
-    group = 16
-    row = lax.broadcasted_iota(jnp.int32, (128, 3 * nz), 0)
-    lane = lax.broadcasted_iota(jnp.int32, (128, 3 * nz), 1)
-    same = (row // LZ) == (lane // nz)
-    point = (row % LZ).astype(F32)
-    for b in range(slots):
-        cz = cz_ref[b : b + 1, :]
-        hat_z = jnp.maximum(0.0, 1.0 - jnp.abs(point - jnp.concatenate([cz, cz, cz], axis=1)))
-        hat_z = split(jnp.where(same, hat_z, 0.0))
-        for x in range(0, nx, group):
-            rows = [out_ref[b, c, x : x + group].reshape(group * ny, nz) for c in range(3)]
-            done = dot3(split(jnp.concatenate(rows, axis=1)), hat_z, 1)
-            zdone[pl.ds((b * nx + x) * ny, group * ny)] = done
-        line = lax.broadcasted_iota(jnp.int32, (LX, nx), 0).astype(F32)
-        hat_x = split(jnp.maximum(0.0, 1.0 - jnp.abs(line - cx_ref[b : b + 1, :])))
-        for y in range(ny):
-            part = zdone[pl.ds(b * nx * ny + y, nx, stride=ny), :]
-            xdone[pl.ds(b * ny + y, LX, stride=slots * ny), :] = dot3(hat_x, split(part))
+        hat_z = hat_along_z(cz_ref[b : b + 1, :], nz)
+        rows = [ends[b, c].reshape(2 * ENDS * ny, nz) for c in range(3)]
+        done = dot(thrice(jnp.concatenate(rows, axis=1), 1, True), hat_z, 1)
+        zdone[0 : 2 * ENDS * ny] = done
+        zdone[2 * ENDS * ny : eight * ny] = jnp.zeros(((eight - 2 * ENDS) * ny, 128), F32)
+        coord = jnp.full((LX, 4 * eight), -4.0, F32)
+        for k in range(2 * ENDS):
+            at = k if k < ENDS else len_ref[b] - 2 * ENDS + k
+            coord = jnp.where(lane % eight == k, cx_ref[b, at], coord)
+        hat = jnp.maximum(0.0, 1.0 - jnp.abs(line - coord))
+        high, low = split(hat)
+        hat_x = jnp.where(lane < 2 * eight, high.astype(F32), low.astype(F32)).astype(BF16)
+        for y in range(0, ny, 2):
+            part = [zdone[pl.ds(y + k, eight, stride=ny), :] for k in range(2)]
+            high, low = split(jnp.concatenate(part, axis=1))
+            high, low = high.astype(F32), low.astype(F32)
+            stack = jnp.concatenate([high, low, high, jnp.zeros_like(high)], axis=0)
+            done = dot(hat_x, stack.astype(BF16))
+            for k in range(2):
+                at = pl.ds(b * ny + y + k, LX, stride=slots * ny)
+                xdone[at, :] = done[:, 128 * k : 128 * (k + 1)]
 
     depth = per * slots * ny
     row = lax.broadcasted_iota(jnp.int32, (LY * per, depth), 0).astype(F32)
@@ -265,35 +364,43 @@
     inside = row - which * per
     owner = jnp.floor((lane + 0.5) * (1.0 / (slots * ny)))
     hat_y = jnp.maximum(0.0, 1.0 - jnp.abs(which - cy_ref[...]))
-    hat_y = split(jnp.where(inside == owner, hat_y, 0.0))
+    hat_y = thrice(jnp.where(inside == owner, hat_y, 0.0), 1, False)
     third_rows = LY // 4 * per
     pieces = keep_ref.shape[3]
+    size = 3 * third_rows // 8
     tail = lax.broadcasted_iota(jnp.int32, (third_rows, 128), 1) >= 3 * LZ
 
-    def close(number, _):
-        start = number * depth
-        if depth % 8 == 0:
-            start = pl.multiple_of(start, 8)
-        done = dot3(hat_y, split(xdone[pl.ds(start, depth), :]))
-        last = done[3 * third_rows :]
-        dense = []
-        for q in range(3):
-            moved = pltpu.roll(last, 3 * LZ - q * LZ, 1)
-            dense.append(jnp.where(tail, moved, done[q * third_rows : (q + 1) * third_rows]))
-        dense = jnp.concatenate(dense, axis=0)
-        size = 3 * third_rows // 8
-        d, t = number // pieces, number % pieces
-        for core in range(2):
-
-            @pl.when(dest_ref[0] == core)
-            def _(core=core):
-                for g in range(8):
-                    ref = keep_ref if g // 4 == core else send_ref
-                    ref[d, g // 2 % 2, g % 2, t] = dense[g * size : (g + 1) * size]
+    def close(pair, _):
+        terms = []
+        for k in range(2):
+            start = (2 * pair + k) * depth
+            if depth % 8 == 0:
+                start = pl.multiple_of(start, 8)
+            terms.append(part_ref[pl.ds(start, depth), :] + xdone[pl.ds(start, depth), :])
+        both = dot(hat_y, thrice(jnp.concatenate(terms, axis=1), 0, True))
+        for k in range(2):
+            done = both[:, 128 * k : 128 * (k + 1)]
+            tops = done[3 * third_rows :]
+            dense = []
+            for q in range(3):
+                moved = pltpu.roll(tops, 3 * LZ - q * LZ, 1)
+                dense.append(jnp.where(tail, moved, done[q * third_rows : (q + 1) * third_rows]))
+            dense = jnp.concatenate(dense, axis=0)
+            number = 2 * pair + k
+            d, t = number // pieces, number % pieces
+            for core in range(2):
+
+                @pl.when(dest_ref[0] == core)
+                def _(core=core, dense=dense, d=d, t=t):
+                    for g in range(8):
+                        ref = keep_ref if g // 4 == core else send_ref
+                        ref[d, g // 2 % 2, g % 2, t] = dense[g * size : (g + 1) * size]
 
         return 0
 
-    lax.fori_loop(0, LX // per, close, 0)
+    lax.fori_loop(0, LX // per // 2, close, 0)
+    for copy in copies:
+        copy.wait()
 
 
 def core_kernel(dest_ref, keep_ref, got_ref, keep_y, send_y, keep_x, send_x):
@@ -384,52 +491,77 @@
         in_specs=[SMEM, SMEM, SMEM, VMEM, VMEM],
         out_specs=VMEM,
         scratch_shapes=[pltpu.VMEM((faces, PLANES * ny, nz), F32)],
-        compiler_params=params(),
+        compiler_params=params(8),
         name="pack",
     )(lengths, low, up, seed, stiff)
     spread = lax.all_to_all(packed, "dev", 0, 0)
+    ext = (nx + 2, ny + 16, nz)
+    plain = pltpu.VMEM((nx, ny, nz), F32)
+    early, edges = pl.pallas_call(
+        inner_kernel,
+        out_shape=(shape(slots, 3, nx, ny, nz), shape(faces, EDGES, ny, nz)),
+        in_specs=[SMEM, VMEM, VMEM],
+        out_specs=(VMEM, VMEM),
+        scratch_shapes=[
+            pltpu.VMEM(ext, F32),
+            pltpu.VMEM((3, *ext), F32),
+            pltpu.VMEM((3, *ext), F32),
+            plain,
+            plain,
+        ],
+        compiler_params=params(24),
+        cost_estimate=pl.CostEstimate(flops=4 * 10**8, bytes_accessed=2 * 10**7, transcendentals=0),
+        name="inner",
+    )(lengths, seed, stiff)
     routed = pl.pallas_call(
         route_kernel,
         out_shape=shape(devs, rows, nz),
         in_specs=[VMEM],
         out_specs=VMEM,
-        compiler_params=params(),
+        compiler_params=params(4),
         name="route",
     )(spread)
+    early, routed = lax.optimization_barrier((early, routed))
     halos = lax.all_to_all(routed, "dev", 0, 0)
-
-    ext = pltpu.VMEM((nx + 2, ny, nz), F32)
-    ext3 = pltpu.VMEM((3, nx + 2, ny, nz), F32)
-    plain = pltpu.VMEM((nx, ny, nz), F32)
+    inside = pl.pallas_call(
+        lattice_kernel,
+        out_shape=shape(LX * slots * ny, 128),
+        in_specs=[SMEM, VMEM, VMEM, VMEM],
+        out_specs=VMEM,
+        scratch_shapes=[pltpu.VMEM((slots * nx * ny, 128), F32)],
+        compiler_params=params(16),
+        cost_estimate=pl.CostEstimate(flops=2 * 10**9, bytes_accessed=2 * 10**7, transcendentals=0),
+        name="lattice",
+    )(lengths, early, jnp.tile(coord_x, (1, 3)), coord_z)
+
     half = shape(devs, 2, 2, pieces, size, 128)
     adjoint, keep, send = pl.pallas_call(
-        functools.partial(main_kernel, per),
+        functools.partial(outer_kernel, per),
         out_shape=(shape(slots, 3, nx, ny, nz), half, half),
-        in_specs=[SMEM] * 4 + [VMEM] * 6,
-        out_specs=(VMEM,) * 3,
+        in_specs=[SMEM] * 5 + [VMEM] * 5 + [ANY],
+        out_specs=(ANY, VMEM, VMEM),
         scratch_shapes=[
             pltpu.VMEM((faces, PLANES, ny, nz), F32),
-            ext,
-            ext3,
-            ext3,
-            plain,
-            plain,
-            pltpu.VMEM((slots * nx * ny, 128), F32),
+            pltpu.VMEM((slots, 3, 2 * ENDS, ny, nz), F32),
+            pltpu.VMEM((8 * ny, 128), F32),
             pltpu.VMEM((LX * slots * ny, 128), F32),
+            pltpu.SemaphoreType.DMA((faces, 3)),
         ],
-        compiler_params=params(),
-        name="main",
+        input_output_aliases={10: 0},
+        compiler_params=params(16),
+        name="outer",
     )(
         dest,
         lengths,
         low,
         up,
-        seed,
-        stiff,
+        coord_x,
         halos,
-        coord_x,
+        edges,
+        inside,
         jnp.tile(coord_y.reshape(1, slots * ny), (1, per)),
         coord_z,
+        early,
     )
 
     scale = math.sqrt(LX * LY * LZ / (groups * devs * slots * nx * ny * nz))
@@ -441,7 +573,7 @@
             in_specs=[SMEM if a is dest else VMEM for a in args],
             out_specs=jax.tree.map(lambda _: VMEM, outs),
             scratch_shapes=scratch,
-            compiler_params=params(),
+            compiler_params=params(8),
         )(*args)
 
     piece = (2, pieces, size, 128)

time: 117 us -> 93.5 us (0.80)
  blocking collectives: 17.9 us -> 0 us
  Pallas kernels: 49.2 us -> 37.3 us
  starting transfers between devices: 14.1 us -> 24.3 us
  waiting for transfers between devices: 29 us -> 24.1 us
  local copies, waits for them, and re-layouts: 5.03 us -> 6.37 us
    all_to_all x1 -> x0, blocking collectives: 17.9 us -> none  [on_device(): spread = lax.all_to_all(packed, 'dev', 0, 0)]
    all_to_all x0 -> x1, starting transfers between devices: none -> 7.31 us  [on_device(): spread = lax.all_to_all(packed, 'dev', 0, 0)]
    pallas_call x5, Pallas kernels: 10.7 us -> 3.73 us  [small(): pl.pallas_call(kernel, out_shape=outs, in_specs=[SMEM if a is dest else V...]
    all_to_all x1, waiting for transfers between devices: 7.05 us -> 3.09 us  [on_device(): halos = lax.all_to_all(routed, 'dev', 0, 0)]
    pallas_call x1 -> x3, Pallas kernels: 34.1 us -> 31.1 us  [the longest x1 19.8 us: on_device(): pl.pallas_call(inner_kernel, out_shape=(shape(slots, 3, nx, ny, nz), shap...]
    all_to_all x1, starting transfers between devices: 3.41 us -> 5.99 us  [on_device(): halos = lax.all_to_all(routed, 'dev', 0, 0)]
    unnamed x26 -> x28, local copies, waits for them, and re-layouts: 4.38 us -> 6.12 us
  transfers between devices with their start and end apart: 12 -> 13, of which waited for: 10 -> 10; matrix products, arithmetic and copies ran while one was open for 1% -> 0% of each run, Pallas kernels for 0% -> 25%
where the time goes in v2:
time: 93.5 us; the launch traced here: 93 us
  Pallas kernels  37.3 us (40%)
  starting transfers between devices  24.3 us (26%)
  waiting for transfers between devices  24.1 us (26%)
  local copies, waits for them, and re-layouts  6.37 us (7%)
    ppermute x11, waiting for transfers between devices, move(): return lax.ppermute(value, ('group', 'dev'), links)  21.1 us
    pallas_call x1, Pallas kernels, on_device(): pl.pallas_call(inner_kernel, out_shape=(shape(slots, 3, nx, ny, nz), shap...  19.8 us
    ppermute x11, starting transfers between devices, move(): return lax.ppermute(value, ('group', 'dev'), links)  11 us
    pallas_call x1, Pallas kernels, on_device(): pl.pallas_call(functools.partial(outer_kernel, per), out_shape=(shape(slo...  7.9 us
    all_to_all x1, starting transfers between devices, on_device(): spread = lax.all_to_all(packed, 'dev', 0, 0)  7.31 us
    unnamed x28, local copies, waits for them, and re-layouts  6.12 us
    all_to_all x1, starting transfers between devices, on_device(): halos = lax.all_to_all(routed, 'dev', 0, 0)  5.99 us
    pallas_call x5, Pallas kernels, small(): pl.pallas_call(kernel, out_shape=outs, in_specs=[SMEM if a is dest else V...  3.73 us
  transfers between devices with their start and end apart: 13, of which 10 were waited for; matrix products, arithmetic and copies ran while one was open for 0% of the time, Pallas kernels for 25%

profile of v2, /device:TPU:0, one launch (start us, length us, event | category | flops | bytes accessed | tf_op | source)
XLA Modules:
  0.0 93.0 jit_solution(366020214393588712)
XLA Ops:
  0.6 0.0 copy-start
  0.6 1.3 %copy-done = bf16[2,3,48,16,128]{4,3,2,1,0:T(8,128)(2,1)S(1)} copy-done((bf16[2,3,48,16,128]{4,3,2,1,0:T(8,128)(2,1)S(1)}, bf16[2,3,48,16,128]{4,3,2,1,0:T(8,128)(2,1)}, u32[]{:S(2)}) %copy-start) | copy-done | bytes 1179672
  1.9 0.0 copy-start.2
  1.9 1.1 %copy-done.2 = f32[2,48,16,128]{3,2,1,0:T(8,128)S(1)} copy-done((f32[2,48,16,128]{3,2,1,0:T(8,128)S(1)}, f32[2,48,16,128]{3,2,1,0:T(8,128)}, u32[]{:S(2)}) %copy-start.2) | copy-done | bytes 786456
  3.0 0.0 copy-start.5
  3.0 0.7 copy-done.5
  3.7 0.0 copy-start.7
  3.7 0.7 copy-done.7
  4.4 0.0 copy-start.9
  4.4 0.7 copy-done.9
  5.0 0.0 copy-start.1
  5.1 0.0 copy-start.3
  5.1 0.0 copy-start.6
  5.1 1.5 %pack.1 = f32[8,72,128]{2,1,0:T(8,128)} custom-call(s32[2]{0:T(128)S(1)} %copy-done.5, s32[2,3]{1,0:T(2,128)S(1)} %copy-done.7, s32[2,3]{1,0:T(2,128)S(1)} %copy-done.9, bf16[2,3,48,16,128]{4,3,2,1,0:T(8,128)(2,1)S(1)} %copy-done, f32[2,48,16,128]{3,2,1,0:T(8,128)S(1)} %copy-done.2), custom_call_target="tpu_custom_call" | custom-call | tf_op jit(solution)/shard_map/pack/pallas_call | solution.py:488
  6.6 7.3 %all-to-all-start = ((f32[8,72,128]{2,1,0:T(8,128)}), f32[8,72,128]{2,1,0:T(8,128)S(1)}, u32[]{:S(2)}, u32[]{:S(2)}) async-start(f32[8,72,128]{2,1,0:T(8,128)} %pack.1), calls=%async_computation | async-start | bytes 589824 | tf_op jit(solution)/shard_map/all_to_all | solution.py:497
  13.9 0.0 copy-done.1
  13.9 0.0 copy-done.3
  13.9 0.0 copy-done.6
  13.9 0.0 copy-start.13
  13.9 0.0 copy-start.11
  14.0 0.0 copy-start.12
  14.0 19.8 %inner.1 = (f32[2,3,48,16,128]{4,3,2,1,0:T(8,128)}, f32[4,20,16,128]{3,2,1,0:T(8,128)S(1)}) custom-call(s32[2]{0:T(128)S(1)} %copy-done.6, bf16[2,3,48,16,128]{4,3,2,1,0:T(8,128)(2,1)S(1)} %copy-done.1, f32[2,48,16,128]{3,2,1,0:T(8,128)S(1)} %copy-done.3), custom_call_target="tpu_custom_call" | custom-call | flops 400000000 | bytes 20000000 | tf_op jit(solution)/shard_map/inner/pallas_call | solution.py:500
  33.7 0.0 all-to-all-done.in_ref
  33.8 1.0 %route.1 = f32[8,64,128]{2,1,0:T(8,128)} custom-call(f32[8,72,128]{2,1,0:T(8,128)S(1)} %all-to-all-done.in_ref), custom_call_target="tpu_custom_call" | custom-call | tf_op jit(solution)/shard_map/route/pallas_call | solution.py:516
  34.7 6.0 %all-to-all-start.1 = ((f32[8,64,128]{2,1,0:T(8,128)}), f32[8,64,128]{2,1,0:T(8,128)S(1)}, u32[]{:S(2)}, u32[]{:S(2)}) async-start(f32[8,64,128]{2,1,0:T(8,128)} %route.1), calls=%async_computation.1 | async-start | bytes 524288 | tf_op jit(solution)/shard_map/all_to_all | solution.py:525
  40.7 0.0 copy-done.13
  40.7 0.1 tile.21
  40.8 0.1 tile.23.cy_ref
  40.9 0.0 copy-done.11
  40.9 0.1 tile.20.cx_ref
  41.0 0.1 pad_add_fusion.dest_ref
  41.1 0.0 copy-done.12
  41.1 1.7 %copy-done.4 = f32[2,3,48,16,128]{4,3,2,1,0:T(8,128)S(1)} copy-done((f32[2,3,48,16,128]{4,3,2,1,0:T(8,128)S(1)}, f32[2,3,48,16,128]{4,3,2,1,0:T(8,128)}, u32[]{:S(2)}) %copy-start.4) | copy-done | bytes 2359320
  42.8 3.4 %lattice.1.part_ref = f32[3072,128]{1,0:T(8,128)S(1)} custom-call(s32[2]{0:T(128)S(1)} %copy-done.6, f32[2,3,48,16,128]{4,3,2,1,0:T(8,128)S(1)} %copy-done.4, f32[2,144]{1,0:T(2,128)S(1)} %tile.20.cx_ref, f32[2,128]{1,0:T(2,128)S(1)} %copy-done.12), custom_call_target="tpu_custom_call" | custom-call | flops 2000000000 | bytes 20000000 | tf_op jit(solution)/shard_map/lattice/pallas_call | solution.py:526
  46.1 3.1 %all-to-all-done.1.halo_ref = f32[8,64,128]{2,1,0:T(8,128)S(1)} async-done(((f32[8,64,128]{2,1,0:T(8,128)}), f32[8,64,128]{2,1,0:T(8,128)S(1)}, u32[]{:S(2)}, u32[]{:S(2)}) %all-to-all-start.1) | async-done | bytes 262176 | tf_op jit(solution)/shard_map/all_to_all | solution.py:525
  49.2 0.0 copy-done.8
  49.2 0.0 copy-done.10
  49.2 7.9 %outer.1 = (f32[2,3,48,16,128]{4,3,2,1,0:T(8,128)}, f32[8,2,2,3,24,128]{5,4,3,2,1,0:T(8,128)S(1)}, f32[8,2,2,3,24,128]{5,4,3,2,1,0:T(8,128)S(1)}) custom-call(s32[4]{0:T(128)S(1)} %pad_add_fusion.dest_ref, s32[2]{0:T(128)S(1)} %copy-done.6, s32[2,3]{1,0:T(2,128)S(1)} %copy-done.8, s32[2,3]{1,0:T(2,128)S(1)} %copy-done.10, ...), custom_call_target="tpu_custom_call", output_to_operand_aliasing={{0}: (10, {})} | custom-call | tf_op jit(solution)/shard_map/outer/pallas_call | solution.py:538
  57.1 0.1 collective-permute-start
  57.2 2.8 %collective-permute-done = f32[8,2,2,3,24,128]{5,4,3,2,1,0:T(8,128)S(1)} collective-permute-done((f32[8,2,2,3,24,128]{5,4,3,2,1,0:T(8,128)S(1)}, f32[8,2,2,3,24,128]{5,4,3,2,1,0:T(8,128)S(1)}, u32[]{:S(2)}, u32[]{:S(2)}) %collective-permute-start) | collective-permute-done | bytes 1179680 | tf_op jit(solution)/shard_map/ppermute | solution.py:590
  60.1 0.7 shard_map.95
  60.8 1.4 %collective-permute-start.1 = (f32[4,2,72,128]{3,2,1,0:T(8,128)S(1)}, f32[4,2,72,128]{3,2,1,0:T(8,128)S(1)}, u32[]{:S(2)}, u32[]{:S(2)}) collective-permute-start(f32[4,2,72,128]{3,2,1,0:T(8,128)S(1)} %get-tuple-element.29), channel_id=1, source_target_pairs={{0,1},{1,0},{2,3},{3,2},{4,5},{5,4},{6,7},{7,6},{8,9},{9,8},{10,11... | collective-permute-start | bytes 884744 | tf_op jit(solution)/shard_map/ppermute | solution.py:590
  62.2 1.5 %collective-permute-start.2 = (f32[4,2,72,128]{3,2,1,0:T(8,128)S(1)}, f32[4,2,72,128]{3,2,1,0:T(8,128)S(1)}, u32[]{:S(2)}, u32[]{:S(2)}) collective-permute-start(f32[4,2,72,128]{3,2,1,0:T(8,128)S(1)} %get-tuple-element.31), channel_id=1, source_target_pairs={{0,16},{1,17},{2,18},{3,19},{4,20},{5,21},{6,22},{7,23},{8,24},{9,... | collective-permute-start | bytes 884744 | tf_op jit(solution)/shard_map/ppermute | solution.py:590
  63.6 6.2 %collective-permute-done.1.got_y = f32[4,2,72,128]{3,2,1,0:T(8,128)S(1)} collective-permute-done((f32[4,2,72,128]{3,2,1,0:T(8,128)S(1)}, f32[4,2,72,128]{3,2,1,0:T(8,128)S(1)}, u32[]{:S(2)}, u32[]{:S(2)}) %collective-permute-start.1) | collective-permute-done | bytes 294944 | tf_op jit(solution)/shard_map/ppermute | solution.py:590
  69.9 1.1 %collective-permute-done.2.got_x = f32[4,2,72,128]{3,2,1,0:T(8,128)S(1)} collective-permute-done((f32[4,2,72,128]{3,2,1,0:T(8,128)S(1)}, f32[4,2,72,128]{3,2,1,0:T(8,128)S(1)}, u32[]{:S(2)}, u32[]{:S(2)}) %collective-permute-start.2) | collective-permute-done | bytes 294944 | tf_op jit(solution)/shard_map/ppermute | solution.py:590
  70.9 0.6 shard_map.96
  71.6 1.5 %collective-permute-start.3 = (f32[4,72,128]{2,1,0:T(8,128)S(1)}, f32[4,72,128]{2,1,0:T(8,128)S(1)}, u32[]{:S(2)}, u32[]{:S(2)}) collective-permute-start(f32[4,72,128]{2,1,0:T(8,128)S(1)} %get-tuple-element.33), channel_id=1, source_target_pairs={{0,16},{1,17},{2,18},{3,19},{4,20},{5,21},{6,22},{7,23},{8,24},{9,... | collective-permute-start | bytes 442376 | tf_op jit(solution)/shard_map/ppermute | solution.py:590
  73.1 0.8 collective-permute-start.4
  73.8 2.9 %collective-permute-done.3.got_0 = f32[4,72,128]{2,1,0:T(8,128)S(1)} collective-permute-done((f32[4,72,128]{2,1,0:T(8,128)S(1)}, f32[4,72,128]{2,1,0:T(8,128)S(1)}, u32[]{:S(2)}, u32[]{:S(2)}) %collective-permute-start.3) | collective-permute-done | bytes 147488 | tf_op jit(solution)/shard_map/ppermute | solution.py:590
  76.8 1.5 %collective-permute-done.4.got_1 = f32[4,72,128]{2,1,0:T(8,128)S(1)} collective-permute-done((f32[4,72,128]{2,1,0:T(8,128)S(1)}, f32[4,72,128]{2,1,0:T(8,128)S(1)}, u32[]{:S(2)}, u32[]{:S(2)}) %collective-permute-start.4) | collective-permute-done | bytes 147488 | tf_op jit(solution)/shard_map/ppermute | solution.py:590
  78.2 0.6 shard_map.97
  78.8 0.1 collective-permute-start.5
  78.9 2.0 %collective-permute-start.6 = (f32[2,72,128]{2,1,0:T(8,128)S(1)}, f32[2,72,128]{2,1,0:T(8,128)S(1)}, u32[]{:S(2)}, u32[]{:S(2)}) collective-permute-start(f32[2,72,128]{2,1,0:T(8,128)S(1)} %get-tuple-element.38), channel_id=1, source_target_pairs={{0,4},{1,5},{2,6},{3,7},{4,0},{5,1},{6,2},{7,3},{8,12},{9,13},{10,... | collective-permute-start | bytes 221192 | tf_op jit(solution)/shard_map/ppermute | solution.py:590
  80.8 1.8 %collective-permute-start.7 = (f32[2,72,128]{2,1,0:T(8,128)S(1)}, f32[2,72,128]{2,1,0:T(8,128)S(1)}, u32[]{:S(2)}, u32[]{:S(2)}) collective-permute-start(f32[2,72,128]{2,1,0:T(8,128)S(1)} %get-tuple-element.39), channel_id=1, source_target_pairs={{0,6},{1,7},{2,0},{3,1},{4,2},{5,3},{6,4},{7,5},{8,14},{9,15},{10,... | collective-permute-start | bytes 221192 | tf_op jit(solution)/shard_map/ppermute | solution.py:590
  82.7 2.4 %collective-permute-done.5.refs_1_ = f32[2,72,128]{2,1,0:T(8,128)S(1)} collective-permute-done((f32[2,72,128]{2,1,0:T(8,128)S(1)}, f32[2,72,128]{2,1,0:T(8,128)S(1)}, u32[]{:S(2)}, u32[]{:S(2)}) %collective-permute-start.5) | collective-permute-done | bytes 73760 | tf_op jit(solution)/shard_map/ppermute | solution.py:590
  85.1 0.0 collective-permute-done.6.refs_2_
  85.1 0.8 collective-permute-done.7.refs_3_
  85.9 0.1 collective-permute-start.10
  86.0 0.6 collective-permute-start.9
  86.5 1.3 %collective-permute-start.8 = (f32[2,72,128]{2,1,0:T(8,128)S(1)}, f32[2,72,128]{2,1,0:T(8,128)S(1)}, u32[]{:S(2)}, u32[]{:S(2)}) collective-permute-start(f32[2,72,128]{2,1,0:T(8,128)S(1)} %shard_map.98), channel_id=1, source_target_pairs={{0,8},{1,9},{2,10},{3,11},{4,12},{5,13},{6,14},{7,15},{8,0},{9,1},... | collective-permute-start | bytes 221192 | tf_op jit(solution)/shard_map/ppermute | solution.py:590
  87.8 2.0 %collective-permute-done.10 = f32[2,72,128]{2,1,0:T(8,128)S(1)} collective-permute-done((f32[2,72,128]{2,1,0:T(8,128)S(1)}, f32[2,72,128]{2,1,0:T(8,128)S(1)}, u32[]{:S(2)}, u32[]{:S(2)}) %collective-permute-start.10) | collective-permute-done | bytes 73760 | tf_op jit(solution)/shard_map/ppermute | solution.py:590
  89.8 1.3 %collective-permute-done.9 = f32[2,72,128]{2,1,0:T(8,128)S(1)} collective-permute-done((f32[2,72,128]{2,1,0:T(8,128)S(1)}, f32[2,72,128]{2,1,0:T(8,128)S(1)}, u32[]{:S(2)}, u32[]{:S(2)}) %collective-permute-start.9) | collective-permute-done | bytes 73760 | tf_op jit(solution)/shard_map/ppermute | solution.py:590
  91.2 0.0 collective-permute-done.8
  91.2 1.8 %shard_map.99 = f32[12,6144]{1,0:T(8,128)} custom-call(s32[4]{0:T(128)S(1)} %pad_add_fusion.dest_ref, f32[2,3,24,128]{3,2,1,0:T(8,128)S(1)} %bitcast.12, f32[2,3,24,128]{3,2,1,0:T(8,128)S(1)} %bitcast.15, f32[2,3,24,128]{3,2,1,0:T(8,128)S(1)} %bitcast.14, f32[2,3,24,128]{3,2,1,0:T(8,128)S(1)} %bitcast.13), custom_call_target="tpu_custom_call" | custom-call | tf_op jit(solution)/shard_map/pallas_call | solution.py:570
  (6 shorter events, 0.0 us)
Async XLA Ops:
  0.6 1.3 %copy-start = (bf16[2,3,48,16,128]{4,3,2,1,0:T(8,128)(2,1)S(1)}, bf16[2,3,48,16,128]{4,3,2,1,0:T(8,128)(2,1)}, u32[]{:S(2)}) copy-start(bf16[2,3,48,16,128]{4,3,2,1,0:T(8,128)(2,1)} %seed_ref.3) | copy-start | bytes 3538948
  1.9 1.1 %copy-start.2 = (f32[2,48,16,128]{3,2,1,0:T(8,128)S(1)}, f32[2,48,16,128]{3,2,1,0:T(8,128)}, u32[]{:S(2)}) copy-start(f32[2,48,16,128]{3,2,1,0:T(8,128)} %stiff_ref.3) | copy-start | bytes 2359300
  3.0 0.7 copy-start.5
  3.7 0.7 copy-start.7
  4.4 0.7 copy-start.9
  5.0 8.9 %copy-start.1 = (bf16[2,3,48,16,128]{4,3,2,1,0:T(8,128)(2,1)S(1)}, bf16[2,3,48,16,128]{4,3,2,1,0:T(8,128)(2,1)}, u32[]{:S(2)}) copy-start(bf16[2,3,48,16,128]{4,3,2,1,0:T(8,128)(2,1)} %seed_ref.3) | copy-start | bytes 3538948
  5.1 8.9 %copy-start.3 = (f32[2,48,16,128]{3,2,1,0:T(8,128)S(1)}, f32[2,48,16,128]{3,2,1,0:T(8,128)}, u32[]{:S(2)}) copy-start(f32[2,48,16,128]{3,2,1,0:T(8,128)} %stiff_ref.3) | copy-start | bytes 2359300
  5.1 8.9 %copy-start.6 = (s32[2]{0:T(128)S(1)}, s32[2]{0:T(128)}, u32[]{:S(2)}) copy-start(s32[2]{0:T(128)} %len_ref.7) | copy-start | bytes 28
  6.6 27.2 %all-to-all-start = ((f32[8,72,128]{2,1,0:T(8,128)}), f32[8,72,128]{2,1,0:T(8,128)S(1)}, u32[]{:S(2)}, u32[]{:S(2)}) async-start(f32[8,72,128]{2,1,0:T(8,128)} %pack.1), calls=%async_computation | async-start | bytes 589824 | tf_op jit(solution)/shard_map/all_to_all | solution.py:497
  13.9 26.8 %copy-start.13 = (f32[2,16]{1,0:T(2,128)S(1)}, f32[2,16]{1,0:T(2,128)}, u32[]{:S(2)}) copy-start(f32[2,16]{1,0:T(2,128)} %param.14) | copy-start | bytes 388
  13.9 27.0 %copy-start.11 = (f32[2,48]{1,0:T(2,128)S(1)}, f32[2,48]{1,0:T(2,128)}, u32[]{:S(2)}) copy-start(f32[2,48]{1,0:T(2,128)} %cx_ref.1) | copy-start | bytes 1156
  14.0 27.1 %copy-start.12 = (f32[2,128]{1,0:T(2,128)S(1)}, f32[2,128]{1,0:T(2,128)}, u32[]{:S(2)}) copy-start(f32[2,128]{1,0:T(2,128)} %cz_ref.3) | copy-start | bytes 3076
  34.7 14.5 %all-to-all-start.1 = ((f32[8,64,128]{2,1,0:T(8,128)}), f32[8,64,128]{2,1,0:T(8,128)S(1)}, u32[]{:S(2)}, u32[]{:S(2)}) async-start(f32[8,64,128]{2,1,0:T(8,128)} %route.1), calls=%async_computation.1 | async-start | bytes 524288 | tf_op jit(solution)/shard_map/all_to_all | solution.py:525
  41.1 1.7 %copy-start.4 = (f32[2,3,48,16,128]{4,3,2,1,0:T(8,128)S(1)}, f32[2,3,48,16,128]{4,3,2,1,0:T(8,128)}, u32[]{:S(2)}) copy-start(f32[2,3,48,16,128]{4,3,2,1,0:T(8,128)} %get-tuple-element.24.adj_ref.adj_in) | copy-start | bytes 7077892
  42.7 6.5 %copy-start.8 = (s32[2,3]{1,0:T(2,128)S(1)}, s32[2,3]{1,0:T(2,128)}, u32[]{:S(2)}) copy-start(s32[2,3]{1,0:T(2,128)} %low_ref.3) | copy-start | bytes 76
  42.7 6.5 %copy-start.10 = (s32[2,3]{1,0:T(2,128)S(1)}, s32[2,3]{1,0:T(2,128)}, u32[]{:S(2)}) copy-start(s32[2,3]{1,0:T(2,128)} %up_ref.3) | copy-start | bytes 76
  57.1 2.9 %collective-permute-start = (f32[8,2,2,3,24,128]{5,4,3,2,1,0:T(8,128)S(1)}, f32[8,2,2,3,24,128]{5,4,3,2,1,0:T(8,128)S(1)}, u32[]{:S(2)}, u32[]{:S(2)}) collective-permute-start(f32[8,2,2,3,24,128]{5,4,3,2,1,0:T(8,128)S(1)} %get-tuple-element.27), channel_id=1, source_target_pairs={{0,8},{1,9},{2,10},{3,11},{4,12},{5,13},{6,14},{7,15},{8,0},{9,1},... | collective-permute-start | bytes 3538952 | tf_op jit(solution)/shard_map/ppermute | solution.py:590
  60.8 9.1 %collective-permute-start.1 = (f32[4,2,72,128]{3,2,1,0:T(8,128)S(1)}, f32[4,2,72,128]{3,2,1,0:T(8,128)S(1)}, u32[]{:S(2)}, u32[]{:S(2)}) collective-permute-start(f32[4,2,72,128]{3,2,1,0:T(8,128)S(1)} %get-tuple-element.29), channel_id=1, source_target_pairs={{0,1},{1,0},{2,3},{3,2},{4,5},{5,4},{6,7},{7,6},{8,9},{9,8},{10,11... | collective-permute-start | bytes 884744 | tf_op jit(solution)/shard_map/ppermute | solution.py:590
  62.2 8.8 %collective-permute-start.2 = (f32[4,2,72,128]{3,2,1,0:T(8,128)S(1)}, f32[4,2,72,128]{3,2,1,0:T(8,128)S(1)}, u32[]{:S(2)}, u32[]{:S(2)}) collective-permute-start(f32[4,2,72,128]{3,2,1,0:T(8,128)S(1)} %get-tuple-element.31), channel_id=1, source_target_pairs={{0,16},{1,17},{2,18},{3,19},{4,20},{5,21},{6,22},{7,23},{8,24},{9,... | collective-permute-start | bytes 884744 | tf_op jit(solution)/shard_map/ppermute | solution.py:590
  71.6 5.2 %collective-permute-start.3 = (f32[4,72,128]{2,1,0:T(8,128)S(1)}, f32[4,72,128]{2,1,0:T(8,128)S(1)}, u32[]{:S(2)}, u32[]{:S(2)}) collective-permute-start(f32[4,72,128]{2,1,0:T(8,128)S(1)} %get-tuple-element.33), channel_id=1, source_target_pairs={{0,16},{1,17},{2,18},{3,19},{4,20},{5,21},{6,22},{7,23},{8,24},{9,... | collective-permute-start | bytes 442376 | tf_op jit(solution)/shard_map/ppermute | solution.py:590
  73.1 5.1 %collective-permute-start.4 = (f32[4,72,128]{2,1,0:T(8,128)S(1)}, f32[4,72,128]{2,1,0:T(8,128)S(1)}, u32[]{:S(2)}, u32[]{:S(2)}) collective-permute-start(f32[4,72,128]{2,1,0:T(8,128)S(1)} %get-tuple-element.35), channel_id=1, source_target_pairs={{0,1},{1,0},{2,3},{3,2},{4,5},{5,4},{6,7},{7,6},{8,9},{9,8},{10,11... | collective-permute-start | bytes 442376 | tf_op jit(solution)/shard_map/ppermute | solution.py:590
  78.8 6.3 %collective-permute-start.5 = (f32[2,72,128]{2,1,0:T(8,128)S(1)}, f32[2,72,128]{2,1,0:T(8,128)S(1)}, u32[]{:S(2)}, u32[]{:S(2)}) collective-permute-start(f32[2,72,128]{2,1,0:T(8,128)S(1)} %get-tuple-element.37), channel_id=1, source_target_pairs={{0,2},{1,3},{2,4},{3,5},{4,6},{5,7},{6,0},{7,1},{8,10},{9,11},{10,... | collective-permute-start | bytes 221192 | tf_op jit(solution)/shard_map/ppermute | solution.py:590
  78.9 6.2 %collective-permute-start.6 = (f32[2,72,128]{2,1,0:T(8,128)S(1)}, f32[2,72,128]{2,1,0:T(8,128)S(1)}, u32[]{:S(2)}, u32[]{:S(2)}) collective-permute-start(f32[2,72,128]{2,1,0:T(8,128)S(1)} %get-tuple-element.38), channel_id=1, source_target_pairs={{0,4},{1,5},{2,6},{3,7},{4,0},{5,1},{6,2},{7,3},{8,12},{9,13},{10,... | collective-permute-start | bytes 221192 | tf_op jit(solution)/shard_map/ppermute | solution.py:590
  80.8 5.0 %collective-permute-start.7 = (f32[2,72,128]{2,1,0:T(8,128)S(1)}, f32[2,72,128]{2,1,0:T(8,128)S(1)}, u32[]{:S(2)}, u32[]{:S(2)}) collective-permute-start(f32[2,72,128]{2,1,0:T(8,128)S(1)} %get-tuple-element.39), channel_id=1, source_target_pairs={{0,6},{1,7},{2,0},{3,1},{4,2},{5,3},{6,4},{7,5},{8,14},{9,15},{10,... | collective-permute-start | bytes 221192 | tf_op jit(solution)/shard_map/ppermute | solution.py:590
  85.9 4.0 %collective-permute-start.10 = (f32[2,72,128]{2,1,0:T(8,128)S(1)}, f32[2,72,128]{2,1,0:T(8,128)S(1)}, u32[]{:S(2)}, u32[]{:S(2)}) collective-permute-start(f32[2,72,128]{2,1,0:T(8,128)S(1)} %shard_map.98), channel_id=1, source_target_pairs={{0,24},{1,25},{2,26},{3,27},{4,28},{5,29},{6,30},{7,31},{8,16},{9,... | collective-permute-start | bytes 221192 | tf_op jit(solution)/shard_map/ppermute | solution.py:590
  86.0 5.2 %collective-permute-start.9 = (f32[2,72,128]{2,1,0:T(8,128)S(1)}, f32[2,72,128]{2,1,0:T(8,128)S(1)}, u32[]{:S(2)}, u32[]{:S(2)}) collective-permute-start(f32[2,72,128]{2,1,0:T(8,128)S(1)} %shard_map.98), channel_id=1, source_target_pairs={{0,16},{1,17},{2,18},{3,19},{4,20},{5,21},{6,22},{7,23},{8,24},{9,... | collective-permute-start | bytes 221192 | tf_op jit(solution)/shard_map/ppermute | solution.py:590
  86.5 4.6 %collective-permute-start.8 = (f32[2,72,128]{2,1,0:T(8,128)S(1)}, f32[2,72,128]{2,1,0:T(8,128)S(1)}, u32[]{:S(2)}, u32[]{:S(2)}) collective-permute-start(f32[2,72,128]{2,1,0:T(8,128)S(1)} %shard_map.98), channel_id=1, source_target_pairs={{0,8},{1,9},{2,10},{3,11},{4,12},{5,13},{6,14},{7,15},{8,0},{9,1},... | collective-permute-start | bytes 221192 | tf_op jit(solution)/shard_map/ppermute | solution.py:590

commit v3 on v2

--- a/solution.py
+++ b/solution.py
@@ -22,6 +22,7 @@
 SMEM = pl.BlockSpec(memory_space=pltpu.SMEM)
 VMEM = pl.BlockSpec(memory_space=pltpu.VMEM)
 ANY = pl.BlockSpec(memory_space=pl.ANY)
+HBM = pl.BlockSpec(memory_space=pltpu.HBM)
 
 
 def params(mib):
@@ -72,34 +73,57 @@
     return lax.dot_general(a, b, numbers, preferred_element_type=F32)
 
 
-def pack_kernel(devs, len_ref, low_ref, up_ref, seed_ref, stiff_ref, out_ref, packet):
-    slots, _, cy, cz = stiff_ref.shape
-    rows = PLANES * cy
+def pack_kernel(devs, slots, nx, ny, nz, len_in, low_in, up_in, seed_in, stiff_in, out_ref, *scratch):
+    len_ref, low_ref, up_ref, seed_ref, stiff_ref, packet, sems = scratch
+    rows = PLANES * ny
     chunk = rows // devs
+    small = []
+    for k, (src, dst) in enumerate(((len_in, len_ref), (low_in, low_ref), (up_in, up_ref))):
+        small.append(pltpu.make_async_copy(src, dst, sems.at[0, k]))
+        small[k].start()
+    copies = {}
+
+    def fetch(s, side):
+        f = 2 * s + side
+        start = [0, 0] if side == 0 else [len_ref[s] - 3, len_ref[s] - 2]
+        copies[f] = (
+            pltpu.make_async_copy(stiff_in.at[s, pl.ds(start[0], 3)], stiff_ref.at[f], sems.at[1, f]),
+            pltpu.make_async_copy(seed_in.at[s, :, pl.ds(start[1], 2)], seed_ref.at[f], sems.at[2, f]),
+        )
+        for copy in copies[f]:
+            copy.start()
+
     for s in range(slots):
-        length = len_ref[s]
-        for side in range(2):
-            at = [k if side == 0 else length - 1 - k for k in range(3)]
-            stiff = [stiff_ref[s, i] for i in at]
-            parts = [plane_parts(v) for v in stiff]
-            inner = parts[0][1] + parts[1][0]
-            next_near = parts[1][1] + parts[0][0] + parts[2][0]
-            scale = 1.0 / (DOMINANCE * next_near)
-            planes = [stiff[0], inner]
-            planes += [seed_ref[s, c, at[0]].astype(F32) for c in range(3)]
-            for c in range(3):
-                planes.append(plane_parts(seed_ref[s, c, at[1]].astype(F32) * scale)[0])
-            for k, plane in enumerate(planes):
-                packet[2 * s + side, k * cy : (k + 1) * cy] = plane
+        fetch(s, 0)
+    small[0].wait()
+    for s in range(slots):
+        fetch(s, 1)
+    small[1].wait()
+    small[2].wait()
     wanted = []
     for s in range(slots):
         for side, ref in ((0, low_ref), (1, up_ref)):
             number = jnp.maximum(ref[s, 0], 0) * (2 * slots) + ref[s, 1] * 2 + (1 - side)
             wanted.append(number.astype(F32))
-    row = lax.broadcasted_iota(jnp.int32, (8, cz), 0)
-    note = jnp.zeros((8, cz), F32)
+    row = lax.broadcasted_iota(jnp.int32, (8, nz), 0)
+    note = jnp.zeros((8, nz), F32)
     for f, number in enumerate(wanted):
         note = jnp.where(row == f, number, note)
+    for f in (0, 2, 1, 3):
+        side = f % 2
+        for copy in copies[f]:
+            copy.wait()
+        stiff = [stiff_ref[f, k if side == 0 else 2 - k] for k in range(3)]
+        parts = [plane_parts(v) for v in stiff]
+        inner = parts[0][1] + parts[1][0]
+        next_near = parts[1][1] + parts[0][0] + parts[2][0]
+        scale = 1.0 / (DOMINANCE * next_near)
+        planes = [stiff[0], inner]
+        planes += [seed_ref[f, c, side].astype(F32) for c in range(3)]
+        for c in range(3):
+            planes.append(plane_parts(seed_ref[f, c, 1 - side].astype(F32) * scale)[0])
+        for k, plane in enumerate(planes):
+            packet[f, k * ny : (k + 1) * ny] = plane
     for j in range(devs):
         for f in range(2 * slots):
             out_ref[j, f * chunk : (f + 1) * chunk] = packet[f, j * chunk : (j + 1) * chunk]
@@ -121,92 +145,6 @@
             out_ref[e, f * chunk : (f + 1) * chunk] = in_ref[source, pl.ds(start, chunk)]
 
 
-def inner_kernel(len_ref, seed_ref, stiff_ref, out_ref, edge_ref, s_ext, w_ext, v_ext, fac_ref, mul_ref):
-    slots, nx, ny, nz = stiff_ref.shape
-    last = 8 + ny
-    zeros = jnp.zeros((nx + 2, 8, nz), F32)
-    for ref, lead in ((s_ext, ()), *((r, (c,)) for r in (w_ext, v_ext) for c in range(3))):
-        ref[(*lead, slice(None), slice(0, 8))] = zeros
-        ref[(*lead, slice(None), slice(last, last + 8))] = zeros
-        for i in (0, nx + 1):
-            ref[(*lead, i, slice(8, last))] = jnp.zeros((ny, nz), F32)
-
-    def loop(body):
-        def step(k, _):
-            body(k * STEP)
-            return 0
-
-        lax.fori_loop(0, nx // STEP, step, 0)
-
-    for b in range(slots):
-        length = len_ref[b]
-
-        def active_at(i, length=length):
-            return i + lax.broadcasted_iota(jnp.int32, (STEP, ny, nz), 0) < length
-
-        def fill(i, b=b, active_at=active_at):
-            s_ext[pl.ds(i + 1, STEP), 8:last] = jnp.where(
-                active_at(i), stiff_ref[b, pl.ds(i, STEP)], 0.0
-            )
-
-        loop(fill)
-
-        def first(i, b=b, active_at=active_at):
-            stiff, near = padded_stencil(s_ext, (), i, STEP)
-            active = active_at(i)
-            safe = jnp.where(active, DOMINANCE * stiff * near, 1.0)
-            inv = jnp.where(active, 1.0 / safe, 0.0)
-            fac = stiff * inv
-            fac_ref[pl.ds(i, STEP)] = fac
-            mul_ref[pl.ds(i, STEP)] = stiff * fac
-            for c in range(3):
-                seed = seed_ref[b, c, pl.ds(i, STEP)].astype(F32)
-                w_ext[c, pl.ds(i + 1, STEP), 8:last] = seed * fac
-                out_ref[b, c, pl.ds(i, STEP)] = seed * inv
-
-        loop(first)
-
-        for c in range(3):
-            for side in range(2):
-                f = 2 * b + side
-                for k, at in ((11 + c, 1), (14 + c, 2)):
-                    row = at if side == 0 else length - 1 - at
-                    edge_ref[f, k] = out_ref[b, c, row]
-
-        for c in range(3):
-
-            def second(i, c=c):
-                here, near = padded_stencil(w_ext, (c,), i, STEP)
-                v_ext[c, pl.ds(i + 1, STEP), 8:last] = here + mul_ref[pl.ds(i, STEP)] * near
-
-            loop(second)
-
-            def third(i, b=b, c=c):
-                _, near = padded_stencil(v_ext, (c,), i, STEP)
-                out_ref[b, c, pl.ds(i, STEP)] += fac_ref[pl.ds(i, STEP)] * near
-
-            loop(third)
-
-        for side in range(2):
-            f = 2 * b + side
-            at = [k if side == 0 else length - 1 - k for k in range(4)]
-            stiff = [stiff_ref[b, at[k]] for k in range(2)]
-            edge_ref[f, 0] = stiff[0]
-            edge_ref[f, 1] = plane_parts(stiff[0])[1] + plane_parts(stiff[1])[0]
-            mul_1, fac_1, fac_2 = mul_ref[at[1]], fac_ref[at[1]], fac_ref[at[2]]
-            edge_ref[f, 17], edge_ref[f, 18], edge_ref[f, 19] = mul_1, fac_1, fac_2
-            for c in range(3):
-                edge_ref[f, 2 + c] = seed_ref[b, c, at[0]].astype(F32)
-                w_1, w_2 = w_ext[c, at[1] + 1, 8:last], w_ext[c, at[2] + 1, 8:last]
-                v_2, v_3 = v_ext[c, at[2] + 1, 8:last], v_ext[c, at[3] + 1, 8:last]
-                beside, own = plane_parts(w_1)
-                edge_ref[f, 5 + c] = beside
-                edge_ref[f, 8 + c] = w_1 + mul_1 * (own + plane_parts(w_2)[0])
-                beside, own = plane_parts(v_2)
-                edge_ref[f, 11 + c] += fac_1 * beside
-                edge_ref[f, 14 + c] += fac_2 * (own + plane_parts(v_3)[0])
-
-
 def hat_along_z(coord, nz):
     row = lax.broadcasted_iota(jnp.int32, (128, 3 * nz), 0)
     lane = lax.broadcasted_iota(jnp.int32, (128, 3 * nz), 1)
@@ -215,28 +153,124 @@
     return thrice(jnp.where((row // LZ) == (lane // nz), hat, 0.0), 1, False)
 
 
-def lattice_kernel(len_ref, adj_ref, cx_ref, cz_ref, out_ref, zdone):
-    slots, _, nx, ny, nz = adj_ref.shape
+def block_kernel(b, len_ref, seed_in, stiff_in, cx_ref, cz_ref, *refs):
+    adj_out, edge_ref, part_ref, s_ext, w_ext, v_ext, fac_ref, mul_ref, adj, seeds, zdone, sems = refs[-12:]
+    nx, ny, nz = fac_ref.shape
+    last = 8 + ny
+    length = len_ref[b]
+    loads = (
+        pltpu.make_async_copy(
+            stiff_in.at[b], s_ext.at[pl.ds(1, nx), pl.ds(8, ny)], sems.at[0]
+        ),
+        pltpu.make_async_copy(seed_in.at[b], seeds, sems.at[1]),
+    )
+    for copy in loads:
+        copy.start()
+    zeros = jnp.zeros((nx + 2, 8, nz), F32)
+    plane = jnp.zeros((ny, nz), F32)
+    for ref, lead in ((s_ext, ()), *((r, (c,)) for r in (w_ext, v_ext) for c in range(3))):
+        ref[(*lead, slice(None), slice(0, 8))] = zeros
+        ref[(*lead, slice(None), slice(last, last + 8))] = zeros
+        for i in (0, nx + 1):
+            ref[(*lead, i, slice(8, last))] = plane
+    hat_z = hat_along_z(cz_ref[b : b + 1, :], nz)
+    line = lax.broadcasted_iota(jnp.int32, (LX, 3 * nx), 0).astype(F32)
+    lane = lax.broadcasted_iota(jnp.int32, (LX, 3 * nx), 1)
+    x = lane % nx
+    coord = jnp.concatenate([cx_ref[b : b + 1, :]] * 3, axis=1)
+    hat = jnp.maximum(0.0, 1.0 - jnp.abs(line - coord))
+    hat = jnp.where(jnp.logical_and(x >= ENDS, x < length - ENDS), hat, 0.0)
+    high, low = split(hat)
+    hat_x = jnp.where(lane < 2 * nx, high.astype(F32), low.astype(F32)).astype(BF16)
+    for copy in loads:
+        copy.wait()
+
+    def clear(i, _):
+        s_ext[i + 1, 8:last] = plane
+        return 0
+
+    lax.fori_loop(length, nx, clear, 0)
+
+    def loop(body):
+        def step(k, _):
+            body(k * STEP)
+            return 0
+
+        lax.fori_loop(0, nx // STEP, step, 0)
+
+    def first(i):
+        stiff, near = padded_stencil(s_ext, (), i, STEP)
+        active = i + lax.broadcasted_iota(jnp.int32, (STEP, ny, nz), 0) < length
+        safe = jnp.where(active, DOMINANCE * stiff * near, 1.0)
+        inv = jnp.where(active, 1.0 / safe, 0.0)
+        fac = stiff * inv
+        fac_ref[pl.ds(i, STEP)] = fac
+        mul_ref[pl.ds(i, STEP)] = stiff * fac
+        for c in range(3):
+            seed = seeds[c, pl.ds(i, STEP)].astype(F32)
+            w_ext[c, pl.ds(i + 1, STEP), 8:last] = seed * fac
+            adj[c, pl.ds(i, STEP)] = seed * inv
+
+    loop(first)
+
+    at = [[k if side == 0 else length - 1 - k for k in range(4)] for side in range(2)]
+    for f in range(2):
+        for c in range(3):
+            edge_ref[f, 11 + c] = adj[c, at[f][1]]
+            edge_ref[f, 14 + c] = adj[c, at[f][2]]
+
+    def second(i):
+        mul = mul_ref[pl.ds(i, STEP)]
+        for c in range(3):
+            here, near = padded_stencil(w_ext, (c,), i, STEP)
+            v_ext[c, pl.ds(i + 1, STEP), 8:last] = here + mul * near
+
+    loop(second)
+
+    def third(i):
+        fac = fac_ref[pl.ds(i, STEP)]
+        for c in range(3):
+            _, near = padded_stencil(v_ext, (c,), i, STEP)
+            adj[c, pl.ds(i, STEP)] += fac * near
+
+    loop(third)
+    store = pltpu.make_async_copy(adj, adj_out.at[b], sems.at[2])
+    store.start()
+
+    def parts(ref, *lead):
+        v = ref[(*lead, slice(8, last))]
+        t = ref[(*lead, slice(7, last - 1))] + ref[(*lead, slice(9, last + 1))]
+        own = t + neighbours(v + 0.5 * t, 1)
+        return v + 0.5 * t + neighbours(0.5 * v + (1.0 / 3.0) * t, 1), own
+
+    for f in range(2):
+        edge_ref[f, 0] = s_ext[at[f][0] + 1, 8:last]
+        edge_ref[f, 1] = parts(s_ext, at[f][0] + 1)[1] + parts(s_ext, at[f][1] + 1)[0]
+        mul_1, fac_1, fac_2 = mul_ref[at[f][1]], fac_ref[at[f][1]], fac_ref[at[f][2]]
+        edge_ref[f, 17], edge_ref[f, 18], edge_ref[f, 19] = mul_1, fac_1, fac_2
+        for c in range(3):
+            edge_ref[f, 2 + c] = seeds[c, at[f][0]].astype(F32)
+            beside, own = parts(w_ext, c, at[f][1] + 1)
+            edge_ref[f, 5 + c] = beside
+            own = own + parts(w_ext, c, at[f][2] + 1)[0]
+            edge_ref[f, 8 + c] = w_ext[c, at[f][1] + 1, 8:last] + mul_1 * own
+            beside, own = parts(v_ext, c, at[f][2] + 1)
+            edge_ref[f, 11 + c] += fac_1 * beside
+            edge_ref[f, 14 + c] += fac_2 * (own + parts(v_ext, c, at[f][3] + 1)[0])
+
     group = 16
-    for b in range(slots):
-        hat_z = hat_along_z(cz_ref[b : b + 1, :], nz)
-        for x in range(0, nx, group):
-            rows = [adj_ref[b, c, x : x + group].reshape(group * ny, nz) for c in range(3)]
-            done = dot(thrice(jnp.concatenate(rows, axis=1), 1, True), hat_z, 1)
-            zdone[pl.ds((b * nx + x) * ny, group * ny)] = done
-        line = lax.broadcasted_iota(jnp.int32, (LX, 3 * nx), 0).astype(F32)
-        lane = lax.broadcasted_iota(jnp.int32, (LX, 3 * nx), 1)
-        x = lane % nx
-        hat = jnp.maximum(0.0, 1.0 - jnp.abs(line - cx_ref[b : b + 1, :]))
-        hat = jnp.where(jnp.logical_and(x >= ENDS, x < len_ref[b] - ENDS), hat, 0.0)
-        high, low = split(hat)
-        hat_x = jnp.where(lane < 2 * nx, high.astype(F32), low.astype(F32)).astype(BF16)
-        for y in range(0, ny, 2):
-            part = [zdone[pl.ds(b * nx * ny + y + k, nx, stride=ny), :] for k in range(2)]
-            done = dot(hat_x, thrice(jnp.concatenate(part, axis=1), 0, True))
-            for k in range(2):
-                at = pl.ds(b * ny + y + k, LX, stride=slots * ny)
-                out_ref[at, :] = done[:, 128 * k : 128 * (k + 1)]
+    pitch = ny + 1
+    for x in range(0, nx, group):
+        rows = [adj[c, x : x + group].reshape(group * ny, nz) for c in range(3)]
+        done = dot(thrice(jnp.concatenate(rows, axis=1), 1, True), hat_z, 1)
+        for k in range(group):
+            zdone[(x + k) * pitch : (x + k) * pitch + ny] = done[k * ny : (k + 1) * ny]
+    for y in range(0, ny, 2):
+        part = [zdone[pl.ds(y + k, nx, stride=pitch), :] for k in range(2)]
+        done = dot(hat_x, thrice(jnp.concatenate(part, axis=1), 0, True))
+        for k in range(2):
+            part_ref[pl.ds(y + k, LX, stride=pitch), :] = done[:, 128 * k : 128 * (k + 1)]
+    store.wait()
 
 
 def outer_kernel(
@@ -247,8 +281,10 @@
     up_ref,
     cx_ref,
     halo_ref,
-    edge_ref,
-    part_ref,
+    edge_0,
+    edge_1,
+    part_0,
+    part_1,
     cy_ref,
     cz_ref,
     adj_in,
@@ -262,8 +298,10 @@
     sems,
 ):
     del adj_in
-    faces, _, ny, nz = edge_ref.shape
-    slots = faces // 2
+    slots = 2
+    faces = 2 * slots
+    _, _, ny, nz = edge_0.shape
+    pitch = ny + 1
     chunk = halo_ref.shape[1] // faces
     zero_plane = jnp.zeros((ny, nz), F32)
 
@@ -297,28 +335,29 @@
     copies = []
     for f in range(faces):
         b, side = f // 2, f % 2
-        stiff, inside = edge_ref[f, 0], edge_ref[f, 1]
+        edge = (edge_0, edge_1)[b].at[side]
+        stiff, inside = edge[0], edge[1]
         beside = plane_parts(stiff)[0]
         there = 1.0 / (DOMINANCE * (pack[f, 1] + beside))
         inv = 1.0 / (DOMINANCE * stiff * (inside + plane_parts(pack[f, 0])[0]))
         fac = stiff * inv
-        mul_1, fac_1, fac_2 = edge_ref[f, 17], edge_ref[f, 18], edge_ref[f, 19]
-        for c in range(3):
-            seed = edge_ref[f, 2 + c]
+        mul_1, fac_1, fac_2 = edge[17], edge[18], edge[19]
+        for c in range(3):
+            seed = edge[2 + c]
             w_n = pack[f, 2 + c] * there
             w_0 = seed * fac
             beside_n, own_n = plane_parts(w_n)
             beside_0, own_0 = plane_parts(w_0)
             v_n = w_n + pack[f, 0] * there * (own_n + pack[f, 5 + c] + beside_0)
-            v_0 = w_0 + stiff * fac * (own_0 + edge_ref[f, 5 + c] + beside_n)
-            v_1 = edge_ref[f, 8 + c] + mul_1 * beside_0
+            v_0 = w_0 + stiff * fac * (own_0 + edge[5 + c] + beside_n)
+            v_1 = edge[8 + c] + mul_1 * beside_0
             beside_n = plane_parts(v_n)[0]
             beside_0, own_0 = plane_parts(v_0)
             beside_1, own_1 = plane_parts(v_1)
             rows = [
                 seed * inv + fac * (own_0 + beside_1 + beside_n),
-                edge_ref[f, 11 + c] + fac_1 * (own_1 + beside_0),
-                edge_ref[f, 14 + c] + fac_2 * beside_1,
+                edge[11 + c] + fac_1 * (own_1 + beside_0),
+                edge[14 + c] + fac_2 * beside_1,
             ]
             for k, row in enumerate(rows):
                 ends[b, c, k if side == 0 else 2 * ENDS - 1 - k] = row
@@ -338,8 +377,9 @@
         hat_z = hat_along_z(cz_ref[b : b + 1, :], nz)
         rows = [ends[b, c].reshape(2 * ENDS * ny, nz) for c in range(3)]
         done = dot(thrice(jnp.concatenate(rows, axis=1), 1, True), hat_z, 1)
-        zdone[0 : 2 * ENDS * ny] = done
-        zdone[2 * ENDS * ny : eight * ny] = jnp.zeros(((eight - 2 * ENDS) * ny, 128), F32)
+        for k in range(eight):
+            rows = done[k * ny : (k + 1) * ny] if k < 2 * ENDS else jnp.zeros((ny, 128), F32)
+            zdone[k * pitch : k * pitch + ny] = rows
         coord = jnp.full((LX, 4 * eight), -4.0, F32)
         for k in range(2 * ENDS):
             at = k if k < ENDS else len_ref[b] - 2 * ENDS + k
@@ -348,14 +388,13 @@
         high, low = split(hat)
         hat_x = jnp.where(lane < 2 * eight, high.astype(F32), low.astype(F32)).astype(BF16)
         for y in range(0, ny, 2):
-            part = [zdone[pl.ds(y + k, eight, stride=ny), :] for k in range(2)]
+            part = [zdone[pl.ds(y + k, eight, stride=pitch), :] for k in range(2)]
             high, low = split(jnp.concatenate(part, axis=1))
             high, low = high.astype(F32), low.astype(F32)
             stack = jnp.concatenate([high, low, high, jnp.zeros_like(high)], axis=0)
             done = dot(hat_x, stack.astype(BF16))
             for k in range(2):
-                at = pl.ds(b * ny + y + k, LX, stride=slots * ny)
-                xdone[at, :] = done[:, 128 * k : 128 * (k + 1)]
+                xdone[b, pl.ds(y + k, LX, stride=pitch), :] = done[:, 128 * k : 128 * (k + 1)]
 
     depth = per * slots * ny
     row = lax.broadcasted_iota(jnp.int32, (LY * per, depth), 0).astype(F32)
@@ -363,20 +402,22 @@
     which = jnp.floor((row + 0.5) * (1.0 / per))
     inside = row - which * per
     owner = jnp.floor((lane + 0.5) * (1.0 / (slots * ny)))
-    hat_y = jnp.maximum(0.0, 1.0 - jnp.abs(which - cy_ref[...]))
+    coord = jnp.concatenate([cy_ref[b : b + 1, :] for b in range(slots)] * per, axis=1)
+    hat_y = jnp.maximum(0.0, 1.0 - jnp.abs(which - coord))
     hat_y = thrice(jnp.where(inside == owner, hat_y, 0.0), 1, False)
     third_rows = LY // 4 * per
     pieces = keep_ref.shape[3]
     size = 3 * third_rows // 8
     tail = lax.broadcasted_iota(jnp.int32, (third_rows, 128), 1) >= 3 * LZ
-
-    def close(pair, _):
+    even = dest_ref[0] == 0
+    for pair in range(LX // per // 2):
         terms = []
-        for k in range(2):
-            start = (2 * pair + k) * depth
-            if depth % 8 == 0:
-                start = pl.multiple_of(start, 8)
-            terms.append(part_ref[pl.ds(start, depth), :] + xdone[pl.ds(start, depth), :])
+        for number in (2 * pair, 2 * pair + 1):
+            rows = []
+            for line in range(number * per, (number + 1) * per):
+                at = slice(line * pitch, line * pitch + ny)
+                rows += [part_0[at] + xdone[0, at], part_1[at] + xdone[1, at]]
+            terms.append(jnp.concatenate(rows, axis=0))
         both = dot(hat_y, thrice(jnp.concatenate(terms, axis=1), 0, True))
         for k in range(2):
             done = both[:, 128 * k : 128 * (k + 1)]
@@ -388,17 +429,11 @@
             dense = jnp.concatenate(dense, axis=0)
             number = 2 * pair + k
             d, t = number // pieces, number % pieces
-            for core in range(2):
-
-                @pl.when(dest_ref[0] == core)
-                def _(core=core, dense=dense, d=d, t=t):
-                    for g in range(8):
-                        ref = keep_ref if g // 4 == core else send_ref
-                        ref[d, g // 2 % 2, g % 2, t] = dense[g * size : (g + 1) * size]
-
-        return 0
-
-    lax.fori_loop(0, LX // per // 2, close, 0)
+            for g in range(4):
+                first = dense[g * size : (g + 1) * size]
+                second = dense[(g + 4) * size : (g + 5) * size]
+                keep_ref[d, g // 2, g % 2, t] = jnp.where(even, first, second)
+                send_ref[d, g // 2, g % 2, t] = jnp.where(even, second, first)
     for copy in copies:
         copy.wait()
 
@@ -486,33 +521,57 @@
     shape = lambda *dims: jax.ShapeDtypeStruct(dims, F32)
 
     packed = pl.pallas_call(
-        functools.partial(pack_kernel, devs),
+        functools.partial(pack_kernel, devs, slots, nx, ny, nz),
         out_shape=shape(devs, rows + 8, nz),
-        in_specs=[SMEM, SMEM, SMEM, VMEM, VMEM],
+        in_specs=[HBM] * 5,
         out_specs=VMEM,
-        scratch_shapes=[pltpu.VMEM((faces, PLANES * ny, nz), F32)],
-        compiler_params=params(8),
+        scratch_shapes=[
+            pltpu.SMEM((slots,), jnp.int32),
+            pltpu.SMEM((slots, 3), jnp.int32),
+            pltpu.SMEM((slots, 3), jnp.int32),
+            pltpu.VMEM((faces, 3, 2, ny, nz), seed.dtype),
+            pltpu.VMEM((faces, 3, ny, nz), F32),
+            pltpu.VMEM((faces, PLANES * ny, nz), F32),
+            pltpu.SemaphoreType.DMA((3, faces)),
+        ],
+        compiler_params=params(4),
         name="pack",
     )(lengths, low, up, seed, stiff)
     spread = lax.all_to_all(packed, "dev", 0, 0)
     ext = (nx + 2, ny + 16, nz)
     plain = pltpu.VMEM((nx, ny, nz), F32)
-    early, edges = pl.pallas_call(
-        inner_kernel,
-        out_shape=(shape(slots, 3, nx, ny, nz), shape(faces, EDGES, ny, nz)),
-        in_specs=[SMEM, VMEM, VMEM],
-        out_specs=(VMEM, VMEM),
-        scratch_shapes=[
-            pltpu.VMEM(ext, F32),
-            pltpu.VMEM((3, *ext), F32),
-            pltpu.VMEM((3, *ext), F32),
-            plain,
-            plain,
-        ],
-        compiler_params=params(24),
-        cost_estimate=pl.CostEstimate(flops=4 * 10**8, bytes_accessed=2 * 10**7, transcendentals=0),
-        name="inner",
-    )(lengths, seed, stiff)
+
+    def one_block(b, adjoint):
+        given = () if adjoint is None else (adjoint,)
+        return pl.pallas_call(
+            functools.partial(block_kernel, b),
+            out_shape=(
+                shape(slots, 3, nx, ny, nz),
+                shape(2, EDGES, ny, nz),
+                shape(LX * (ny + 1), 128),
+            ),
+            in_specs=[SMEM, ANY, ANY, VMEM, VMEM] + [HBM] * len(given),
+            out_specs=(HBM, VMEM, VMEM),
+            scratch_shapes=[
+                pltpu.VMEM(ext, F32),
+                pltpu.VMEM((3, *ext), F32),
+                pltpu.VMEM((3, *ext), F32),
+                plain,
+                plain,
+                pltpu.VMEM((3, nx, ny, nz), F32),
+                pltpu.VMEM((3, nx, ny, nz), seed.dtype),
+                pltpu.VMEM((nx * (ny + 1), 128), F32),
+                pltpu.SemaphoreType.DMA((3,)),
+            ],
+            input_output_aliases={5: 0} if given else {},
+            compiler_params=params(16),
+            cost_estimate=pl.CostEstimate(
+                flops=3 * 10**9, bytes_accessed=10**7, transcendentals=0
+            ),
+            name=f"block_{b}",
+        )(lengths, seed, stiff, coord_x, coord_z, *given)
+
+    early, edge_0, part_0 = one_block(0, None)
     routed = pl.pallas_call(
         route_kernel,
         out_shape=shape(devs, rows, nz),
@@ -523,31 +582,22 @@
     )(spread)
     early, routed = lax.optimization_barrier((early, routed))
     halos = lax.all_to_all(routed, "dev", 0, 0)
-    inside = pl.pallas_call(
-        lattice_kernel,
-        out_shape=shape(LX * slots * ny, 128),
-        in_specs=[SMEM, VMEM, VMEM, VMEM],
-        out_specs=VMEM,
-        scratch_shapes=[pltpu.VMEM((slots * nx * ny, 128), F32)],
-        compiler_params=params(16),
-        cost_estimate=pl.CostEstimate(flops=2 * 10**9, bytes_accessed=2 * 10**7, transcendentals=0),
-        name="lattice",
-    )(lengths, early, jnp.tile(coord_x, (1, 3)), coord_z)
+    early, edge_1, part_1 = one_block(1, early)
 
     half = shape(devs, 2, 2, pieces, size, 128)
     adjoint, keep, send = pl.pallas_call(
         functools.partial(outer_kernel, per),
         out_shape=(shape(slots, 3, nx, ny, nz), half, half),
-        in_specs=[SMEM] * 5 + [VMEM] * 5 + [ANY],
-        out_specs=(ANY, VMEM, VMEM),
+        in_specs=[SMEM] * 5 + [VMEM] * 7 + [HBM],
+        out_specs=(HBM, VMEM, VMEM),
         scratch_shapes=[
             pltpu.VMEM((faces, PLANES, ny, nz), F32),
             pltpu.VMEM((slots, 3, 2 * ENDS, ny, nz), F32),
-            pltpu.VMEM((8 * ny, 128), F32),
-            pltpu.VMEM((LX * slots * ny, 128), F32),
+            pltpu.VMEM((8 * (ny + 1), 128), F32),
+            pltpu.VMEM((slots, LX * (ny + 1), 128), F32),
             pltpu.SemaphoreType.DMA((faces, 3)),
         ],
-        input_output_aliases={10: 0},
+        input_output_aliases={12: 0},
         compiler_params=params(16),
         name="outer",
     )(
@@ -557,9 +607,11 @@
         up,
         coord_x,
         halos,
-        edges,
-        inside,
-        jnp.tile(coord_y.reshape(1, slots * ny), (1, per)),
+        edge_0,
+        edge_1,
+        part_0,
+        part_1,
+        coord_y,
         coord_z,
         early,
     )

time: 93.5 us -> 82.3 us (0.88)
  Pallas kernels: 37.3 us -> 26.3 us
  waiting for transfers between devices: 24.1 us -> 23.1 us
    pallas_call x3, Pallas kernels: 24.7 us -> 17.6 us  [the longest x2 15.4 us: one_block(): pl.pallas_call(functools.partial(block_kernel, b), out_shape=(shape(slots...]
    pallas_call x1, Pallas kernels: 7.9 us -> 3.93 us  [on_device(): pl.pallas_call(functools.partial(outer_kernel, per), out_shape=(shape(slo...]
    all_to_all x1, waiting for transfers between devices: 3.09 us -> 0.01 us  [on_device(): halos = lax.all_to_all(routed, 'dev', 0, 0)]
    all_to_all x1, waiting for transfers between devices: 0.01 us -> 1.95 us  [on_device(): spread = lax.all_to_all(packed, 'dev', 0, 0)]
    all_to_all x1, starting transfers between devices: 5.99 us -> 4.17 us  [on_device(): halos = lax.all_to_all(routed, 'dev', 0, 0)]
    ppermute x11, starting transfers between devices: 11 us -> 12.8 us  [move(): return lax.ppermute(value, ('group', 'dev'), links)]
    unnamed x28 -> x32, local copies, waits for them, and re-layouts: 6.12 us -> 7.26 us
  transfers between devices with their start and end apart: 13 -> 13, of which waited for: 10 -> 11; matrix products, arithmetic and copies ran while one was open for 0% -> 0% of each run, Pallas kernels for 25% -> 19%
where the time goes in v3:
time: 82.3 us; the launch traced here: 81.8 us
  Pallas kernels  26.3 us (32%)
  starting transfers between devices  24.3 us (30%)
  waiting for transfers between devices  23.1 us (28%)
  local copies, waits for them, and re-layouts  7.26 us (9%)
    ppermute x11, waiting for transfers between devices, move(): return lax.ppermute(value, ('group', 'dev'), links)  21.1 us
    pallas_call x2, Pallas kernels, one_block(): pl.pallas_call(functools.partial(block_kernel, b), out_shape=(shape(slots...  15.4 us
    ppermute x11, starting transfers between devices, move(): return lax.ppermute(value, ('group', 'dev'), links)  12.8 us
    all_to_all x1, starting transfers between devices, on_device(): spread = lax.all_to_all(packed, 'dev', 0, 0)  7.32 us
    unnamed x32, local copies, waits for them, and re-layouts  7.26 us
    all_to_all x1, starting transfers between devices, on_device(): halos = lax.all_to_all(routed, 'dev', 0, 0)  4.17 us
    pallas_call x1, Pallas kernels, on_device(): pl.pallas_call(functools.partial(outer_kernel, per), out_shape=(shape(slo...  3.93 us
    pallas_call x5, Pallas kernels, small(): pl.pallas_call(kernel, out_shape=outs, in_specs=[SMEM if a is dest else V...  3.73 us
  transfers between devices with their start and end apart: 13, of which 11 were waited for; matrix products, arithmetic and copies ran while one was open for 0% of the time, Pallas kernels for 19%

profile of v3, /device:TPU:0, one launch (start us, length us, event | category | flops | bytes accessed | tf_op | source)
XLA Modules:
  0.0 81.8 jit_solution(2833065406319595078)
XLA Ops:
  0.6 0.0 copy-start
  0.6 1.3 %copy-done = bf16[2,3,48,16,128]{4,3,2,1,0:T(8,128)(2,1)S(1)} copy-done((bf16[2,3,48,16,128]{4,3,2,1,0:T(8,128)(2,1)S(1)}, bf16[2,3,48,16,128]{4,3,2,1,0:T(8,128)(2,1)}, u32[]{:S(2)}) %copy-start) | copy-done | bytes 1179672
  1.9 0.0 copy-start.2
  1.9 1.1 %copy-done.2 = f32[2,48,16,128]{3,2,1,0:T(8,128)S(1)} copy-done((f32[2,48,16,128]{3,2,1,0:T(8,128)S(1)}, f32[2,48,16,128]{3,2,1,0:T(8,128)}, u32[]{:S(2)}) %copy-start.2) | copy-done | bytes 786456
  3.0 0.0 copy-start.7
  3.0 0.7 copy-done.7
  3.7 0.0 copy-start.9
  3.7 0.7 copy-done.9
  4.4 0.0 copy-start.11
  4.4 0.7 copy-done.11
  5.1 0.0 copy-start.1
  5.1 0.0 copy-start.3
  5.1 0.0 copy-start.12
  5.1 0.0 copy-start.13
  5.1 0.0 copy-start.14
  5.1 2.2 %pack.1 = f32[8,72,128]{2,1,0:T(8,128)} custom-call(s32[2]{0:T(128)S(1)} %copy-done.11, s32[2,3]{1,0:T(2,128)S(1)} %copy-done.7, s32[2,3]{1,0:T(2,128)S(1)} %copy-done.9, bf16[2,3,48,16,128]{4,3,2,1,0:T(8,128)(2,1)S(1)} %copy-done, f32[2,48,16,128]{3,2,1,0:T(8,128)S(1)} %copy-done.2), custom_call_target="tpu_custom_call" | custom-call | tf_op jit(solution)/shard_map/pack/pallas_call | solution.py:523
  7.3 7.3 %all-to-all-start = ((f32[8,72,128]{2,1,0:T(8,128)}), f32[8,72,128]{2,1,0:T(8,128)S(1)}, u32[]{:S(2)}, u32[]{:S(2)}) async-start(f32[8,72,128]{2,1,0:T(8,128)} %pack.1), calls=%async_computation | async-start | bytes 589824 | tf_op jit(solution)/shard_map/all_to_all | solution.py:540
  14.6 0.0 copy-done.1
  14.6 0.0 copy-done.3
  14.7 0.0 copy-done.12
  14.7 0.0 copy-done.13
  14.7 0.0 copy-done.14
  14.7 7.6 %block_0.1 = (f32[2,3,48,16,128]{4,3,2,1,0:T(8,128)}, f32[2,20,16,128]{3,2,1,0:T(8,128)S(1)}, f32[1632,128]{1,0:T(8,128)S(1)}) custom-call(s32[2]{0:T(128)S(1)} %copy-done.12, bf16[2,3,48,16,128]{4,3,2,1,0:T(8,128)(2,1)S(1)} %copy-done.1, f32[2,48,16,128]{3,2,1,0:T(8,128)S(1)} %copy-done.3, f32[2,48]{1,0:T(2,128)S(1)} %copy-done.13, f32[2,128]{1,0:T(2,128)S(1)} %copy-done.14), custom_call_target="tpu_custom_call" | custom-call | flops 3000000000 | bytes 10000000 | tf_op jit(solution)/shard_map/block_0/pallas_call | solution.py:546
  22.3 2.0 %all-to-all-done.in_ref = f32[8,72,128]{2,1,0:T(8,128)S(1)} async-done(((f32[8,72,128]{2,1,0:T(8,128)}), f32[8,72,128]{2,1,0:T(8,128)S(1)}, u32[]{:S(2)}, u32[]{:S(2)}) %all-to-all-start) | async-done | bytes 294944 | tf_op jit(solution)/shard_map/all_to_all | solution.py:540
  24.3 1.0 %route.1 = f32[8,64,128]{2,1,0:T(8,128)} custom-call(f32[8,72,128]{2,1,0:T(8,128)S(1)} %all-to-all-done.in_ref), custom_call_target="tpu_custom_call" | custom-call | tf_op jit(solution)/shard_map/route/pallas_call | solution.py:575
  25.2 4.2 %all-to-all-start.1 = ((f32[8,64,128]{2,1,0:T(8,128)}), f32[8,64,128]{2,1,0:T(8,128)S(1)}, u32[]{:S(2)}, u32[]{:S(2)}) async-start(f32[8,64,128]{2,1,0:T(8,128)} %route.1), calls=%async_computation.1 | async-start | bytes 524288 | tf_op jit(solution)/shard_map/all_to_all | solution.py:584
  29.4 0.1 pad_add_fusion.dest_ref
  29.5 1.1 %copy-done.4 = f32[2,48,16,128]{3,2,1,0:T(8,128)S(1)} copy-done((f32[2,48,16,128]{3,2,1,0:T(8,128)S(1)}, f32[2,48,16,128]{3,2,1,0:T(8,128)}, u32[]{:S(2)}) %copy-start.4) | copy-done | bytes 786456
  30.6 7.8 %block_1.1 = (f32[2,3,48,16,128]{4,3,2,1,0:T(8,128)}, f32[2,20,16,128]{3,2,1,0:T(8,128)S(1)}, f32[1632,128]{1,0:T(8,128)S(1)}) custom-call(s32[2]{0:T(128)S(1)} %copy-done.12, bf16[2,3,48,16,128]{4,3,2,1,0:T(8,128)(2,1)S(1)} %copy-done.1, f32[2,48,16,128]{3,2,1,0:T(8,128)S(1)} %copy-done.4, f32[2,48]{1,0:T(2,128)S(1)} %copy-done.13, ...), custom_call_target="tpu_custom_call", output_to_operand_aliasing={{0}: (5, {})} | custom-call | flops 3000000000 | bytes 10000000 | tf_op jit(solution)/shard_map/block_1/pallas_call | solution.py:546
  38.4 0.0 copy-start.5
  38.4 0.7 copy-done.5
  39.1 0.0 all-to-all-done.1.halo_ref
  39.1 0.0 copy-done.8
  39.1 0.0 copy-done.10
  39.1 0.0 copy-done.15
  39.2 0.0 copy-start.6
  39.2 1.0 %copy-done.6 = f32[2,20,16,128]{3,2,1,0:T(8,128)S(1)} copy-done((f32[2,20,16,128]{3,2,1,0:T(8,128)S(1)}, f32[2,20,16,128]{3,2,1,0:T(8,128)}, u32[]{:S(2)}) %copy-start.6) | copy-done | bytes 327704
  40.1 3.9 %outer.1 = (f32[2,3,48,16,128]{4,3,2,1,0:T(8,128)}, f32[8,2,2,3,24,128]{5,4,3,2,1,0:T(8,128)S(1)}, f32[8,2,2,3,24,128]{5,4,3,2,1,0:T(8,128)S(1)}) custom-call(s32[4]{0:T(128)S(1)} %pad_add_fusion.dest_ref, s32[2]{0:T(128)S(1)} %copy-done.12, s32[2,3]{1,0:T(2,128)S(1)} %copy-done.8, s32[2,3]{1,0:T(2,128)S(1)} %copy-done.10, ...), custom_call_target="tpu_custom_call", output_to_operand_aliasing={{0}: (12, {})} | custom-call | tf_op jit(solution)/shard_map/outer/pallas_call | solution.py:588
  44.1 0.1 collective-permute-start
  44.2 2.8 %collective-permute-done = f32[8,2,2,3,24,128]{5,4,3,2,1,0:T(8,128)S(1)} collective-permute-done((f32[8,2,2,3,24,128]{5,4,3,2,1,0:T(8,128)S(1)}, f32[8,2,2,3,24,128]{5,4,3,2,1,0:T(8,128)S(1)}, u32[]{:S(2)}, u32[]{:S(2)}) %collective-permute-start) | collective-permute-done | bytes 1179680 | tf_op jit(solution)/shard_map/ppermute | solution.py:642
  47.0 0.7 shard_map.95
  47.7 2.1 %collective-permute-start.1 = (f32[4,2,72,128]{3,2,1,0:T(8,128)S(1)}, f32[4,2,72,128]{3,2,1,0:T(8,128)S(1)}, u32[]{:S(2)}, u32[]{:S(2)}) collective-permute-start(f32[4,2,72,128]{3,2,1,0:T(8,128)S(1)} %get-tuple-element.37), channel_id=1, source_target_pairs={{0,1},{1,0},{2,3},{3,2},{4,5},{5,4},{6,7},{7,6},{8,9},{9,8},{10,11... | collective-permute-start | bytes 884744 | tf_op jit(solution)/shard_map/ppermute | solution.py:642
  49.7 1.5 %collective-permute-start.2 = (f32[4,2,72,128]{3,2,1,0:T(8,128)S(1)}, f32[4,2,72,128]{3,2,1,0:T(8,128)S(1)}, u32[]{:S(2)}, u32[]{:S(2)}) collective-permute-start(f32[4,2,72,128]{3,2,1,0:T(8,128)S(1)} %get-tuple-element.39), channel_id=1, source_target_pairs={{0,16},{1,17},{2,18},{3,19},{4,20},{5,21},{6,22},{7,23},{8,24},{9,... | collective-permute-start | bytes 884744 | tf_op jit(solution)/shard_map/ppermute | solution.py:642
  51.2 5.9 %collective-permute-done.1.got_y = f32[4,2,72,128]{3,2,1,0:T(8,128)S(1)} collective-permute-done((f32[4,2,72,128]{3,2,1,0:T(8,128)S(1)}, f32[4,2,72,128]{3,2,1,0:T(8,128)S(1)}, u32[]{:S(2)}, u32[]{:S(2)}) %collective-permute-start.1) | collective-permute-done | bytes 294944 | tf_op jit(solution)/shard_map/ppermute | solution.py:642
  57.1 1.5 %collective-permute-done.2.got_x = f32[4,2,72,128]{3,2,1,0:T(8,128)S(1)} collective-permute-done((f32[4,2,72,128]{3,2,1,0:T(8,128)S(1)}, f32[4,2,72,128]{3,2,1,0:T(8,128)S(1)}, u32[]{:S(2)}, u32[]{:S(2)}) %collective-permute-start.2) | collective-permute-done | bytes 294944 | tf_op jit(solution)/shard_map/ppermute | solution.py:642
  58.5 0.6 shard_map.96
  59.1 1.5 %collective-permute-start.3 = (f32[4,72,128]{2,1,0:T(8,128)S(1)}, f32[4,72,128]{2,1,0:T(8,128)S(1)}, u32[]{:S(2)}, u32[]{:S(2)}) collective-permute-start(f32[4,72,128]{2,1,0:T(8,128)S(1)} %get-tuple-element.41), channel_id=1, source_target_pairs={{0,16},{1,17},{2,18},{3,19},{4,20},{5,21},{6,22},{7,23},{8,24},{9,... | collective-permute-start | bytes 442376 | tf_op jit(solution)/shard_map/ppermute | solution.py:642
  60.7 0.4 collective-permute-start.4
  61.0 3.3 %collective-permute-done.3.got_0 = f32[4,72,128]{2,1,0:T(8,128)S(1)} collective-permute-done((f32[4,72,128]{2,1,0:T(8,128)S(1)}, f32[4,72,128]{2,1,0:T(8,128)S(1)}, u32[]{:S(2)}, u32[]{:S(2)}) %collective-permute-start.3) | collective-permute-done | bytes 147488 | tf_op jit(solution)/shard_map/ppermute | solution.py:642
  64.3 1.5 %collective-permute-done.4.got_1 = f32[4,72,128]{2,1,0:T(8,128)S(1)} collective-permute-done((f32[4,72,128]{2,1,0:T(8,128)S(1)}, f32[4,72,128]{2,1,0:T(8,128)S(1)}, u32[]{:S(2)}, u32[]{:S(2)}) %collective-permute-start.4) | collective-permute-done | bytes 147488 | tf_op jit(solution)/shard_map/ppermute | solution.py:642
  65.8 0.6 shard_map.97
  66.4 1.6 %collective-permute-start.5 = (f32[2,72,128]{2,1,0:T(8,128)S(1)}, f32[2,72,128]{2,1,0:T(8,128)S(1)}, u32[]{:S(2)}, u32[]{:S(2)}) collective-permute-start(f32[2,72,128]{2,1,0:T(8,128)S(1)} %get-tuple-element.45), channel_id=1, source_target_pairs={{0,2},{1,3},{2,4},{3,5},{4,6},{5,7},{6,0},{7,1},{8,10},{9,11},{10,... | collective-permute-start | bytes 221192 | tf_op jit(solution)/shard_map/ppermute | solution.py:642
  68.0 2.3 %collective-permute-start.6 = (f32[2,72,128]{2,1,0:T(8,128)S(1)}, f32[2,72,128]{2,1,0:T(8,128)S(1)}, u32[]{:S(2)}, u32[]{:S(2)}) collective-permute-start(f32[2,72,128]{2,1,0:T(8,128)S(1)} %get-tuple-element.46), channel_id=1, source_target_pairs={{0,4},{1,5},{2,6},{3,7},{4,0},{5,1},{6,2},{7,3},{8,12},{9,13},{10,... | collective-permute-start | bytes 221192 | tf_op jit(solution)/shard_map/ppermute | solution.py:642
  70.3 1.5 %collective-permute-start.7 = (f32[2,72,128]{2,1,0:T(8,128)S(1)}, f32[2,72,128]{2,1,0:T(8,128)S(1)}, u32[]{:S(2)}, u32[]{:S(2)}) collective-permute-start(f32[2,72,128]{2,1,0:T(8,128)S(1)} %get-tuple-element.47), channel_id=1, source_target_pairs={{0,6},{1,7},{2,0},{3,1},{4,2},{5,3},{6,4},{7,5},{8,14},{9,15},{10,... | collective-permute-start | bytes 221192 | tf_op jit(solution)/shard_map/ppermute | solution.py:642
  71.8 0.9 %collective-permute-done.5.refs_1_ = f32[2,72,128]{2,1,0:T(8,128)S(1)} collective-permute-done((f32[2,72,128]{2,1,0:T(8,128)S(1)}, f32[2,72,128]{2,1,0:T(8,128)S(1)}, u32[]{:S(2)}, u32[]{:S(2)}) %collective-permute-start.5) | collective-permute-done | bytes 73760 | tf_op jit(solution)/shard_map/ppermute | solution.py:642
  72.7 0.8 collective-permute-done.6.refs_2_
  73.4 1.2 %collective-permute-done.7.refs_3_ = f32[2,72,128]{2,1,0:T(8,128)S(1)} collective-permute-done((f32[2,72,128]{2,1,0:T(8,128)S(1)}, f32[2,72,128]{2,1,0:T(8,128)S(1)}, u32[]{:S(2)}, u32[]{:S(2)}) %collective-permute-start.7) | collective-permute-done | bytes 73760 | tf_op jit(solution)/shard_map/ppermute | solution.py:642
  74.6 0.1 collective-permute-start.10
  74.7 0.8 collective-permute-start.9
  75.5 1.1 %collective-permute-start.8 = (f32[2,72,128]{2,1,0:T(8,128)S(1)}, f32[2,72,128]{2,1,0:T(8,128)S(1)}, u32[]{:S(2)}, u32[]{:S(2)}) collective-permute-start(f32[2,72,128]{2,1,0:T(8,128)S(1)} %shard_map.98), channel_id=1, source_target_pairs={{0,8},{1,9},{2,10},{3,11},{4,12},{5,13},{6,14},{7,15},{8,0},{9,1},... | collective-permute-start | bytes 221192 | tf_op jit(solution)/shard_map/ppermute | solution.py:642
  76.6 2.2 %collective-permute-done.10 = f32[2,72,128]{2,1,0:T(8,128)S(1)} collective-permute-done((f32[2,72,128]{2,1,0:T(8,128)S(1)}, f32[2,72,128]{2,1,0:T(8,128)S(1)}, u32[]{:S(2)}, u32[]{:S(2)}) %collective-permute-start.10) | collective-permute-done | bytes 73760 | tf_op jit(solution)/shard_map/ppermute | solution.py:642
  78.7 1.2 %collective-permute-done.9 = f32[2,72,128]{2,1,0:T(8,128)S(1)} collective-permute-done((f32[2,72,128]{2,1,0:T(8,128)S(1)}, f32[2,72,128]{2,1,0:T(8,128)S(1)}, u32[]{:S(2)}, u32[]{:S(2)}) %collective-permute-start.9) | collective-permute-done | bytes 73760 | tf_op jit(solution)/shard_map/ppermute | solution.py:642
  79.9 0.0 collective-permute-done.8
  79.9 1.8 %shard_map.99 = f32[12,6144]{1,0:T(8,128)} custom-call(s32[4]{0:T(128)S(1)} %pad_add_fusion.dest_ref, f32[2,3,24,128]{3,2,1,0:T(8,128)S(1)} %bitcast.12, f32[2,3,24,128]{3,2,1,0:T(8,128)S(1)} %bitcast.15, f32[2,3,24,128]{3,2,1,0:T(8,128)S(1)} %bitcast.14, f32[2,3,24,128]{3,2,1,0:T(8,128)S(1)} %bitcast.13), custom_call_target="tpu_custom_call" | custom-call | tf_op jit(solution)/shard_map/pallas_call | solution.py:622
  (5 shorter events, 0.0 us)
Async XLA Ops:
  0.6 1.3 %copy-start = (bf16[2,3,48,16,128]{4,3,2,1,0:T(8,128)(2,1)S(1)}, bf16[2,3,48,16,128]{4,3,2,1,0:T(8,128)(2,1)}, u32[]{:S(2)}) copy-start(bf16[2,3,48,16,128]{4,3,2,1,0:T(8,128)(2,1)} %seed_in.5) | copy-start | bytes 3538948
  1.9 1.1 %copy-start.2 = (f32[2,48,16,128]{3,2,1,0:T(8,128)S(1)}, f32[2,48,16,128]{3,2,1,0:T(8,128)}, u32[]{:S(2)}) copy-start(f32[2,48,16,128]{3,2,1,0:T(8,128)} %stiff_in.5) | copy-start | bytes 2359300
  3.0 0.7 copy-start.7
  3.7 0.7 copy-start.9
  4.4 0.7 copy-start.11
  5.1 9.6 %copy-start.1 = (bf16[2,3,48,16,128]{4,3,2,1,0:T(8,128)(2,1)S(1)}, bf16[2,3,48,16,128]{4,3,2,1,0:T(8,128)(2,1)}, u32[]{:S(2)}) copy-start(bf16[2,3,48,16,128]{4,3,2,1,0:T(8,128)(2,1)} %seed_in.5) | copy-start | bytes 3538948
  5.1 9.6 %copy-start.3 = (f32[2,48,16,128]{3,2,1,0:T(8,128)S(1)}, f32[2,48,16,128]{3,2,1,0:T(8,128)}, u32[]{:S(2)}) copy-start(f32[2,48,16,128]{3,2,1,0:T(8,128)} %stiff_in.5) | copy-start | bytes 2359300
  5.1 9.6 %copy-start.12 = (s32[2]{0:T(128)S(1)}, s32[2]{0:T(128)}, u32[]{:S(2)}) copy-start(s32[2]{0:T(128)} %len_ref.5) | copy-start | bytes 28
  5.1 9.6 %copy-start.13 = (f32[2,48]{1,0:T(2,128)S(1)}, f32[2,48]{1,0:T(2,128)}, u32[]{:S(2)}) copy-start(f32[2,48]{1,0:T(2,128)} %cx_ref.5) | copy-start | bytes 1156
  5.1 9.6 %copy-start.14 = (f32[2,128]{1,0:T(2,128)S(1)}, f32[2,128]{1,0:T(2,128)}, u32[]{:S(2)}) copy-start(f32[2,128]{1,0:T(2,128)} %cz_ref.5) | copy-start | bytes 3076
  7.3 16.9 %all-to-all-start = ((f32[8,72,128]{2,1,0:T(8,128)}), f32[8,72,128]{2,1,0:T(8,128)S(1)}, u32[]{:S(2)}, u32[]{:S(2)}) async-start(f32[8,72,128]{2,1,0:T(8,128)} %pack.1), calls=%async_computation | async-start | bytes 589824 | tf_op jit(solution)/shard_map/all_to_all | solution.py:540
  25.2 13.9 %all-to-all-start.1 = ((f32[8,64,128]{2,1,0:T(8,128)}), f32[8,64,128]{2,1,0:T(8,128)S(1)}, u32[]{:S(2)}, u32[]{:S(2)}) async-start(f32[8,64,128]{2,1,0:T(8,128)} %route.1), calls=%async_computation.1 | async-start | bytes 524288 | tf_op jit(solution)/shard_map/all_to_all | solution.py:584
  29.5 1.1 %copy-start.4 = (f32[2,48,16,128]{3,2,1,0:T(8,128)S(1)}, f32[2,48,16,128]{3,2,1,0:T(8,128)}, u32[]{:S(2)}) copy-start(f32[2,48,16,128]{3,2,1,0:T(8,128)} %stiff_in.5) | copy-start | bytes 2359300
  30.6 8.5 %copy-start.8 = (s32[2,3]{1,0:T(2,128)S(1)}, s32[2,3]{1,0:T(2,128)}, u32[]{:S(2)}) copy-start(s32[2,3]{1,0:T(2,128)} %low_ref.1) | copy-start | bytes 76
  30.6 8.5 %copy-start.10 = (s32[2,3]{1,0:T(2,128)S(1)}, s32[2,3]{1,0:T(2,128)}, u32[]{:S(2)}) copy-start(s32[2,3]{1,0:T(2,128)} %up_ref.1) | copy-start | bytes 76
  30.6 8.5 %copy-start.15 = (f32[2,16]{1,0:T(2,128)S(1)}, f32[2,16]{1,0:T(2,128)}, u32[]{:S(2)}) copy-start(f32[2,16]{1,0:T(2,128)} %cy_ref.1) | copy-start | bytes 388
  38.4 0.7 copy-start.5
  39.2 1.0 %copy-start.6 = (f32[2,20,16,128]{3,2,1,0:T(8,128)S(1)}, f32[2,20,16,128]{3,2,1,0:T(8,128)}, u32[]{:S(2)}) copy-start(f32[2,20,16,128]{3,2,1,0:T(8,128)} %copy-done.5) | copy-start | bytes 983044
  44.1 2.9 %collective-permute-start = (f32[8,2,2,3,24,128]{5,4,3,2,1,0:T(8,128)S(1)}, f32[8,2,2,3,24,128]{5,4,3,2,1,0:T(8,128)S(1)}, u32[]{:S(2)}, u32[]{:S(2)}) collective-permute-start(f32[8,2,2,3,24,128]{5,4,3,2,1,0:T(8,128)S(1)} %get-tuple-element.35), channel_id=1, source_target_pairs={{0,8},{1,9},{2,10},{3,11},{4,12},{5,13},{6,14},{7,15},{8,0},{9,1},... | collective-permute-start | bytes 3538952 | tf_op jit(solution)/shard_map/ppermute | solution.py:642
  47.7 9.4 %collective-permute-start.1 = (f32[4,2,72,128]{3,2,1,0:T(8,128)S(1)}, f32[4,2,72,128]{3,2,1,0:T(8,128)S(1)}, u32[]{:S(2)}, u32[]{:S(2)}) collective-permute-start(f32[4,2,72,128]{3,2,1,0:T(8,128)S(1)} %get-tuple-element.37), channel_id=1, source_target_pairs={{0,1},{1,0},{2,3},{3,2},{4,5},{5,4},{6,7},{7,6},{8,9},{9,8},{10,11... | collective-permute-start | bytes 884744 | tf_op jit(solution)/shard_map/ppermute | solution.py:642
  49.7 8.8 %collective-permute-start.2 = (f32[4,2,72,128]{3,2,1,0:T(8,128)S(1)}, f32[4,2,72,128]{3,2,1,0:T(8,128)S(1)}, u32[]{:S(2)}, u32[]{:S(2)}) collective-permute-start(f32[4,2,72,128]{3,2,1,0:T(8,128)S(1)} %get-tuple-element.39), channel_id=1, source_target_pairs={{0,16},{1,17},{2,18},{3,19},{4,20},{5,21},{6,22},{7,23},{8,24},{9,... | collective-permute-start | bytes 884744 | tf_op jit(solution)/shard_map/ppermute | solution.py:642
  59.1 5.2 %collective-permute-start.3 = (f32[4,72,128]{2,1,0:T(8,128)S(1)}, f32[4,72,128]{2,1,0:T(8,128)S(1)}, u32[]{:S(2)}, u32[]{:S(2)}) collective-permute-start(f32[4,72,128]{2,1,0:T(8,128)S(1)} %get-tuple-element.41), channel_id=1, source_target_pairs={{0,16},{1,17},{2,18},{3,19},{4,20},{5,21},{6,22},{7,23},{8,24},{9,... | collective-permute-start | bytes 442376 | tf_op jit(solution)/shard_map/ppermute | solution.py:642
  60.7 5.1 %collective-permute-start.4 = (f32[4,72,128]{2,1,0:T(8,128)S(1)}, f32[4,72,128]{2,1,0:T(8,128)S(1)}, u32[]{:S(2)}, u32[]{:S(2)}) collective-permute-start(f32[4,72,128]{2,1,0:T(8,128)S(1)} %get-tuple-element.43), channel_id=1, source_target_pairs={{0,1},{1,0},{2,3},{3,2},{4,5},{5,4},{6,7},{7,6},{8,9},{9,8},{10,11... | collective-permute-start | bytes 442376 | tf_op jit(solution)/shard_map/ppermute | solution.py:642
  66.4 6.3 %collective-permute-start.5 = (f32[2,72,128]{2,1,0:T(8,128)S(1)}, f32[2,72,128]{2,1,0:T(8,128)S(1)}, u32[]{:S(2)}, u32[]{:S(2)}) collective-permute-start(f32[2,72,128]{2,1,0:T(8,128)S(1)} %get-tuple-element.45), channel_id=1, source_target_pairs={{0,2},{1,3},{2,4},{3,5},{4,6},{5,7},{6,0},{7,1},{8,10},{9,11},{10,... | collective-permute-start | bytes 221192 | tf_op jit(solution)/shard_map/ppermute | solution.py:642
  68.0 5.5 %collective-permute-start.6 = (f32[2,72,128]{2,1,0:T(8,128)S(1)}, f32[2,72,128]{2,1,0:T(8,128)S(1)}, u32[]{:S(2)}, u32[]{:S(2)}) collective-permute-start(f32[2,72,128]{2,1,0:T(8,128)S(1)} %get-tuple-element.46), channel_id=1, source_target_pairs={{0,4},{1,5},{2,6},{3,7},{4,0},{5,1},{6,2},{7,3},{8,12},{9,13},{10,... | collective-permute-start | bytes 221192 | tf_op jit(solution)/shard_map/ppermute | solution.py:642
  70.3 4.4 %collective-permute-start.7 = (f32[2,72,128]{2,1,0:T(8,128)S(1)}, f32[2,72,128]{2,1,0:T(8,128)S(1)}, u32[]{:S(2)}, u32[]{:S(2)}) collective-permute-start(f32[2,72,128]{2,1,0:T(8,128)S(1)} %get-tuple-element.47), channel_id=1, source_target_pairs={{0,6},{1,7},{2,0},{3,1},{4,2},{5,3},{6,4},{7,5},{8,14},{9,15},{10,... | collective-permute-start | bytes 221192 | tf_op jit(solution)/shard_map/ppermute | solution.py:642
  74.6 4.1 %collective-permute-start.10 = (f32[2,72,128]{2,1,0:T(8,128)S(1)}, f32[2,72,128]{2,1,0:T(8,128)S(1)}, u32[]{:S(2)}, u32[]{:S(2)}) collective-permute-start(f32[2,72,128]{2,1,0:T(8,128)S(1)} %shard_map.98), channel_id=1, source_target_pairs={{0,24},{1,25},{2,26},{3,27},{4,28},{5,29},{6,30},{7,31},{8,16},{9,... | collective-permute-start | bytes 221192 | tf_op jit(solution)/shard_map/ppermute | solution.py:642
  74.7 5.2 %collective-permute-start.9 = (f32[2,72,128]{2,1,0:T(8,128)S(1)}, f32[2,72,128]{2,1,0:T(8,128)S(1)}, u32[]{:S(2)}, u32[]{:S(2)}) collective-permute-start(f32[2,72,128]{2,1,0:T(8,128)S(1)} %shard_map.98), channel_id=1, source_target_pairs={{0,16},{1,17},{2,18},{3,19},{4,20},{5,21},{6,22},{7,23},{8,24},{9,... | collective-permute-start | bytes 221192 | tf_op jit(solution)/shard_map/ppermute | solution.py:642
  75.5 4.4 %collective-permute-start.8 = (f32[2,72,128]{2,1,0:T(8,128)S(1)}, f32[2,72,128]{2,1,0:T(8,128)S(1)}, u32[]{:S(2)}, u32[]{:S(2)}) collective-permute-start(f32[2,72,128]{2,1,0:T(8,128)S(1)} %shard_map.98), channel_id=1, source_target_pairs={{0,8},{1,9},{2,10},{3,11},{4,12},{5,13},{6,14},{7,15},{8,0},{9,1},... | collective-permute-start | bytes 221192 | tf_op jit(solution)/shard_map/ppermute | solution.py:642

commit v4 on v3

--- a/solution.py
+++ b/solution.py
@@ -13,7 +13,7 @@
 LZ = 32
 DOMINANCE = 1.25
 PLANES = 8
-STEP = 4
+STEP = 24
 ENDS = 3
 EDGES = 20
 
@@ -153,19 +153,38 @@
     return thrice(jnp.where((row // LZ) == (lane // nz), hat, 0.0), 1, False)
 
 
+class Planes:
+    def __init__(self, ref, start, ny):
+        self.ref, self.start, self.ny = ref, start, ny
+
+    def rows(self, key):
+        return pl.ds(self.start + (key[0] * EDGES + key[1]) * self.ny, self.ny)
+
+    def __getitem__(self, key):
+        return self.ref[self.rows(key)]
+
+    def __setitem__(self, key, value):
+        self.ref[self.rows(key)] = value
+
+
 def block_kernel(b, len_ref, seed_in, stiff_in, cx_ref, cz_ref, *refs):
-    adj_out, edge_ref, part_ref, s_ext, w_ext, v_ext, fac_ref, mul_ref, adj, seeds, zdone, sems = refs[-12:]
+    s_ext, w_ext, v_ext, fac_ref, mul_ref, adj, seeds, zdone, sems = refs[-9:]
+    adj_out, part_ref, *passed = refs[:3] if b == 0 else refs[1:3]
     nx, ny, nz = fac_ref.shape
+    edge_ref = Planes(part_ref, LX * (ny + 1), ny)
     last = 8 + ny
     length = len_ref[b]
     loads = (
         pltpu.make_async_copy(
-            stiff_in.at[b], s_ext.at[pl.ds(1, nx), pl.ds(8, ny)], sems.at[0]
+            stiff_in.at[0] if b == 0 else stiff_in, s_ext.at[pl.ds(1, nx), pl.ds(8, ny)], sems.at[0]
         ),
         pltpu.make_async_copy(seed_in.at[b], seeds, sems.at[1]),
     )
     for copy in loads:
         copy.start()
+    if b == 0:
+        ahead = pltpu.make_async_copy(stiff_in.at[1], passed[0], sems.at[3])
+        ahead.start()
     zeros = jnp.zeros((nx + 2, 8, nz), F32)
     plane = jnp.zeros((ny, nz), F32)
     for ref, lead in ((s_ext, ()), *((r, (c,)) for r in (w_ext, v_ext) for c in range(3))):
@@ -271,6 +290,8 @@
         for k in range(2):
             part_ref[pl.ds(y + k, LX, stride=pitch), :] = done[:, 128 * k : 128 * (k + 1)]
     store.wait()
+    if b == 0:
+        ahead.wait()
 
 
 def outer_kernel(
@@ -281,8 +302,6 @@
     up_ref,
     cx_ref,
     halo_ref,
-    edge_0,
-    edge_1,
     part_0,
     part_1,
     cy_ref,
@@ -300,7 +319,7 @@
     del adj_in
     slots = 2
     faces = 2 * slots
-    _, _, ny, nz = edge_0.shape
+    _, _, _, ny, nz = ends.shape
     pitch = ny + 1
     chunk = halo_ref.shape[1] // faces
     zero_plane = jnp.zeros((ny, nz), F32)
@@ -335,29 +354,29 @@
     copies = []
     for f in range(faces):
         b, side = f // 2, f % 2
-        edge = (edge_0, edge_1)[b].at[side]
-        stiff, inside = edge[0], edge[1]
+        edge = Planes((part_0, part_1)[b], LX * pitch, ny)
+        stiff, inside = edge[side, 0], edge[side, 1]
         beside = plane_parts(stiff)[0]
         there = 1.0 / (DOMINANCE * (pack[f, 1] + beside))
         inv = 1.0 / (DOMINANCE * stiff * (inside + plane_parts(pack[f, 0])[0]))
         fac = stiff * inv
-        mul_1, fac_1, fac_2 = edge[17], edge[18], edge[19]
+        mul_1, fac_1, fac_2 = edge[side, 17], edge[side, 18], edge[side, 19]
         for c in range(3):
-            seed = edge[2 + c]
+            seed = edge[side, 2 + c]
             w_n = pack[f, 2 + c] * there
             w_0 = seed * fac
             beside_n, own_n = plane_parts(w_n)
             beside_0, own_0 = plane_parts(w_0)
             v_n = w_n + pack[f, 0] * there * (own_n + pack[f, 5 + c] + beside_0)
-            v_0 = w_0 + stiff * fac * (own_0 + edge[5 + c] + beside_n)
-            v_1 = edge[8 + c] + mul_1 * beside_0
+            v_0 = w_0 + stiff * fac * (own_0 + edge[side, 5 + c] + beside_n)
+            v_1 = edge[side, 8 + c] + mul_1 * beside_0
             beside_n = plane_parts(v_n)[0]
             beside_0, own_0 = plane_parts(v_0)
             beside_1, own_1 = plane_parts(v_1)
             rows = [
                 seed * inv + fac * (own_0 + beside_1 + beside_n),
-                edge[11 + c] + fac_1 * (own_1 + beside_0),
-                edge[14 + c] + fac_2 * beside_1,
+                edge[side, 11 + c] + fac_1 * (own_1 + beside_0),
+                edge[side, 14 + c] + fac_2 * beside_1,
             ]
             for k, row in enumerate(rows):
                 ends[b, c, k if side == 0 else 2 * ENDS - 1 - k] = row
@@ -534,24 +553,23 @@
             pltpu.VMEM((faces, PLANES * ny, nz), F32),
             pltpu.SemaphoreType.DMA((3, faces)),
         ],
-        compiler_params=params(4),
+        compiler_params=params(60),
         name="pack",
     )(lengths, low, up, seed, stiff)
     spread = lax.all_to_all(packed, "dev", 0, 0)
     ext = (nx + 2, ny + 16, nz)
     plain = pltpu.VMEM((nx, ny, nz), F32)
 
-    def one_block(b, adjoint):
-        given = () if adjoint is None else (adjoint,)
+    def one_block(b, stiff, *given):
         return pl.pallas_call(
             functools.partial(block_kernel, b),
             out_shape=(
                 shape(slots, 3, nx, ny, nz),
-                shape(2, EDGES, ny, nz),
-                shape(LX * (ny + 1), 128),
+                shape(LX * (ny + 1) + 2 * EDGES * ny, 128),
+                *([shape(nx, ny, nz)] if b == 0 else []),
             ),
             in_specs=[SMEM, ANY, ANY, VMEM, VMEM] + [HBM] * len(given),
-            out_specs=(HBM, VMEM, VMEM),
+            out_specs=(HBM, VMEM, VMEM) if b == 0 else (HBM, VMEM),
             scratch_shapes=[
                 pltpu.VMEM(ext, F32),
                 pltpu.VMEM((3, *ext), F32),
@@ -561,17 +579,17 @@
                 pltpu.VMEM((3, nx, ny, nz), F32),
                 pltpu.VMEM((3, nx, ny, nz), seed.dtype),
                 pltpu.VMEM((nx * (ny + 1), 128), F32),
-                pltpu.SemaphoreType.DMA((3,)),
+                pltpu.SemaphoreType.DMA((4,)),
             ],
             input_output_aliases={5: 0} if given else {},
-            compiler_params=params(16),
+            compiler_params=params(12),
             cost_estimate=pl.CostEstimate(
                 flops=3 * 10**9, bytes_accessed=10**7, transcendentals=0
             ),
             name=f"block_{b}",
         )(lengths, seed, stiff, coord_x, coord_z, *given)
 
-    early, edge_0, part_0 = one_block(0, None)
+    early, part_0, stiff_1 = one_block(0, stiff)
     routed = pl.pallas_call(
         route_kernel,
         out_shape=shape(devs, rows, nz),
@@ -582,13 +600,13 @@
     )(spread)
     early, routed = lax.optimization_barrier((early, routed))
     halos = lax.all_to_all(routed, "dev", 0, 0)
-    early, edge_1, part_1 = one_block(1, early)
+    early, part_1 = one_block(1, stiff_1, early)
 
     half = shape(devs, 2, 2, pieces, size, 128)
     adjoint, keep, send = pl.pallas_call(
         functools.partial(outer_kernel, per),
         out_shape=(shape(slots, 3, nx, ny, nz), half, half),
-        in_specs=[SMEM] * 5 + [VMEM] * 7 + [HBM],
+        in_specs=[SMEM] * 5 + [VMEM] * 5 + [HBM],
         out_specs=(HBM, VMEM, VMEM),
         scratch_shapes=[
             pltpu.VMEM((faces, PLANES, ny, nz), F32),
@@ -597,8 +615,8 @@
             pltpu.VMEM((slots, LX * (ny + 1), 128), F32),
             pltpu.SemaphoreType.DMA((faces, 3)),
         ],
-        input_output_aliases={12: 0},
-        compiler_params=params(16),
+        input_output_aliases={10: 0},
+        compiler_params=params(12),
         name="outer",
     )(
         dest,
@@ -607,8 +625,6 @@
         up,
         coord_x,
         halos,
-        edge_0,
-        edge_1,
         part_0,
         part_1,
         coord_y,

time: 82.3 us -> 75.3 us (0.915)
  local copies, waits for them, and re-layouts: 7.26 us -> 3.04 us
  Pallas kernels: 26.3 us -> 22.1 us
  waiting for transfers between devices: 23.1 us -> 26.8 us
  starting transfers between devices: 24.3 us -> 22 us
    pallas_call x2, Pallas kernels: 15.4 us -> 10.6 us  [one_block(): pl.pallas_call(functools.partial(block_kernel, b), out_shape=(shape(slots...]
    unnamed x32 -> x24, local copies, waits for them, and re-layouts: 7.26 us -> 3.04 us
    all_to_all x1, waiting for transfers between devices: 1.95 us -> 3.93 us  [on_device(): spread = lax.all_to_all(packed, 'dev', 0, 0)]
    ppermute x11, starting transfers between devices: 12.8 us -> 11.1 us  [move(): return lax.ppermute(value, ('group', 'dev'), links)]
    all_to_all x1, waiting for transfers between devices: 0.01 us -> 1.71 us  [on_device(): halos = lax.all_to_all(routed, 'dev', 0, 0)]
  transfers between devices with their start and end apart: 13 -> 13, of which waited for: 11 -> 11; matrix products, arithmetic and copies ran while one was open for 0% -> 0% of each run, Pallas kernels for 19% -> 14%
where the time goes in v4:
time: 75.3 us; the launch traced here: 74.9 us
  waiting for transfers between devices  26.8 us (36%)
  Pallas kernels  22.1 us (29%)
  starting transfers between devices  22 us (29%)
  local copies, waits for them, and re-layouts  3.04 us (4%)
  between operations  0.83 us (1%)
    ppermute x11, waiting for transfers between devices, move(): return lax.ppermute(value, ('group', 'dev'), links)  21.2 us
    ppermute x11, starting transfers between devices, move(): return lax.ppermute(value, ('group', 'dev'), links)  11.1 us
    pallas_call x2, Pallas kernels, one_block(): pl.pallas_call(functools.partial(block_kernel, b), out_shape=(shape(slots...  10.6 us
    all_to_all x1, starting transfers between devices, on_device(): spread = lax.all_to_all(packed, 'dev', 0, 0)  7.32 us
    pallas_call x1, Pallas kernels, on_device(): pl.pallas_call(functools.partial(outer_kernel, per), out_shape=(shape(slo...  4.11 us
    all_to_all x1, waiting for transfers between devices, on_device(): spread = lax.all_to_all(packed, 'dev', 0, 0)  3.93 us
    pallas_call x5, Pallas kernels, small(): pl.pallas_call(kernel, out_shape=outs, in_specs=[SMEM if a is dest else V...  3.71 us
    all_to_all x1, starting transfers between devices, on_device(): halos = lax.all_to_all(routed, 'dev', 0, 0)  3.62 us
  transfers between devices with their start and end apart: 13, of which 11 were waited for; matrix products, arithmetic and copies ran while one was open for 0% of the time, Pallas kernels for 14%

profile of v4, /device:TPU:0, one launch (start us, length us, event | category | flops | bytes accessed | tf_op | source)
XLA Modules:
  0.0 74.9 jit_solution(13773761808998295973)
XLA Ops:
  0.6 0.0 copy-start.6
  0.6 0.0 copy-start
  0.7 0.0 copy-start.3
  0.7 0.0 copy-start.8
  0.7 0.0 copy-start.7
  0.7 2.7 %pack.1 = f32[8,72,128]{2,1,0:T(8,128)} custom-call(s32[2]{0:T(128)} %len_ref.5, s32[2,3]{1,0:T(2,128)} %low_ref.1, s32[2,3]{1,0:T(2,128)} %up_ref.1, bf16[2,3,48,16,128]{4,3,2,1,0:T(8,128)(2,1)} %seed_in.5, f32[2,48,16,128]{3,2,1,0:T(8,128)} %stiff_in.3), custom_call_target="tpu_custom_call" | custom-call | tf_op jit(solution)/shard_map/pack/pallas_call | solution.py:542
  3.4 7.3 %all-to-all-start = ((f32[8,72,128]{2,1,0:T(8,128)}), f32[8,72,128]{2,1,0:T(8,128)S(1)}, u32[]{:S(2)}, u32[]{:S(2)}) async-start(f32[8,72,128]{2,1,0:T(8,128)} %pack.1), calls=%async_computation | async-start | bytes 589824 | tf_op jit(solution)/shard_map/all_to_all | solution.py:559
  10.8 0.0 copy-done.6
  10.8 0.0 copy-done
  10.8 0.0 copy-done.3
  10.8 0.0 copy-done.8
  10.8 0.0 copy-done.7
  10.8 4.9 %block_0.1 = (f32[2,3,48,16,128]{4,3,2,1,0:T(8,128)}, f32[2272,128]{1,0:T(8,128)S(1)}, f32[48,16,128]{2,1,0:T(8,128)S(1)}) custom-call(s32[2]{0:T(128)S(1)} %copy-done.6, bf16[2,3,48,16,128]{4,3,2,1,0:T(8,128)(2,1)S(1)} %copy-done, f32[2,48,16,128]{3,2,1,0:T(8,128)S(1)} %copy-done.3, f32[2,48]{1,0:T(2,128)S(1)} %copy-done.7, f32[2,128]{1,0:T(2,128)S(1)} %copy-done.8), custom_call_target="tpu_custom_call" | custom-call | flops 3000000000 | bytes 10000000 | tf_op jit(solution)/shard_map/block_0/pallas_call | solution.py:564
  15.7 0.0 copy-start.10
  15.7 0.7 copy-done.10
  16.4 3.9 %all-to-all-done.in_ref = f32[8,72,128]{2,1,0:T(8,128)S(1)} async-done(((f32[8,72,128]{2,1,0:T(8,128)}), f32[8,72,128]{2,1,0:T(8,128)S(1)}, u32[]{:S(2)}, u32[]{:S(2)}) %all-to-all-start) | async-done | bytes 294944 | tf_op jit(solution)/shard_map/all_to_all | solution.py:559
  20.4 0.0 copy-start.11
  20.4 1.0 %route.1 = f32[8,64,128]{2,1,0:T(8,128)} custom-call(f32[8,72,128]{2,1,0:T(8,128)S(1)} %all-to-all-done.in_ref), custom_call_target="tpu_custom_call" | custom-call | tf_op jit(solution)/shard_map/route/pallas_call | solution.py:593
  21.3 3.6 %all-to-all-start.1 = ((f32[8,64,128]{2,1,0:T(8,128)}), f32[8,64,128]{2,1,0:T(8,128)S(1)}, u32[]{:S(2)}, u32[]{:S(2)}) async-start(f32[8,64,128]{2,1,0:T(8,128)} %route.1), calls=%async_computation.1 | async-start | bytes 524288 | tf_op jit(solution)/shard_map/all_to_all | solution.py:602
  25.0 0.1 pad_add_fusion.dest_ref
  25.0 0.0 copy-done.11
  25.0 0.0 copy-start.4
  25.0 0.0 copy-start.5
  25.0 0.0 copy-start.9
  25.1 5.7 %block_1.1 = (f32[2,3,48,16,128]{4,3,2,1,0:T(8,128)}, f32[2272,128]{1,0:T(8,128)S(1)}) custom-call(s32[2]{0:T(128)S(1)} %copy-done.6, bf16[2,3,48,16,128]{4,3,2,1,0:T(8,128)(2,1)S(1)} %copy-done, f32[48,16,128]{2,1,0:T(8,128)S(1)} %copy-done.11, f32[2,48]{1,0:T(2,128)S(1)} %copy-done.7, f32[2,128]{1,0:T(2,128)S(1)} %copy-done.8, ...), custom_call_target="tpu_custom_call", output_to_operand_aliasing={{0}: (5, {})} | custom-call | flops 3000000000 | bytes 10000000 | tf_op jit(solution)/shard_map/block_1/pallas_call | solution.py:564
  30.8 0.0 copy-start.1
  30.8 1.0 %copy-done.1 = f32[2272,128]{1,0:T(8,128)} copy-done((f32[2272,128]{1,0:T(8,128)}, f32[2272,128]{1,0:T(8,128)S(1)}, u32[]{:S(2)}) %copy-start.1) | copy-done | bytes 1163288
  31.8 1.7 %all-to-all-done.1.halo_ref = f32[8,64,128]{2,1,0:T(8,128)S(1)} async-done(((f32[8,64,128]{2,1,0:T(8,128)}), f32[8,64,128]{2,1,0:T(8,128)S(1)}, u32[]{:S(2)}, u32[]{:S(2)}) %all-to-all-start.1) | async-done | bytes 262176 | tf_op jit(solution)/shard_map/all_to_all | solution.py:602
  33.5 0.0 copy-done.4
  33.5 0.0 copy-done.5
  33.5 0.0 copy-done.9
  33.5 0.0 copy-start.2
  33.5 1.3 %copy-done.2 = f32[2272,128]{1,0:T(8,128)S(1)} copy-done((f32[2272,128]{1,0:T(8,128)S(1)}, f32[2272,128]{1,0:T(8,128)}, u32[]{:S(2)}) %copy-start.2) | copy-done | bytes 1163288
  34.8 4.1 %outer.1 = (f32[2,3,48,16,128]{4,3,2,1,0:T(8,128)}, f32[8,2,2,3,24,128]{5,4,3,2,1,0:T(8,128)S(1)}, f32[8,2,2,3,24,128]{5,4,3,2,1,0:T(8,128)S(1)}) custom-call(s32[4]{0:T(128)S(1)} %pad_add_fusion.dest_ref, s32[2]{0:T(128)S(1)} %copy-done.6, s32[2,3]{1,0:T(2,128)S(1)} %copy-done.4, s32[2,3]{1,0:T(2,128)S(1)} %copy-done.5, ...), custom_call_target="tpu_custom_call", output_to_operand_aliasing={{0}: (10, {})} | custom-call | tf_op jit(solution)/shard_map/outer/pallas_call | solution.py:606
  38.9 0.1 collective-permute-start
  39.0 2.8 %collective-permute-done = f32[8,2,2,3,24,128]{5,4,3,2,1,0:T(8,128)S(1)} collective-permute-done((f32[8,2,2,3,24,128]{5,4,3,2,1,0:T(8,128)S(1)}, f32[8,2,2,3,24,128]{5,4,3,2,1,0:T(8,128)S(1)}, u32[]{:S(2)}, u32[]{:S(2)}) %collective-permute-start) | collective-permute-done | bytes 1179680 | tf_op jit(solution)/shard_map/ppermute | solution.py:658
  41.8 0.7 shard_map.95
  42.5 1.5 %collective-permute-start.1 = (f32[4,2,72,128]{3,2,1,0:T(8,128)S(1)}, f32[4,2,72,128]{3,2,1,0:T(8,128)S(1)}, u32[]{:S(2)}, u32[]{:S(2)}) collective-permute-start(f32[4,2,72,128]{3,2,1,0:T(8,128)S(1)} %get-tuple-element.35), channel_id=1, source_target_pairs={{0,1},{1,0},{2,3},{3,2},{4,5},{5,4},{6,7},{7,6},{8,9},{9,8},{10,11... | collective-permute-start | bytes 884744 | tf_op jit(solution)/shard_map/ppermute | solution.py:658
  44.0 1.4 %collective-permute-start.2 = (f32[4,2,72,128]{3,2,1,0:T(8,128)S(1)}, f32[4,2,72,128]{3,2,1,0:T(8,128)S(1)}, u32[]{:S(2)}, u32[]{:S(2)}) collective-permute-start(f32[4,2,72,128]{3,2,1,0:T(8,128)S(1)} %get-tuple-element.37), channel_id=1, source_target_pairs={{0,16},{1,17},{2,18},{3,19},{4,20},{5,21},{6,22},{7,23},{8,24},{9,... | collective-permute-start | bytes 884744 | tf_op jit(solution)/shard_map/ppermute | solution.py:658
  45.4 6.2 %collective-permute-done.1.got_y = f32[4,2,72,128]{3,2,1,0:T(8,128)S(1)} collective-permute-done((f32[4,2,72,128]{3,2,1,0:T(8,128)S(1)}, f32[4,2,72,128]{3,2,1,0:T(8,128)S(1)}, u32[]{:S(2)}, u32[]{:S(2)}) %collective-permute-start.1) | collective-permute-done | bytes 294944 | tf_op jit(solution)/shard_map/ppermute | solution.py:658
  51.6 1.2 %collective-permute-done.2.got_x = f32[4,2,72,128]{3,2,1,0:T(8,128)S(1)} collective-permute-done((f32[4,2,72,128]{3,2,1,0:T(8,128)S(1)}, f32[4,2,72,128]{3,2,1,0:T(8,128)S(1)}, u32[]{:S(2)}, u32[]{:S(2)}) %collective-permute-start.2) | collective-permute-done | bytes 294944 | tf_op jit(solution)/shard_map/ppermute | solution.py:658
  52.7 0.6 shard_map.96
  53.3 1.5 %collective-permute-start.3 = (f32[4,72,128]{2,1,0:T(8,128)S(1)}, f32[4,72,128]{2,1,0:T(8,128)S(1)}, u32[]{:S(2)}, u32[]{:S(2)}) collective-permute-start(f32[4,72,128]{2,1,0:T(8,128)S(1)} %get-tuple-element.39), channel_id=1, source_target_pairs={{0,16},{1,17},{2,18},{3,19},{4,20},{5,21},{6,22},{7,23},{8,24},{9,... | collective-permute-start | bytes 442376 | tf_op jit(solution)/shard_map/ppermute | solution.py:658
  54.8 0.6 collective-permute-start.4
  55.4 3.2 %collective-permute-done.3.got_0 = f32[4,72,128]{2,1,0:T(8,128)S(1)} collective-permute-done((f32[4,72,128]{2,1,0:T(8,128)S(1)}, f32[4,72,128]{2,1,0:T(8,128)S(1)}, u32[]{:S(2)}, u32[]{:S(2)}) %collective-permute-start.3) | collective-permute-done | bytes 147488 | tf_op jit(solution)/shard_map/ppermute | solution.py:658
  58.6 1.4 %collective-permute-done.4.got_1 = f32[4,72,128]{2,1,0:T(8,128)S(1)} collective-permute-done((f32[4,72,128]{2,1,0:T(8,128)S(1)}, f32[4,72,128]{2,1,0:T(8,128)S(1)}, u32[]{:S(2)}, u32[]{:S(2)}) %collective-permute-start.4) | collective-permute-done | bytes 147488 | tf_op jit(solution)/shard_map/ppermute | solution.py:658
  60.0 0.6 shard_map.97
  60.6 0.3 collective-permute-start.5
  60.8 2.5 %collective-permute-start.6 = (f32[2,72,128]{2,1,0:T(8,128)S(1)}, f32[2,72,128]{2,1,0:T(8,128)S(1)}, u32[]{:S(2)}, u32[]{:S(2)}) collective-permute-start(f32[2,72,128]{2,1,0:T(8,128)S(1)} %get-tuple-element.44), channel_id=1, source_target_pairs={{0,4},{1,5},{2,6},{3,7},{4,0},{5,1},{6,2},{7,3},{8,12},{9,13},{10,... | collective-permute-start | bytes 221192 | tf_op jit(solution)/shard_map/ppermute | solution.py:658
  63.3 1.4 %collective-permute-start.7 = (f32[2,72,128]{2,1,0:T(8,128)S(1)}, f32[2,72,128]{2,1,0:T(8,128)S(1)}, u32[]{:S(2)}, u32[]{:S(2)}) collective-permute-start(f32[2,72,128]{2,1,0:T(8,128)S(1)} %get-tuple-element.45), channel_id=1, source_target_pairs={{0,6},{1,7},{2,0},{3,1},{4,2},{5,3},{6,4},{7,5},{8,14},{9,15},{10,... | collective-permute-start | bytes 221192 | tf_op jit(solution)/shard_map/ppermute | solution.py:658
  64.7 2.2 %collective-permute-done.5.refs_1_ = f32[2,72,128]{2,1,0:T(8,128)S(1)} collective-permute-done((f32[2,72,128]{2,1,0:T(8,128)S(1)}, f32[2,72,128]{2,1,0:T(8,128)S(1)}, u32[]{:S(2)}, u32[]{:S(2)}) %collective-permute-start.5) | collective-permute-done | bytes 73760 | tf_op jit(solution)/shard_map/ppermute | solution.py:658
  66.9 0.9 %collective-permute-done.6.refs_2_ = f32[2,72,128]{2,1,0:T(8,128)S(1)} collective-permute-done((f32[2,72,128]{2,1,0:T(8,128)S(1)}, f32[2,72,128]{2,1,0:T(8,128)S(1)}, u32[]{:S(2)}, u32[]{:S(2)}) %collective-permute-start.6) | collective-permute-done | bytes 73760 | tf_op jit(solution)/shard_map/ppermute | solution.py:658
  67.7 0.0 collective-permute-done.7.refs_3_
  67.8 0.1 collective-permute-start.10
  67.8 0.7 collective-permute-start.9
  68.5 1.2 %collective-permute-start.8 = (f32[2,72,128]{2,1,0:T(8,128)S(1)}, f32[2,72,128]{2,1,0:T(8,128)S(1)}, u32[]{:S(2)}, u32[]{:S(2)}) collective-permute-start(f32[2,72,128]{2,1,0:T(8,128)S(1)} %shard_map.98), channel_id=1, source_target_pairs={{0,8},{1,9},{2,10},{3,11},{4,12},{5,13},{6,14},{7,15},{8,0},{9,1},... | collective-permute-start | bytes 221192 | tf_op jit(solution)/shard_map/ppermute | solution.py:658
  69.7 2.0 %collective-permute-done.10 = f32[2,72,128]{2,1,0:T(8,128)S(1)} collective-permute-done((f32[2,72,128]{2,1,0:T(8,128)S(1)}, f32[2,72,128]{2,1,0:T(8,128)S(1)}, u32[]{:S(2)}, u32[]{:S(2)}) %collective-permute-start.10) | collective-permute-done | bytes 73760 | tf_op jit(solution)/shard_map/ppermute | solution.py:658
  71.7 1.3 %collective-permute-done.9 = f32[2,72,128]{2,1,0:T(8,128)S(1)} collective-permute-done((f32[2,72,128]{2,1,0:T(8,128)S(1)}, f32[2,72,128]{2,1,0:T(8,128)S(1)}, u32[]{:S(2)}, u32[]{:S(2)}) %collective-permute-start.9) | collective-permute-done | bytes 73760 | tf_op jit(solution)/shard_map/ppermute | solution.py:658
  73.0 0.0 collective-permute-done.8
  73.0 1.8 %shard_map.99 = f32[12,6144]{1,0:T(8,128)} custom-call(s32[4]{0:T(128)S(1)} %pad_add_fusion.dest_ref, f32[2,3,24,128]{3,2,1,0:T(8,128)S(1)} %bitcast.12, f32[2,3,24,128]{3,2,1,0:T(8,128)S(1)} %bitcast.15, f32[2,3,24,128]{3,2,1,0:T(8,128)S(1)} %bitcast.14, f32[2,3,24,128]{3,2,1,0:T(8,128)S(1)} %bitcast.13), custom_call_target="tpu_custom_call" | custom-call | tf_op jit(solution)/shard_map/pallas_call | solution.py:638
  (1 shorter events, 0.0 us)
Async XLA Ops:
  0.6 10.1 %copy-start.6 = (s32[2]{0:T(128)S(1)}, s32[2]{0:T(128)}, u32[]{:S(2)}) copy-start(s32[2]{0:T(128)} %len_ref.5) | copy-start | bytes 28
  0.6 10.1 %copy-start = (bf16[2,3,48,16,128]{4,3,2,1,0:T(8,128)(2,1)S(1)}, bf16[2,3,48,16,128]{4,3,2,1,0:T(8,128)(2,1)}, u32[]{:S(2)}) copy-start(bf16[2,3,48,16,128]{4,3,2,1,0:T(8,128)(2,1)} %seed_in.5) | copy-start | bytes 3538948
  0.7 10.1 %copy-start.3 = (f32[2,48,16,128]{3,2,1,0:T(8,128)S(1)}, f32[2,48,16,128]{3,2,1,0:T(8,128)}, u32[]{:S(2)}) copy-start(f32[2,48,16,128]{3,2,1,0:T(8,128)} %stiff_in.3) | copy-start | bytes 2359300
  0.7 10.1 %copy-start.8 = (f32[2,128]{1,0:T(2,128)S(1)}, f32[2,128]{1,0:T(2,128)}, u32[]{:S(2)}) copy-start(f32[2,128]{1,0:T(2,128)} %cz_ref.5) | copy-start | bytes 3076
  0.7 10.1 %copy-start.7 = (f32[2,48]{1,0:T(2,128)S(1)}, f32[2,48]{1,0:T(2,128)}, u32[]{:S(2)}) copy-start(f32[2,48]{1,0:T(2,128)} %cx_ref.5) | copy-start | bytes 1156
  3.4 16.9 %all-to-all-start = ((f32[8,72,128]{2,1,0:T(8,128)}), f32[8,72,128]{2,1,0:T(8,128)S(1)}, u32[]{:S(2)}, u32[]{:S(2)}) async-start(f32[8,72,128]{2,1,0:T(8,128)} %pack.1), calls=%async_computation | async-start | bytes 589824 | tf_op jit(solution)/shard_map/all_to_all | solution.py:559
  15.7 0.7 copy-start.10
  20.4 4.7 %copy-start.11 = (f32[48,16,128]{2,1,0:T(8,128)S(1)}, f32[48,16,128]{2,1,0:T(8,128)}, u32[]{:S(2)}) copy-start(f32[48,16,128]{2,1,0:T(8,128)} %copy-done.10) | copy-start | bytes 1179652
  21.3 12.1 %all-to-all-start.1 = ((f32[8,64,128]{2,1,0:T(8,128)}), f32[8,64,128]{2,1,0:T(8,128)S(1)}, u32[]{:S(2)}, u32[]{:S(2)}) async-start(f32[8,64,128]{2,1,0:T(8,128)} %route.1), calls=%async_computation.1 | async-start | bytes 524288 | tf_op jit(solution)/shard_map/all_to_all | solution.py:602
  25.0 8.5 %copy-start.4 = (s32[2,3]{1,0:T(2,128)S(1)}, s32[2,3]{1,0:T(2,128)}, u32[]{:S(2)}) copy-start(s32[2,3]{1,0:T(2,128)} %low_ref.1) | copy-start | bytes 76
  25.0 8.5 %copy-start.5 = (s32[2,3]{1,0:T(2,128)S(1)}, s32[2,3]{1,0:T(2,128)}, u32[]{:S(2)}) copy-start(s32[2,3]{1,0:T(2,128)} %up_ref.1) | copy-start | bytes 76
  25.0 8.5 %copy-start.9 = (f32[2,16]{1,0:T(2,128)S(1)}, f32[2,16]{1,0:T(2,128)}, u32[]{:S(2)}) copy-start(f32[2,16]{1,0:T(2,128)} %cy_ref.1) | copy-start | bytes 388
  30.8 1.0 %copy-start.1 = (f32[2272,128]{1,0:T(8,128)}, f32[2272,128]{1,0:T(8,128)S(1)}, u32[]{:S(2)}) copy-start(f32[2272,128]{1,0:T(8,128)S(1)} %get-tuple-element.29.part_1) | copy-start | bytes 3489796
  33.5 1.3 %copy-start.2 = (f32[2272,128]{1,0:T(8,128)S(1)}, f32[2272,128]{1,0:T(8,128)}, u32[]{:S(2)}) copy-start(f32[2272,128]{1,0:T(8,128)} %copy-done.1) | copy-start | bytes 3489796
  38.9 2.9 %collective-permute-start = (f32[8,2,2,3,24,128]{5,4,3,2,1,0:T(8,128)S(1)}, f32[8,2,2,3,24,128]{5,4,3,2,1,0:T(8,128)S(1)}, u32[]{:S(2)}, u32[]{:S(2)}) collective-permute-start(f32[8,2,2,3,24,128]{5,4,3,2,1,0:T(8,128)S(1)} %get-tuple-element.33), channel_id=1, source_target_pairs={{0,8},{1,9},{2,10},{3,11},{4,12},{5,13},{6,14},{7,15},{8,0},{9,1},... | collective-permute-start | bytes 3538952 | tf_op jit(solution)/shard_map/ppermute | solution.py:658
  42.5 9.1 %collective-permute-start.1 = (f32[4,2,72,128]{3,2,1,0:T(8,128)S(1)}, f32[4,2,72,128]{3,2,1,0:T(8,128)S(1)}, u32[]{:S(2)}, u32[]{:S(2)}) collective-permute-start(f32[4,2,72,128]{3,2,1,0:T(8,128)S(1)} %get-tuple-element.35), channel_id=1, source_target_pairs={{0,1},{1,0},{2,3},{3,2},{4,5},{5,4},{6,7},{7,6},{8,9},{9,8},{10,11... | collective-permute-start | bytes 884744 | tf_op jit(solution)/shard_map/ppermute | solution.py:658
  44.0 8.8 %collective-permute-start.2 = (f32[4,2,72,128]{3,2,1,0:T(8,128)S(1)}, f32[4,2,72,128]{3,2,1,0:T(8,128)S(1)}, u32[]{:S(2)}, u32[]{:S(2)}) collective-permute-start(f32[4,2,72,128]{3,2,1,0:T(8,128)S(1)} %get-tuple-element.37), channel_id=1, source_target_pairs={{0,16},{1,17},{2,18},{3,19},{4,20},{5,21},{6,22},{7,23},{8,24},{9,... | collective-permute-start | bytes 884744 | tf_op jit(solution)/shard_map/ppermute | solution.py:658
  53.3 5.2 %collective-permute-start.3 = (f32[4,72,128]{2,1,0:T(8,128)S(1)}, f32[4,72,128]{2,1,0:T(8,128)S(1)}, u32[]{:S(2)}, u32[]{:S(2)}) collective-permute-start(f32[4,72,128]{2,1,0:T(8,128)S(1)} %get-tuple-element.39), channel_id=1, source_target_pairs={{0,16},{1,17},{2,18},{3,19},{4,20},{5,21},{6,22},{7,23},{8,24},{9,... | collective-permute-start | bytes 442376 | tf_op jit(solution)/shard_map/ppermute | solution.py:658
  54.8 5.1 %collective-permute-start.4 = (f32[4,72,128]{2,1,0:T(8,128)S(1)}, f32[4,72,128]{2,1,0:T(8,128)S(1)}, u32[]{:S(2)}, u32[]{:S(2)}) collective-permute-start(f32[4,72,128]{2,1,0:T(8,128)S(1)} %get-tuple-element.41), channel_id=1, source_target_pairs={{0,1},{1,0},{2,3},{3,2},{4,5},{5,4},{6,7},{7,6},{8,9},{9,8},{10,11... | collective-permute-start | bytes 442376 | tf_op jit(solution)/shard_map/ppermute | solution.py:658
  60.6 6.3 %collective-permute-start.5 = (f32[2,72,128]{2,1,0:T(8,128)S(1)}, f32[2,72,128]{2,1,0:T(8,128)S(1)}, u32[]{:S(2)}, u32[]{:S(2)}) collective-permute-start(f32[2,72,128]{2,1,0:T(8,128)S(1)} %get-tuple-element.43), channel_id=1, source_target_pairs={{0,2},{1,3},{2,4},{3,5},{4,6},{5,7},{6,0},{7,1},{8,10},{9,11},{10,... | collective-permute-start | bytes 221192 | tf_op jit(solution)/shard_map/ppermute | solution.py:658
  60.8 6.9 %collective-permute-start.6 = (f32[2,72,128]{2,1,0:T(8,128)S(1)}, f32[2,72,128]{2,1,0:T(8,128)S(1)}, u32[]{:S(2)}, u32[]{:S(2)}) collective-permute-start(f32[2,72,128]{2,1,0:T(8,128)S(1)} %get-tuple-element.44), channel_id=1, source_target_pairs={{0,4},{1,5},{2,6},{3,7},{4,0},{5,1},{6,2},{7,3},{8,12},{9,13},{10,... | collective-permute-start | bytes 221192 | tf_op jit(solution)/shard_map/ppermute | solution.py:658
  63.3 4.4 %collective-permute-start.7 = (f32[2,72,128]{2,1,0:T(8,128)S(1)}, f32[2,72,128]{2,1,0:T(8,128)S(1)}, u32[]{:S(2)}, u32[]{:S(2)}) collective-permute-start(f32[2,72,128]{2,1,0:T(8,128)S(1)} %get-tuple-element.45), channel_id=1, source_target_pairs={{0,6},{1,7},{2,0},{3,1},{4,2},{5,3},{6,4},{7,5},{8,14},{9,15},{10,... | collective-permute-start | bytes 221192 | tf_op jit(solution)/shard_map/ppermute | solution.py:658
  67.8 4.0 %collective-permute-start.10 = (f32[2,72,128]{2,1,0:T(8,128)S(1)}, f32[2,72,128]{2,1,0:T(8,128)S(1)}, u32[]{:S(2)}, u32[]{:S(2)}) collective-permute-start(f32[2,72,128]{2,1,0:T(8,128)S(1)} %shard_map.98), channel_id=1, source_target_pairs={{0,24},{1,25},{2,26},{3,27},{4,28},{5,29},{6,30},{7,31},{8,16},{9,... | collective-permute-start | bytes 221192 | tf_op jit(solution)/shard_map/ppermute | solution.py:658
  67.8 5.2 %collective-permute-start.9 = (f32[2,72,128]{2,1,0:T(8,128)S(1)}, f32[2,72,128]{2,1,0:T(8,128)S(1)}, u32[]{:S(2)}, u32[]{:S(2)}) collective-permute-start(f32[2,72,128]{2,1,0:T(8,128)S(1)} %shard_map.98), channel_id=1, source_target_pairs={{0,16},{1,17},{2,18},{3,19},{4,20},{5,21},{6,22},{7,23},{8,24},{9,... | collective-permute-start | bytes 221192 | tf_op jit(solution)/shard_map/ppermute | solution.py:658
  68.5 4.5 %collective-permute-start.8 = (f32[2,72,128]{2,1,0:T(8,128)S(1)}, f32[2,72,128]{2,1,0:T(8,128)S(1)}, u32[]{:S(2)}, u32[]{:S(2)}) collective-permute-start(f32[2,72,128]{2,1,0:T(8,128)S(1)} %shard_map.98), channel_id=1, source_target_pairs={{0,8},{1,9},{2,10},{3,11},{4,12},{5,13},{6,14},{7,15},{8,0},{9,1},... | collective-permute-start | bytes 221192 | tf_op jit(solution)/shard_map/ppermute | solution.py:658

commit v5 on v4

--- a/solution.py
+++ b/solution.py
@@ -23,6 +23,14 @@
 VMEM = pl.BlockSpec(memory_space=pltpu.VMEM)
 ANY = pl.BlockSpec(memory_space=pl.ANY)
 HBM = pl.BlockSpec(memory_space=pltpu.HBM)
+
+
+def place_of(fast):
+    if not fast:
+        return (jnp.int32(0),) * 4
+    group, dev = lax.axis_index("group"), lax.axis_index("dev")
+    halve = lambda v: lax.shift_right_logical(v, 1)
+    return group & 1, halve(group), dev & 1, halve(dev)
 
 
 def params(mib):
@@ -138,8 +146,8 @@
         for f in range(faces):
             cell = in_ref[e, rows + f : rows + f + 1, 0:1]
             number = cell[0, 0].astype(jnp.int32)
-            source = number // faces
-            start = (number % faces) * chunk
+            source = lax.shift_right_logical(number, 2)
+            start = (number & 3) * chunk
             if chunk % 8 == 0:
                 start = pl.multiple_of(start, 8)
             out_ref[e, f * chunk : (f + 1) * chunk] = in_ref[source, pl.ds(start, chunk)]
@@ -295,8 +303,8 @@
 
 
 def outer_kernel(
+    fast,
     per,
-    dest_ref,
     len_ref,
     low_ref,
     up_ref,
@@ -428,7 +436,7 @@
     pieces = keep_ref.shape[3]
     size = 3 * third_rows // 8
     tail = lax.broadcasted_iota(jnp.int32, (third_rows, 128), 1) >= 3 * LZ
-    even = dest_ref[0] == 0
+    even = place_of(fast)[0] == 0
     for pair in range(LX // per // 2):
         terms = []
         for number in (2 * pair, 2 * pair + 1):
@@ -457,24 +465,24 @@
         copy.wait()
 
 
-def core_kernel(dest_ref, keep_ref, got_ref, keep_y, send_y, keep_x, send_x):
-    y, x = dest_ref[2], dest_ref[1]
+def core_kernel(keep_ref, got_ref, keep_y, send_y, keep_x, send_x):
+    _, x, y, _ = place_of(True)
     keep_y[...] = keep_ref[:, y, 0] + got_ref[:, y, 0]
     send_y[...] = keep_ref[:, 1 - y, 0] + got_ref[:, 1 - y, 0]
     keep_x[...] = keep_ref[:, :, 1, x] + got_ref[:, :, 1, x]
     send_x[...] = keep_ref[:, :, 1, 1 - x] + got_ref[:, :, 1, 1 - x]
 
 
-def plane_kernel(dest_ref, keep_y, got_y, keep_x, got_x, keep_0, send_0, keep_1, send_1):
-    y, x = dest_ref[2], dest_ref[1]
+def plane_kernel(keep_y, got_y, keep_x, got_x, keep_0, send_0, keep_1, send_1):
+    _, x, y, _ = place_of(True)
     keep_0[...] = keep_y[:, x] + got_y[:, x]
     send_0[...] = keep_y[:, 1 - x] + got_y[:, 1 - x]
     keep_1[...] = keep_x[:, y] + got_x[:, y]
     send_1[...] = keep_x[:, 1 - y] + got_x[:, 1 - y]
 
 
-def line_kernel(dest_ref, keep_0, got_0, keep_1, got_1, *outs):
-    z = dest_ref[3]
+def line_kernel(keep_0, got_0, keep_1, got_1, *outs):
+    z = place_of(True)[3]
     count = len(outs)
     for k, out in enumerate(outs):
         at = lax.rem(z + k, count)
@@ -489,36 +497,37 @@
     refs[-1][...] = total * scale
 
 
-def unpack_kernel(per, dest_ref, own, got_c, got_x, got_xc, out_ref, pieces):
-    core, x = dest_ref[0], dest_ref[1]
-    pieces[core, x] = own[...]
-    pieces[1 - core, x] = got_c[...]
-    pieces[core, 1 - x] = got_x[...]
-    pieces[1 - core, 1 - x] = got_xc[...]
-    count = own.shape[1]
-    quarter = LY // 4
-    size = 3 * quarter // 8
-    lane = lax.broadcasted_iota(jnp.int32, (per, 128), 1) // LZ
-    for t in range(count):
-
-        def strip(r):
-            g, at = r // size, r % size
-            return pieces[g // 4, g % 2, g // 2 % 2, t, at * per : (at + 1) * per]
-
+def unpack_kernel(fast, per, own, got_c, got_x, got_xc, out_ref, lines):
+    core, x, _, _ = place_of(fast)
+    parts, count, size, _ = own.shape
+    runs = size // per
+    given = ((own, core, x), (got_c, 1 - core, x), (got_x, core, 1 - x), (got_xc, 1 - core, 1 - x))
+    for ref, c, u in given:
+        for p in range(parts):
+            for t in range(count):
+                for k in range(runs):
+                    at = ((c * parts + p) * 2 + u) * runs + k
+                    lines[at, t * per : (t + 1) * per] = ref[p, t, k * per : (k + 1) * per]
+    rows = count * per
+    lane = lax.broadcasted_iota(jnp.int32, (rows, 128), 1)
+    front = lane < 2 * LZ
+    even = (lane // LZ) % 2 == 0
+    tiles = LY // 4
+    groups = lines.shape[0] // 4
+    per_c = groups // 3
+    for g in range(groups):
+        v = [lines[4 * g + k] for k in range(4)]
+        a = [jnp.where(front, v[k], pltpu.roll(v[k + 2], 2 * LZ, 1)) for k in range(2)]
+        b = [jnp.where(front, pltpu.roll(v[k], 2 * LZ, 1), v[k + 2]) for k in range(2)]
+        turned = []
+        for p, q in (a, b):
+            turned.append(jnp.where(even, p, pltpu.roll(q, LZ, 1)))
+            turned.append(jnp.where(even, pltpu.roll(p, 128 - LZ, 1), q))
         for c in range(3):
-            for m4 in range(LY // 4):
-                tile = None
-                for k in range(4):
-                    m = 4 * m4 + k
-                    if m < 3 * quarter:
-                        value, lies = strip(m), c
-                    else:
-                        value, lies = strip(c * quarter + m - 3 * quarter), 3
-                    shift = ((k - lies) * LZ) % 128
-                    value = pltpu.roll(value, shift, 1) if shift else value
-                    tile = value if tile is None else jnp.where(lane == k, value, tile)
-                at = c * LY * LZ + m4 * 128
-                out_ref[t * per : (t + 1) * per, at : at + 128] = tile
+            at = (c * tiles + g) * 128
+            out_ref[:, at : at + 128] = turned[c]
+        at = (g // per_c * tiles + groups + g % per_c) * 128
+        out_ref[:, at : at + 128] = turned[3]
 
 
 def on_device(groups, devs, seed, stiff, lengths, low, up, coord_x, coord_y, coord_z):
@@ -530,13 +539,7 @@
     per = 4 if mine % 4 == 0 else mine
     pieces = mine // per
     size = 3 * LY // 4 // 8 * per
-    group_at = lax.axis_index("group")
-    dev_at = lax.axis_index("dev")
     fast = groups == 4 and devs % 2 == 0 and size % 8 == 0
-    if fast:
-        dest = jnp.stack([group_at % 2, group_at // 2, dev_at % 2, dev_at // 2]).astype(jnp.int32)
-    else:
-        dest = jnp.zeros((4,), jnp.int32)
     shape = lambda *dims: jax.ShapeDtypeStruct(dims, F32)
 
     packed = pl.pallas_call(
@@ -604,9 +607,9 @@
 
     half = shape(devs, 2, 2, pieces, size, 128)
     adjoint, keep, send = pl.pallas_call(
-        functools.partial(outer_kernel, per),
+        functools.partial(outer_kernel, fast, per),
         out_shape=(shape(slots, 3, nx, ny, nz), half, half),
-        in_specs=[SMEM] * 5 + [VMEM] * 5 + [HBM],
+        in_specs=[SMEM] * 4 + [VMEM] * 5 + [HBM],
         out_specs=(HBM, VMEM, VMEM),
         scratch_shapes=[
             pltpu.VMEM((faces, PLANES, ny, nz), F32),
@@ -615,11 +618,10 @@
             pltpu.VMEM((slots, LX * (ny + 1), 128), F32),
             pltpu.SemaphoreType.DMA((faces, 3)),
         ],
-        input_output_aliases={10: 0},
+        input_output_aliases={9: 0},
         compiler_params=params(12),
         name="outer",
     )(
-        dest,
         lengths,
         low,
         up,
@@ -638,7 +640,7 @@
         return pl.pallas_call(
             kernel,
             out_shape=outs,
-            in_specs=[SMEM if a is dest else VMEM for a in args],
+            in_specs=[VMEM] * len(args),
             out_specs=jax.tree.map(lambda _: VMEM, outs),
             scratch_shapes=scratch,
             compiler_params=params(8),
@@ -665,16 +667,16 @@
         view = (lines, 2, 2, 2, body, 128)
         part = shape(lines, 2, body, 128)
         keep_y, send_y, keep_x, send_x = small(
-            core_kernel, (part,) * 4, (dest, keep.reshape(view), got.reshape(view))
+            core_kernel, (part,) * 4, (keep.reshape(view), got.reshape(view))
         )
         got_y, got_x = move(send_y, flip_y), move(send_x, flip_x)
         part = shape(lines, body, 128)
         keep_0, send_0, keep_1, send_1 = small(
-            plane_kernel, (part,) * 4, (dest, keep_y, got_y, keep_x, got_x)
+            plane_kernel, (part,) * 4, (keep_y, got_y, keep_x, got_x)
         )
         got_0, got_1 = move(send_0, flip_x), move(send_1, flip_y)
         part = shape(2, body, 128)
-        sums = small(line_kernel, (part,) * lines, (dest, keep_0, got_0, keep_1, got_1))
+        sums = small(line_kernel, (part,) * lines, (keep_0, got_0, keep_1, got_1))
         terms = [sums[0]]
         for k in range(1, lines):
             terms.append(move(sums[k], lambda c, x, y, z, k=k: (c, x, y, (z + k) % lines)))
@@ -688,10 +690,10 @@
         owned = owned.reshape(2, 2, 2, pieces, size, 128)
         quarters = [owned[c, :, x] for x in range(2) for c in range(2)]
     lattice = small(
-        functools.partial(unpack_kernel, per),
+        functools.partial(unpack_kernel, fast, per),
         shape(mine, 3 * LY * LZ),
-        (dest, *quarters),
-        [pltpu.VMEM((2, 2, *piece), F32)],
+        tuple(quarters),
+        [pltpu.VMEM((3 * LY // 4, mine, 128), F32)],
     )
     return adjoint, lattice
 

time: 75.3 us -> 74.1 us (0.984)
  Pallas kernels: 22.1 us -> 19.2 us
  local copies, waits for them, and re-layouts: 3.04 us -> 4.03 us
  starting transfers between devices: 22 us -> 22.8 us
    pallas_call x6, Pallas kernels: 7.81 us -> 5.74 us  [the longest x1 4.14 us: on_device(): pl.pallas_call(functools.partial(outer_kernel, fast, per), out_shape=(sha...]
    unnamed x24, local copies, waits for them, and re-layouts: 3.04 us -> 4.03 us
    ppermute x11, starting transfers between devices: 11.1 us -> 11.9 us  [move(): return lax.ppermute(value, ('group', 'dev'), links)]
  transfers between devices with their start and end apart: 13 -> 13, of which waited for: 11 -> 12; matrix products, arithmetic and copies ran while one was open for 0% -> 0% of each run, Pallas kernels for 14% -> 13%
where the time goes in v5:
time: 74.1 us; the launch traced here: 73.8 us
  waiting for transfers between devices  27 us (36%)
  starting transfers between devices  22.8 us (31%)
  Pallas kernels  19.2 us (26%)
  local copies, waits for them, and re-layouts  4.03 us (5%)
  between operations  0.81 us (1%)
    ppermute x11, waiting for transfers between devices, move(): return lax.ppermute(value, ('group', 'dev'), links)  21.5 us
    ppermute x11, starting transfers between devices, move(): return lax.ppermute(value, ('group', 'dev'), links)  11.9 us
    pallas_call x2, Pallas kernels, one_block(): pl.pallas_call(functools.partial(block_kernel, b), out_shape=(shape(slots...  9.9 us
    all_to_all x1, starting transfers between devices, on_device(): spread = lax.all_to_all(packed, 'dev', 0, 0)  7.32 us
    all_to_all x1, waiting for transfers between devices, on_device(): spread = lax.all_to_all(packed, 'dev', 0, 0)  4.26 us
    pallas_call x1, Pallas kernels, on_device(): pl.pallas_call(functools.partial(outer_kernel, fast, per), out_shape=(sha...  4.14 us
    unnamed x24, local copies, waits for them, and re-layouts  4.03 us
    all_to_all x1, starting transfers between devices, on_device(): halos = lax.all_to_all(routed, 'dev', 0, 0)  3.62 us
  transfers between devices with their start and end apart: 13, of which 12 were waited for; matrix products, arithmetic and copies ran while one was open for 0% of the time, Pallas kernels for 13%

profile of v5, /device:TPU:0, one launch (start us, length us, event | category | flops | bytes accessed | tf_op | source)
XLA Modules:
  0.0 73.8 jit_solution(14354907250379733986)
XLA Ops:
  0.6 0.0 copy-start.6
  0.6 0.0 copy-start
  0.7 0.0 copy-start.3
  0.7 0.0 copy-start.8
  0.7 0.0 copy-start.7
  0.7 2.7 %pack.1 = f32[8,72,128]{2,1,0:T(8,128)} custom-call(s32[2]{0:T(128)} %len_ref.5, s32[2,3]{1,0:T(2,128)} %low_ref.1, s32[2,3]{1,0:T(2,128)} %up_ref.1, bf16[2,3,48,16,128]{4,3,2,1,0:T(8,128)(2,1)} %seed_in.5, f32[2,48,16,128]{3,2,1,0:T(8,128)} %stiff_in.3), custom_call_target="tpu_custom_call" | custom-call | tf_op jit(solution)/shard_map/pack/pallas_call | solution.py:545
  3.4 7.3 %all-to-all-start = ((f32[8,72,128]{2,1,0:T(8,128)}), f32[8,72,128]{2,1,0:T(8,128)S(1)}, u32[]{:S(2)}, u32[]{:S(2)}) async-start(f32[8,72,128]{2,1,0:T(8,128)} %pack.1), calls=%async_computation | async-start | bytes 589824 | tf_op jit(solution)/shard_map/all_to_all | solution.py:562
  10.8 0.0 copy-done.6
  10.8 0.0 copy-done
  10.8 0.0 copy-done.3
  10.8 0.0 copy-done.8
  10.8 0.0 copy-done.7
  10.8 4.5 %block_0.1 = (f32[2,3,48,16,128]{4,3,2,1,0:T(8,128)}, f32[2272,128]{1,0:T(8,128)S(1)}, f32[48,16,128]{2,1,0:T(8,128)S(1)}) custom-call(s32[2]{0:T(128)S(1)} %copy-done.6, bf16[2,3,48,16,128]{4,3,2,1,0:T(8,128)(2,1)S(1)} %copy-done, f32[2,48,16,128]{3,2,1,0:T(8,128)S(1)} %copy-done.3, f32[2,48]{1,0:T(2,128)S(1)} %copy-done.7, f32[2,128]{1,0:T(2,128)S(1)} %copy-done.8), custom_call_target="tpu_custom_call" | custom-call | flops 3000000000 | bytes 10000000 | tf_op jit(solution)/shard_map/block_0/pallas_call | solution.py:567
  15.4 0.0 copy-start.10
  15.4 0.7 copy-done.10
  16.1 4.3 %all-to-all-done.in_ref = f32[8,72,128]{2,1,0:T(8,128)S(1)} async-done(((f32[8,72,128]{2,1,0:T(8,128)}), f32[8,72,128]{2,1,0:T(8,128)S(1)}, u32[]{:S(2)}, u32[]{:S(2)}) %all-to-all-start) | async-done | bytes 294944 | tf_op jit(solution)/shard_map/all_to_all | solution.py:562
  20.4 0.8 %route.1 = f32[8,64,128]{2,1,0:T(8,128)} custom-call(f32[8,72,128]{2,1,0:T(8,128)S(1)} %all-to-all-done.in_ref), custom_call_target="tpu_custom_call" | custom-call | tf_op jit(solution)/shard_map/route/pallas_call | solution.py:596
  21.2 3.6 %all-to-all-start.1 = ((f32[8,64,128]{2,1,0:T(8,128)}), f32[8,64,128]{2,1,0:T(8,128)S(1)}, u32[]{:S(2)}, u32[]{:S(2)}) async-start(f32[8,64,128]{2,1,0:T(8,128)} %route.1), calls=%async_computation.1 | async-start | bytes 524288 | tf_op jit(solution)/shard_map/all_to_all | solution.py:605
  24.8 0.0 copy-start.11
  24.8 1.0 %copy-done.11 = f32[48,16,128]{2,1,0:T(8,128)S(1)} copy-done((f32[48,16,128]{2,1,0:T(8,128)S(1)}, f32[48,16,128]{2,1,0:T(8,128)}, u32[]{:S(2)}) %copy-start.11) | copy-done | bytes 393240
  25.8 0.0 copy-start.4
  25.8 0.0 copy-start.5
  25.8 0.0 copy-start.9
  25.8 5.4 %block_1.1 = (f32[2,3,48,16,128]{4,3,2,1,0:T(8,128)}, f32[2272,128]{1,0:T(8,128)S(1)}) custom-call(s32[2]{0:T(128)S(1)} %copy-done.6, bf16[2,3,48,16,128]{4,3,2,1,0:T(8,128)(2,1)S(1)} %copy-done, f32[48,16,128]{2,1,0:T(8,128)S(1)} %copy-done.11, f32[2,48]{1,0:T(2,128)S(1)} %copy-done.7, f32[2,128]{1,0:T(2,128)S(1)} %copy-done.8, ...), custom_call_target="tpu_custom_call", output_to_operand_aliasing={{0}: (5, {})} | custom-call | flops 3000000000 | bytes 10000000 | tf_op jit(solution)/shard_map/block_1/pallas_call | solution.py:567
  31.2 0.0 copy-start.1
  31.2 1.0 %copy-done.1 = f32[2272,128]{1,0:T(8,128)} copy-done((f32[2272,128]{1,0:T(8,128)}, f32[2272,128]{1,0:T(8,128)S(1)}, u32[]{:S(2)}) %copy-start.1) | copy-done | bytes 1163288
  32.2 1.2 %all-to-all-done.1.halo_ref = f32[8,64,128]{2,1,0:T(8,128)S(1)} async-done(((f32[8,64,128]{2,1,0:T(8,128)}), f32[8,64,128]{2,1,0:T(8,128)S(1)}, u32[]{:S(2)}, u32[]{:S(2)}) %all-to-all-start.1) | async-done | bytes 262176 | tf_op jit(solution)/shard_map/all_to_all | solution.py:605
  33.3 0.0 copy-done.4
  33.3 0.0 copy-done.5
  33.3 0.0 copy-done.9
  33.4 0.0 copy-start.2
  33.4 1.3 %copy-done.2 = f32[2272,128]{1,0:T(8,128)S(1)} copy-done((f32[2272,128]{1,0:T(8,128)S(1)}, f32[2272,128]{1,0:T(8,128)}, u32[]{:S(2)}) %copy-start.2) | copy-done | bytes 1163288
  34.6 4.1 %outer.1 = (f32[2,3,48,16,128]{4,3,2,1,0:T(8,128)}, f32[8,2,2,3,24,128]{5,4,3,2,1,0:T(8,128)S(1)}, f32[8,2,2,3,24,128]{5,4,3,2,1,0:T(8,128)S(1)}) custom-call(s32[2]{0:T(128)S(1)} %copy-done.6, s32[2,3]{1,0:T(2,128)S(1)} %copy-done.4, s32[2,3]{1,0:T(2,128)S(1)} %copy-done.5, f32[2,48]{1,0:T(2,128)S(1)} %copy-done.7, ...), custom_call_target="tpu_custom_call", output_to_operand_aliasing={{0}: (9, {})} | custom-call | tf_op jit(solution)/shard_map/outer/pallas_call | solution.py:609
  38.8 0.1 collective-permute-start
  38.8 2.8 %collective-permute-done = f32[8,2,2,3,24,128]{5,4,3,2,1,0:T(8,128)S(1)} collective-permute-done((f32[8,2,2,3,24,128]{5,4,3,2,1,0:T(8,128)S(1)}, f32[8,2,2,3,24,128]{5,4,3,2,1,0:T(8,128)S(1)}, u32[]{:S(2)}, u32[]{:S(2)}) %collective-permute-start) | collective-permute-done | bytes 1179680 | tf_op jit(solution)/shard_map/ppermute | solution.py:660
  41.7 0.1 shard_map.95
  41.8 1.4 %collective-permute-start.1 = (f32[4,2,72,128]{3,2,1,0:T(8,128)S(1)}, f32[4,2,72,128]{3,2,1,0:T(8,128)S(1)}, u32[]{:S(2)}, u32[]{:S(2)}) collective-permute-start(f32[4,2,72,128]{3,2,1,0:T(8,128)S(1)} %get-tuple-element.35), channel_id=1, source_target_pairs={{0,1},{1,0},{2,3},{3,2},{4,5},{5,4},{6,7},{7,6},{8,9},{9,8},{10,11... | collective-permute-start | bytes 884744 | tf_op jit(solution)/shard_map/ppermute | solution.py:660
  43.2 1.6 %collective-permute-start.2 = (f32[4,2,72,128]{3,2,1,0:T(8,128)S(1)}, f32[4,2,72,128]{3,2,1,0:T(8,128)S(1)}, u32[]{:S(2)}, u32[]{:S(2)}) collective-permute-start(f32[4,2,72,128]{3,2,1,0:T(8,128)S(1)} %get-tuple-element.37), channel_id=1, source_target_pairs={{0,16},{1,17},{2,18},{3,19},{4,20},{5,21},{6,22},{7,23},{8,24},{9,... | collective-permute-start | bytes 884744 | tf_op jit(solution)/shard_map/ppermute | solution.py:660
  44.8 6.2 %collective-permute-done.1.got_y = f32[4,2,72,128]{3,2,1,0:T(8,128)S(1)} collective-permute-done((f32[4,2,72,128]{3,2,1,0:T(8,128)S(1)}, f32[4,2,72,128]{3,2,1,0:T(8,128)S(1)}, u32[]{:S(2)}, u32[]{:S(2)}) %collective-permute-start.1) | collective-permute-done | bytes 294944 | tf_op jit(solution)/shard_map/ppermute | solution.py:660
  50.9 1.0 %collective-permute-done.2.got_x = f32[4,2,72,128]{3,2,1,0:T(8,128)S(1)} collective-permute-done((f32[4,2,72,128]{3,2,1,0:T(8,128)S(1)}, f32[4,2,72,128]{3,2,1,0:T(8,128)S(1)}, u32[]{:S(2)}, u32[]{:S(2)}) %collective-permute-start.2) | collective-permute-done | bytes 294944 | tf_op jit(solution)/shard_map/ppermute | solution.py:660
  52.0 0.1 shard_map.96
  52.0 1.6 %collective-permute-start.3 = (f32[4,72,128]{2,1,0:T(8,128)S(1)}, f32[4,72,128]{2,1,0:T(8,128)S(1)}, u32[]{:S(2)}, u32[]{:S(2)}) collective-permute-start(f32[4,72,128]{2,1,0:T(8,128)S(1)} %get-tuple-element.39), channel_id=1, source_target_pairs={{0,16},{1,17},{2,18},{3,19},{4,20},{5,21},{6,22},{7,23},{8,24},{9,... | collective-permute-start | bytes 442376 | tf_op jit(solution)/shard_map/ppermute | solution.py:660
  53.7 0.6 collective-permute-start.4
  54.3 3.0 %collective-permute-done.3.got_0 = f32[4,72,128]{2,1,0:T(8,128)S(1)} collective-permute-done((f32[4,72,128]{2,1,0:T(8,128)S(1)}, f32[4,72,128]{2,1,0:T(8,128)S(1)}, u32[]{:S(2)}, u32[]{:S(2)}) %collective-permute-start.3) | collective-permute-done | bytes 147488 | tf_op jit(solution)/shard_map/ppermute | solution.py:660
  57.2 1.6 %collective-permute-done.4.got_1 = f32[4,72,128]{2,1,0:T(8,128)S(1)} collective-permute-done((f32[4,72,128]{2,1,0:T(8,128)S(1)}, f32[4,72,128]{2,1,0:T(8,128)S(1)}, u32[]{:S(2)}, u32[]{:S(2)}) %collective-permute-start.4) | collective-permute-done | bytes 147488 | tf_op jit(solution)/shard_map/ppermute | solution.py:660
  58.9 1.0 %collective-permute-start.5 = (f32[2,72,128]{2,1,0:T(8,128)S(1)}, f32[2,72,128]{2,1,0:T(8,128)S(1)}, u32[]{:S(2)}, u32[]{:S(2)}) collective-permute-start(f32[2,72,128]{2,1,0:T(8,128)S(1)} %get-tuple-element.43), channel_id=1, source_target_pairs={{0,2},{1,3},{2,4},{3,5},{4,6},{5,7},{6,0},{7,1},{8,10},{9,11},{10,... | collective-permute-start | bytes 221192 | tf_op jit(solution)/shard_map/ppermute | solution.py:660
  59.8 2.3 %collective-permute-start.6 = (f32[2,72,128]{2,1,0:T(8,128)S(1)}, f32[2,72,128]{2,1,0:T(8,128)S(1)}, u32[]{:S(2)}, u32[]{:S(2)}) collective-permute-start(f32[2,72,128]{2,1,0:T(8,128)S(1)} %get-tuple-element.44), channel_id=1, source_target_pairs={{0,4},{1,5},{2,6},{3,7},{4,0},{5,1},{6,2},{7,3},{8,12},{9,13},{10,... | collective-permute-start | bytes 221192 | tf_op jit(solution)/shard_map/ppermute | solution.py:660
  62.1 1.4 %collective-permute-start.7 = (f32[2,72,128]{2,1,0:T(8,128)S(1)}, f32[2,72,128]{2,1,0:T(8,128)S(1)}, u32[]{:S(2)}, u32[]{:S(2)}) collective-permute-start(f32[2,72,128]{2,1,0:T(8,128)S(1)} %get-tuple-element.45), channel_id=1, source_target_pairs={{0,6},{1,7},{2,0},{3,1},{4,2},{5,3},{6,4},{7,5},{8,14},{9,15},{10,... | collective-permute-start | bytes 221192 | tf_op jit(solution)/shard_map/ppermute | solution.py:660
  63.6 1.6 %collective-permute-done.5.refs_1_ = f32[2,72,128]{2,1,0:T(8,128)S(1)} collective-permute-done((f32[2,72,128]{2,1,0:T(8,128)S(1)}, f32[2,72,128]{2,1,0:T(8,128)S(1)}, u32[]{:S(2)}, u32[]{:S(2)}) %collective-permute-start.5) | collective-permute-done | bytes 73760 | tf_op jit(solution)/shard_map/ppermute | solution.py:660
  65.1 1.6 %collective-permute-done.6.refs_2_ = f32[2,72,128]{2,1,0:T(8,128)S(1)} collective-permute-done((f32[2,72,128]{2,1,0:T(8,128)S(1)}, f32[2,72,128]{2,1,0:T(8,128)S(1)}, u32[]{:S(2)}, u32[]{:S(2)}) %collective-permute-start.6) | collective-permute-done | bytes 73760 | tf_op jit(solution)/shard_map/ppermute | solution.py:660
  66.7 0.4 collective-permute-done.7.refs_3_
  67.2 0.1 collective-permute-start.10
  67.3 0.4 collective-permute-start.9
  67.7 1.5 %collective-permute-start.8 = (f32[2,72,128]{2,1,0:T(8,128)S(1)}, f32[2,72,128]{2,1,0:T(8,128)S(1)}, u32[]{:S(2)}, u32[]{:S(2)}) collective-permute-start(f32[2,72,128]{2,1,0:T(8,128)S(1)} %shard_map.98), channel_id=1, source_target_pairs={{0,8},{1,9},{2,10},{3,11},{4,12},{5,13},{6,14},{7,15},{8,0},{9,1},... | collective-permute-start | bytes 221192 | tf_op jit(solution)/shard_map/ppermute | solution.py:660
  69.1 2.0 %collective-permute-done.10 = f32[2,72,128]{2,1,0:T(8,128)S(1)} collective-permute-done((f32[2,72,128]{2,1,0:T(8,128)S(1)}, f32[2,72,128]{2,1,0:T(8,128)S(1)}, u32[]{:S(2)}, u32[]{:S(2)}) %collective-permute-start.10) | collective-permute-done | bytes 73760 | tf_op jit(solution)/shard_map/ppermute | solution.py:660
  71.2 1.3 %collective-permute-done.9 = f32[2,72,128]{2,1,0:T(8,128)S(1)} collective-permute-done((f32[2,72,128]{2,1,0:T(8,128)S(1)}, f32[2,72,128]{2,1,0:T(8,128)S(1)}, u32[]{:S(2)}, u32[]{:S(2)}) %collective-permute-start.9) | collective-permute-done | bytes 73760 | tf_op jit(solution)/shard_map/ppermute | solution.py:660
  72.5 0.0 collective-permute-done.8
  72.5 1.3 %shard_map.99 = f32[12,6144]{1,0:T(8,128)} custom-call(f32[2,3,24,128]{3,2,1,0:T(8,128)S(1)} %bitcast.8, f32[2,3,24,128]{3,2,1,0:T(8,128)S(1)} %bitcast.11, f32[2,3,24,128]{3,2,1,0:T(8,128)S(1)} %bitcast.10, f32[2,3,24,128]{3,2,1,0:T(8,128)S(1)} %bitcast.9), custom_call_target="tpu_custom_call" | custom-call | tf_op jit(solution)/shard_map/pallas_call | solution.py:640
  (2 shorter events, 0.1 us)
Async XLA Ops:
  0.6 10.1 %copy-start.6 = (s32[2]{0:T(128)S(1)}, s32[2]{0:T(128)}, u32[]{:S(2)}) copy-start(s32[2]{0:T(128)} %len_ref.5) | copy-start | bytes 28
  0.6 10.1 %copy-start = (bf16[2,3,48,16,128]{4,3,2,1,0:T(8,128)(2,1)S(1)}, bf16[2,3,48,16,128]{4,3,2,1,0:T(8,128)(2,1)}, u32[]{:S(2)}) copy-start(bf16[2,3,48,16,128]{4,3,2,1,0:T(8,128)(2,1)} %seed_in.5) | copy-start | bytes 3538948
  0.7 10.1 %copy-start.3 = (f32[2,48,16,128]{3,2,1,0:T(8,128)S(1)}, f32[2,48,16,128]{3,2,1,0:T(8,128)}, u32[]{:S(2)}) copy-start(f32[2,48,16,128]{3,2,1,0:T(8,128)} %stiff_in.3) | copy-start | bytes 2359300
  0.7 10.1 %copy-start.8 = (f32[2,128]{1,0:T(2,128)S(1)}, f32[2,128]{1,0:T(2,128)}, u32[]{:S(2)}) copy-start(f32[2,128]{1,0:T(2,128)} %cz_ref.5) | copy-start | bytes 3076
  0.7 10.1 %copy-start.7 = (f32[2,48]{1,0:T(2,128)S(1)}, f32[2,48]{1,0:T(2,128)}, u32[]{:S(2)}) copy-start(f32[2,48]{1,0:T(2,128)} %cx_ref.5) | copy-start | bytes 1156
  3.4 16.9 %all-to-all-start = ((f32[8,72,128]{2,1,0:T(8,128)}), f32[8,72,128]{2,1,0:T(8,128)S(1)}, u32[]{:S(2)}, u32[]{:S(2)}) async-start(f32[8,72,128]{2,1,0:T(8,128)} %pack.1), calls=%async_computation | async-start | bytes 589824 | tf_op jit(solution)/shard_map/all_to_all | solution.py:562
  15.4 0.7 %copy-start.10 = (f32[48,16,128]{2,1,0:T(8,128)}, f32[48,16,128]{2,1,0:T(8,128)S(1)}, u32[]{:S(2)}) copy-start(f32[48,16,128]{2,1,0:T(8,128)S(1)} %get-tuple-element.27.stiff_in) | copy-start | bytes 1179652
  21.2 12.1 %all-to-all-start.1 = ((f32[8,64,128]{2,1,0:T(8,128)}), f32[8,64,128]{2,1,0:T(8,128)S(1)}, u32[]{:S(2)}, u32[]{:S(2)}) async-start(f32[8,64,128]{2,1,0:T(8,128)} %route.1), calls=%async_computation.1 | async-start | bytes 524288 | tf_op jit(solution)/shard_map/all_to_all | solution.py:605
  24.8 1.0 %copy-start.11 = (f32[48,16,128]{2,1,0:T(8,128)S(1)}, f32[48,16,128]{2,1,0:T(8,128)}, u32[]{:S(2)}) copy-start(f32[48,16,128]{2,1,0:T(8,128)} %copy-done.10) | copy-start | bytes 1179652
  25.8 7.5 %copy-start.4 = (s32[2,3]{1,0:T(2,128)S(1)}, s32[2,3]{1,0:T(2,128)}, u32[]{:S(2)}) copy-start(s32[2,3]{1,0:T(2,128)} %low_ref.1) | copy-start | bytes 76
  25.8 7.5 %copy-start.5 = (s32[2,3]{1,0:T(2,128)S(1)}, s32[2,3]{1,0:T(2,128)}, u32[]{:S(2)}) copy-start(s32[2,3]{1,0:T(2,128)} %up_ref.1) | copy-start | bytes 76
  25.8 7.5 %copy-start.9 = (f32[2,16]{1,0:T(2,128)S(1)}, f32[2,16]{1,0:T(2,128)}, u32[]{:S(2)}) copy-start(f32[2,16]{1,0:T(2,128)} %cy_ref.1) | copy-start | bytes 388
  31.2 1.0 %copy-start.1 = (f32[2272,128]{1,0:T(8,128)}, f32[2272,128]{1,0:T(8,128)S(1)}, u32[]{:S(2)}) copy-start(f32[2272,128]{1,0:T(8,128)S(1)} %get-tuple-element.29.part_1) | copy-start | bytes 3489796
  33.4 1.3 %copy-start.2 = (f32[2272,128]{1,0:T(8,128)S(1)}, f32[2272,128]{1,0:T(8,128)}, u32[]{:S(2)}) copy-start(f32[2272,128]{1,0:T(8,128)} %copy-done.1) | copy-start | bytes 3489796
  38.8 2.9 %collective-permute-start = (f32[8,2,2,3,24,128]{5,4,3,2,1,0:T(8,128)S(1)}, f32[8,2,2,3,24,128]{5,4,3,2,1,0:T(8,128)S(1)}, u32[]{:S(2)}, u32[]{:S(2)}) collective-permute-start(f32[8,2,2,3,24,128]{5,4,3,2,1,0:T(8,128)S(1)} %get-tuple-element.33), channel_id=1, source_target_pairs={{0,8},{1,9},{2,10},{3,11},{4,12},{5,13},{6,14},{7,15},{8,0},{9,1},... | collective-permute-start | bytes 3538952 | tf_op jit(solution)/shard_map/ppermute | solution.py:660
  41.8 9.1 %collective-permute-start.1 = (f32[4,2,72,128]{3,2,1,0:T(8,128)S(1)}, f32[4,2,72,128]{3,2,1,0:T(8,128)S(1)}, u32[]{:S(2)}, u32[]{:S(2)}) collective-permute-start(f32[4,2,72,128]{3,2,1,0:T(8,128)S(1)} %get-tuple-element.35), channel_id=1, source_target_pairs={{0,1},{1,0},{2,3},{3,2},{4,5},{5,4},{6,7},{7,6},{8,9},{9,8},{10,11... | collective-permute-start | bytes 884744 | tf_op jit(solution)/shard_map/ppermute | solution.py:660
  43.2 8.8 %collective-permute-start.2 = (f32[4,2,72,128]{3,2,1,0:T(8,128)S(1)}, f32[4,2,72,128]{3,2,1,0:T(8,128)S(1)}, u32[]{:S(2)}, u32[]{:S(2)}) collective-permute-start(f32[4,2,72,128]{3,2,1,0:T(8,128)S(1)} %get-tuple-element.37), channel_id=1, source_target_pairs={{0,16},{1,17},{2,18},{3,19},{4,20},{5,21},{6,22},{7,23},{8,24},{9,... | collective-permute-start | bytes 884744 | tf_op jit(solution)/shard_map/ppermute | solution.py:660
  52.0 5.2 %collective-permute-start.3 = (f32[4,72,128]{2,1,0:T(8,128)S(1)}, f32[4,72,128]{2,1,0:T(8,128)S(1)}, u32[]{:S(2)}, u32[]{:S(2)}) collective-permute-start(f32[4,72,128]{2,1,0:T(8,128)S(1)} %get-tuple-element.39), channel_id=1, source_target_pairs={{0,16},{1,17},{2,18},{3,19},{4,20},{5,21},{6,22},{7,23},{8,24},{9,... | collective-permute-start | bytes 442376 | tf_op jit(solution)/shard_map/ppermute | solution.py:660
  53.7 5.1 %collective-permute-start.4 = (f32[4,72,128]{2,1,0:T(8,128)S(1)}, f32[4,72,128]{2,1,0:T(8,128)S(1)}, u32[]{:S(2)}, u32[]{:S(2)}) collective-permute-start(f32[4,72,128]{2,1,0:T(8,128)S(1)} %get-tuple-element.41), channel_id=1, source_target_pairs={{0,1},{1,0},{2,3},{3,2},{4,5},{5,4},{6,7},{7,6},{8,9},{9,8},{10,11... | collective-permute-start | bytes 442376 | tf_op jit(solution)/shard_map/ppermute | solution.py:660
  58.9 6.3 %collective-permute-start.5 = (f32[2,72,128]{2,1,0:T(8,128)S(1)}, f32[2,72,128]{2,1,0:T(8,128)S(1)}, u32[]{:S(2)}, u32[]{:S(2)}) collective-permute-start(f32[2,72,128]{2,1,0:T(8,128)S(1)} %get-tuple-element.43), channel_id=1, source_target_pairs={{0,2},{1,3},{2,4},{3,5},{4,6},{5,7},{6,0},{7,1},{8,10},{9,11},{10,... | collective-permute-start | bytes 221192 | tf_op jit(solution)/shard_map/ppermute | solution.py:660
  59.8 6.9 %collective-permute-start.6 = (f32[2,72,128]{2,1,0:T(8,128)S(1)}, f32[2,72,128]{2,1,0:T(8,128)S(1)}, u32[]{:S(2)}, u32[]{:S(2)}) collective-permute-start(f32[2,72,128]{2,1,0:T(8,128)S(1)} %get-tuple-element.44), channel_id=1, source_target_pairs={{0,4},{1,5},{2,6},{3,7},{4,0},{5,1},{6,2},{7,3},{8,12},{9,13},{10,... | collective-permute-start | bytes 221192 | tf_op jit(solution)/shard_map/ppermute | solution.py:660
  62.1 5.0 %collective-permute-start.7 = (f32[2,72,128]{2,1,0:T(8,128)S(1)}, f32[2,72,128]{2,1,0:T(8,128)S(1)}, u32[]{:S(2)}, u32[]{:S(2)}) collective-permute-start(f32[2,72,128]{2,1,0:T(8,128)S(1)} %get-tuple-element.45), channel_id=1, source_target_pairs={{0,6},{1,7},{2,0},{3,1},{4,2},{5,3},{6,4},{7,5},{8,14},{9,15},{10,... | collective-permute-start | bytes 221192 | tf_op jit(solution)/shard_map/ppermute | solution.py:660
  67.2 4.0 %collective-permute-start.10 = (f32[2,72,128]{2,1,0:T(8,128)S(1)}, f32[2,72,128]{2,1,0:T(8,128)S(1)}, u32[]{:S(2)}, u32[]{:S(2)}) collective-permute-start(f32[2,72,128]{2,1,0:T(8,128)S(1)} %shard_map.98), channel_id=1, source_target_pairs={{0,24},{1,25},{2,26},{3,27},{4,28},{5,29},{6,30},{7,31},{8,16},{9,... | collective-permute-start | bytes 221192 | tf_op jit(solution)/shard_map/ppermute | solution.py:660
  67.3 5.2 %collective-permute-start.9 = (f32[2,72,128]{2,1,0:T(8,128)S(1)}, f32[2,72,128]{2,1,0:T(8,128)S(1)}, u32[]{:S(2)}, u32[]{:S(2)}) collective-permute-start(f32[2,72,128]{2,1,0:T(8,128)S(1)} %shard_map.98), channel_id=1, source_target_pairs={{0,16},{1,17},{2,18},{3,19},{4,20},{5,21},{6,22},{7,23},{8,24},{9,... | collective-permute-start | bytes 221192 | tf_op jit(solution)/shard_map/ppermute | solution.py:660
  67.7 4.8 %collective-permute-start.8 = (f32[2,72,128]{2,1,0:T(8,128)S(1)}, f32[2,72,128]{2,1,0:T(8,128)S(1)}, u32[]{:S(2)}, u32[]{:S(2)}) collective-permute-start(f32[2,72,128]{2,1,0:T(8,128)S(1)} %shard_map.98), channel_id=1, source_target_pairs={{0,8},{1,9},{2,10},{3,11},{4,12},{5,13},{6,14},{7,15},{8,0},{9,1},... | collective-permute-start | bytes 221192 | tf_op jit(solution)/shard_map/ppermute | solution.py:660

commit v6 on v5

--- a/solution.py
+++ b/solution.py
@@ -91,21 +91,20 @@
         small[k].start()
     copies = {}
 
-    def fetch(s, side):
-        f = 2 * s + side
-        start = [0, 0] if side == 0 else [len_ref[s] - 3, len_ref[s] - 2]
-        copies[f] = (
-            pltpu.make_async_copy(stiff_in.at[s, pl.ds(start[0], 3)], stiff_ref.at[f], sems.at[1, f]),
-            pltpu.make_async_copy(seed_in.at[s, :, pl.ds(start[1], 2)], seed_ref.at[f], sems.at[2, f]),
-        )
-        for copy in copies[f]:
-            copy.start()
+    base = nx // 2 - 3
 
     for s in range(slots):
-        fetch(s, 0)
+        for side in range(2):
+            f = 2 * s + side
+            at = pl.ds(0, 3) if side == 0 else pl.ds(base, nx - base)
+            to = pl.ds(0, 3 if side == 0 else nx - base)
+            copies[f] = (
+                pltpu.make_async_copy(stiff_in.at[s, at], stiff_ref.at[f, to], sems.at[1, f]),
+                pltpu.make_async_copy(seed_in.at[s, :, at], seed_ref.at[f, :, to], sems.at[2, f]),
+            )
+            for copy in copies[f]:
+                copy.start()
     small[0].wait()
-    for s in range(slots):
-        fetch(s, 1)
     small[1].wait()
     small[2].wait()
     wanted = []
@@ -121,15 +120,16 @@
         side = f % 2
         for copy in copies[f]:
             copy.wait()
-        stiff = [stiff_ref[f, k if side == 0 else 2 - k] for k in range(3)]
+        at = [k if side == 0 else len_ref[f // 2] - 1 - k - base for k in range(3)]
+        stiff = [stiff_ref[f, i] for i in at]
         parts = [plane_parts(v) for v in stiff]
         inner = parts[0][1] + parts[1][0]
         next_near = parts[1][1] + parts[0][0] + parts[2][0]
         scale = 1.0 / (DOMINANCE * next_near)
         planes = [stiff[0], inner]
-        planes += [seed_ref[f, c, side].astype(F32) for c in range(3)]
+        planes += [seed_ref[f, c, at[0]].astype(F32) for c in range(3)]
         for c in range(3):
-            planes.append(plane_parts(seed_ref[f, c, 1 - side].astype(F32) * scale)[0])
+            planes.append(plane_parts(seed_ref[f, c, at[1]].astype(F32) * scale)[0])
         for k, plane in enumerate(planes):
             packet[f, k * ny : (k + 1) * ny] = plane
     for j in range(devs):
@@ -177,9 +177,9 @@
 
 def block_kernel(b, len_ref, seed_in, stiff_in, cx_ref, cz_ref, *refs):
     s_ext, w_ext, v_ext, fac_ref, mul_ref, adj, seeds, zdone, sems = refs[-9:]
-    adj_out, part_ref, *passed = refs[:3] if b == 0 else refs[1:3]
+    adj_out, part_ref, edge_out, *passed = refs[:4] if b == 0 else refs[1:4]
     nx, ny, nz = fac_ref.shape
-    edge_ref = Planes(part_ref, LX * (ny + 1), ny)
+    edge_ref = Planes(edge_out, 0, ny)
     last = 8 + ny
     length = len_ref[b]
     loads = (
@@ -302,26 +302,21 @@
         ahead.wait()
 
 
-def outer_kernel(
-    fast,
-    per,
+def ends_kernel(
     len_ref,
     low_ref,
     up_ref,
     cx_ref,
     halo_ref,
-    part_0,
-    part_1,
-    cy_ref,
+    edge_0,
+    edge_1,
     cz_ref,
     adj_in,
     adj_out,
-    keep_ref,
-    send_ref,
+    xdone,
     pack,
     ends,
     zdone,
-    xdone,
     sems,
 ):
     del adj_in
@@ -362,7 +357,7 @@
     copies = []
     for f in range(faces):
         b, side = f // 2, f % 2
-        edge = Planes((part_0, part_1)[b], LX * pitch, ny)
+        edge = Planes((edge_0, edge_1)[b], 0, ny)
         stiff, inside = edge[side, 0], edge[side, 1]
         beside = plane_parts(stiff)[0]
         there = 1.0 / (DOMINANCE * (pack[f, 1] + beside))
@@ -423,6 +418,13 @@
             for k in range(2):
                 xdone[b, pl.ds(y + k, LX, stride=pitch), :] = done[:, 128 * k : 128 * (k + 1)]
 
+    for copy in copies:
+        copy.wait()
+
+
+def close_kernel(fast, per, part_0, part_1, xdone, cy_ref, keep_ref, send_ref):
+    slots, ny = cy_ref.shape
+    pitch = ny + 1
     depth = per * slots * ny
     row = lax.broadcasted_iota(jnp.int32, (LY * per, depth), 0).astype(F32)
     lane = lax.broadcasted_iota(jnp.int32, (LY * per, depth), 1).astype(F32)
@@ -461,8 +463,6 @@
                 second = dense[(g + 4) * size : (g + 5) * size]
                 keep_ref[d, g // 2, g % 2, t] = jnp.where(even, first, second)
                 send_ref[d, g // 2, g % 2, t] = jnp.where(even, second, first)
-    for copy in copies:
-        copy.wait()
 
 
 def core_kernel(keep_ref, got_ref, keep_y, send_y, keep_x, send_x):
@@ -551,8 +551,8 @@
             pltpu.SMEM((slots,), jnp.int32),
             pltpu.SMEM((slots, 3), jnp.int32),
             pltpu.SMEM((slots, 3), jnp.int32),
-            pltpu.VMEM((faces, 3, 2, ny, nz), seed.dtype),
-            pltpu.VMEM((faces, 3, ny, nz), F32),
+            pltpu.VMEM((faces, 3, nx - nx // 2 + 3, ny, nz), seed.dtype),
+            pltpu.VMEM((faces, nx - nx // 2 + 3, ny, nz), F32),
             pltpu.VMEM((faces, PLANES * ny, nz), F32),
             pltpu.SemaphoreType.DMA((3, faces)),
         ],
@@ -568,11 +568,12 @@
             functools.partial(block_kernel, b),
             out_shape=(
                 shape(slots, 3, nx, ny, nz),
-                shape(LX * (ny + 1) + 2 * EDGES * ny, 128),
+                shape(LX * (ny + 1), 128),
+                shape(2 * EDGES * ny, 128),
                 *([shape(nx, ny, nz)] if b == 0 else []),
             ),
             in_specs=[SMEM, ANY, ANY, VMEM, VMEM] + [HBM] * len(given),
-            out_specs=(HBM, VMEM, VMEM) if b == 0 else (HBM, VMEM),
+            out_specs=(HBM, VMEM, VMEM, VMEM) if b == 0 else (HBM, VMEM, VMEM),
             scratch_shapes=[
                 pltpu.VMEM(ext, F32),
                 pltpu.VMEM((3, *ext), F32),
@@ -592,7 +593,7 @@
             name=f"block_{b}",
         )(lengths, seed, stiff, coord_x, coord_z, *given)
 
-    early, part_0, stiff_1 = one_block(0, stiff)
+    early, part_0, edge_0, stiff_1 = one_block(0, stiff)
     routed = pl.pallas_call(
         route_kernel,
         out_shape=shape(devs, rows, nz),
@@ -603,36 +604,33 @@
     )(spread)
     early, routed = lax.optimization_barrier((early, routed))
     halos = lax.all_to_all(routed, "dev", 0, 0)
-    early, part_1 = one_block(1, stiff_1, early)
+    early, part_1, edge_1 = one_block(1, stiff_1, early)
 
     half = shape(devs, 2, 2, pieces, size, 128)
-    adjoint, keep, send = pl.pallas_call(
-        functools.partial(outer_kernel, fast, per),
-        out_shape=(shape(slots, 3, nx, ny, nz), half, half),
-        in_specs=[SMEM] * 4 + [VMEM] * 5 + [HBM],
-        out_specs=(HBM, VMEM, VMEM),
+    pitch = ny + 1
+    adjoint, last = pl.pallas_call(
+        ends_kernel,
+        out_shape=(shape(slots, 3, nx, ny, nz), shape(slots, LX * pitch, 128)),
+        in_specs=[SMEM] * 4 + [VMEM] * 4 + [HBM],
+        out_specs=(HBM, VMEM),
         scratch_shapes=[
             pltpu.VMEM((faces, PLANES, ny, nz), F32),
             pltpu.VMEM((slots, 3, 2 * ENDS, ny, nz), F32),
-            pltpu.VMEM((8 * (ny + 1), 128), F32),
-            pltpu.VMEM((slots, LX * (ny + 1), 128), F32),
+            pltpu.VMEM((8 * pitch, 128), F32),
             pltpu.SemaphoreType.DMA((faces, 3)),
         ],
-        input_output_aliases={9: 0},
+        input_output_aliases={8: 0},
+        compiler_params=params(8),
+        name="ends",
+    )(lengths, low, up, coord_x, halos, edge_0, edge_1, coord_z, early)
+    keep, send = pl.pallas_call(
+        functools.partial(close_kernel, fast, per),
+        out_shape=(half, half),
+        in_specs=[VMEM] * 4,
+        out_specs=(VMEM, VMEM),
         compiler_params=params(12),
-        name="outer",
-    )(
-        lengths,
-        low,
-        up,
-        coord_x,
-        halos,
-        part_0,
-        part_1,
-        coord_y,
-        coord_z,
-        early,
-    )
+        name="close",
+    )(part_0, part_1, last, coord_y)
 
     scale = math.sqrt(LX * LY * LZ / (groups * devs * slots * nx * ny * nz))
 

time: 74.1 us -> 72.8 us (0.982)
  waiting for transfers between devices: 27 us -> 26.1 us
    pallas_call x2, Pallas kernels: 9.9 us -> 10.8 us  [one_block(): pl.pallas_call(functools.partial(block_kernel, b), out_shape=(shape(slots...]
    all_to_all x1, waiting for transfers between devices: 4.26 us -> 3.39 us  [on_device(): spread = lax.all_to_all(packed, 'dev', 0, 0)]
    pallas_call x1 -> x2, Pallas kernels: 4.14 us -> 3.74 us  [the longest x1 2.29 us: on_device(): pl.pallas_call(ends_kernel, out_shape=(shape(slots, 3, nx, ny, nz), shape...]
  transfers between devices with their start and end apart: 13 -> 13, of which waited for: 12 -> 12; matrix products, arithmetic and copies ran while one was open for 0% -> 0% of each run, Pallas kernels for 13% -> 15%
where the time goes in v6:
time: 72.8 us; the launch traced here: 72.5 us
  waiting for transfers between devices  26.1 us (36%)
  starting transfers between devices  22.6 us (31%)
  Pallas kernels  19.5 us (27%)
  local copies, waits for them, and re-layouts  3.46 us (5%)
  between operations  0.81 us (1%)
    ppermute x11, waiting for transfers between devices, move(): return lax.ppermute(value, ('group', 'dev'), links)  21.3 us
    ppermute x11, starting transfers between devices, move(): return lax.ppermute(value, ('group', 'dev'), links)  11.7 us
    pallas_call x2, Pallas kernels, one_block(): pl.pallas_call(functools.partial(block_kernel, b), out_shape=(shape(slots...  10.8 us
    all_to_all x1, starting transfers between devices, on_device(): spread = lax.all_to_all(packed, 'dev', 0, 0)  7.32 us
    all_to_all x1, starting transfers between devices, on_device(): halos = lax.all_to_all(routed, 'dev', 0, 0)  3.62 us
    unnamed x24, local copies, waits for them, and re-layouts  3.46 us
    all_to_all x1, waiting for transfers between devices, on_device(): spread = lax.all_to_all(packed, 'dev', 0, 0)  3.39 us
    pallas_call x1, Pallas kernels, on_device(): pl.pallas_call(functools.partial(pack_kernel, devs, slots, nx, ny, nz), o...  2.53 us
  transfers between devices with their start and end apart: 13, of which 12 were waited for; matrix products, arithmetic and copies ran while one was open for 0% of the time, Pallas kernels for 15%

profile of v6, /device:TPU:0, one launch (start us, length us, event | category | flops | bytes accessed | tf_op | source)
XLA Modules:
  0.0 72.5 jit_solution(12433366100263730529)
XLA Ops:
  0.6 0.0 copy-start.6
  0.6 0.0 copy-start
  0.7 0.0 copy-start.1
  0.7 0.0 copy-start.8
  0.7 0.0 copy-start.7
  0.7 2.5 %pack.1 = f32[8,72,128]{2,1,0:T(8,128)} custom-call(s32[2]{0:T(128)} %len_ref.5, s32[2,3]{1,0:T(2,128)} %low_ref.1, s32[2,3]{1,0:T(2,128)} %up_ref.1, bf16[2,3,48,16,128]{4,3,2,1,0:T(8,128)(2,1)} %seed_in.5, f32[2,48,16,128]{3,2,1,0:T(8,128)} %stiff_in.3), custom_call_target="tpu_custom_call" | custom-call | tf_op jit(solution)/shard_map/pack/pallas_call | solution.py:545
  3.2 7.3 %all-to-all-start = ((f32[8,72,128]{2,1,0:T(8,128)}), f32[8,72,128]{2,1,0:T(8,128)S(1)}, u32[]{:S(2)}, u32[]{:S(2)}) async-start(f32[8,72,128]{2,1,0:T(8,128)} %pack.1), calls=%async_computation | async-start | bytes 589824 | tf_op jit(solution)/shard_map/all_to_all | solution.py:562
  10.5 0.0 copy-done.6
  10.5 0.0 copy-done
  10.6 0.0 copy-done.1
  10.6 0.0 copy-done.8
  10.6 0.0 copy-done.7
  10.6 5.4 %block_0.1 = (f32[2,3,48,16,128]{4,3,2,1,0:T(8,128)}, f32[1632,128]{1,0:T(8,128)S(1)}, f32[640,128]{1,0:T(8,128)S(1)}, f32[48,16,128]{2,1,0:T(8,128)S(1)}) custom-call(s32[2]{0:T(128)S(1)} %copy-done.6, bf16[2,3,48,16,128]{4,3,2,1,0:T(8,128)(2,1)S(1)} %copy-done, f32[2,48,16,128]{3,2,1,0:T(8,128)S(1)} %copy-done.1, f32[2,48]{1,0:T(2,128)S(1)} %copy-done.7, ...), custom_call_target="tpu_custom_call" | custom-call | flops 3000000000 | bytes 10000000 | tf_op jit(solution)/shard_map/block_0/pallas_call | solution.py:567
  16.0 0.0 copy-start.10
  16.0 0.7 %copy-done.10 = f32[48,16,128]{2,1,0:T(8,128)} copy-done((f32[48,16,128]{2,1,0:T(8,128)}, f32[48,16,128]{2,1,0:T(8,128)S(1)}, u32[]{:S(2)}) %copy-start.10) | copy-done | bytes 393240
  16.8 3.4 %all-to-all-done.in_ref = f32[8,72,128]{2,1,0:T(8,128)S(1)} async-done(((f32[8,72,128]{2,1,0:T(8,128)}), f32[8,72,128]{2,1,0:T(8,128)S(1)}, u32[]{:S(2)}, u32[]{:S(2)}) %all-to-all-start) | async-done | bytes 294944 | tf_op jit(solution)/shard_map/all_to_all | solution.py:562
  20.2 0.8 %route.1 = f32[8,64,128]{2,1,0:T(8,128)} custom-call(f32[8,72,128]{2,1,0:T(8,128)S(1)} %all-to-all-done.in_ref), custom_call_target="tpu_custom_call" | custom-call | tf_op jit(solution)/shard_map/route/pallas_call | solution.py:597
  21.0 3.6 %all-to-all-start.1 = ((f32[8,64,128]{2,1,0:T(8,128)}), f32[8,64,128]{2,1,0:T(8,128)S(1)}, u32[]{:S(2)}, u32[]{:S(2)}) async-start(f32[8,64,128]{2,1,0:T(8,128)} %route.1), calls=%async_computation.1 | async-start | bytes 524288 | tf_op jit(solution)/shard_map/all_to_all | solution.py:606
  24.6 0.0 copy-start.11
  24.6 1.0 %copy-done.11 = f32[48,16,128]{2,1,0:T(8,128)S(1)} copy-done((f32[48,16,128]{2,1,0:T(8,128)S(1)}, f32[48,16,128]{2,1,0:T(8,128)}, u32[]{:S(2)}) %copy-start.11) | copy-done | bytes 393240
  25.6 0.0 copy-start.4
  25.6 0.0 copy-start.5
  25.6 5.4 %block_1.1 = (f32[2,3,48,16,128]{4,3,2,1,0:T(8,128)}, f32[1632,128]{1,0:T(8,128)S(1)}, f32[640,128]{1,0:T(8,128)S(1)}) custom-call(s32[2]{0:T(128)S(1)} %copy-done.6, bf16[2,3,48,16,128]{4,3,2,1,0:T(8,128)(2,1)S(1)} %copy-done, f32[48,16,128]{2,1,0:T(8,128)S(1)} %copy-done.11, f32[2,48]{1,0:T(2,128)S(1)} %copy-done.7, ...), custom_call_target="tpu_custom_call", output_to_operand_aliasing={{0}: (5, {})} | custom-call | flops 3000000000 | bytes 10000000 | tf_op jit(solution)/shard_map/block_1/pallas_call | solution.py:567
  31.0 0.0 copy-start.2
  31.0 0.7 copy-done.2
  31.7 0.0 copy-start.9
  31.7 1.4 %all-to-all-done.1.halo_ref = f32[8,64,128]{2,1,0:T(8,128)S(1)} async-done(((f32[8,64,128]{2,1,0:T(8,128)}), f32[8,64,128]{2,1,0:T(8,128)S(1)}, u32[]{:S(2)}, u32[]{:S(2)}) %all-to-all-start.1) | async-done | bytes 262176 | tf_op jit(solution)/shard_map/all_to_all | solution.py:606
  33.1 0.0 copy-done.4
  33.1 0.0 copy-done.5
  33.1 0.0 copy-start.3
  33.1 1.0 %copy-done.3 = f32[640,128]{1,0:T(8,128)S(1)} copy-done((f32[640,128]{1,0:T(8,128)S(1)}, f32[640,128]{1,0:T(8,128)}, u32[]{:S(2)}) %copy-start.3) | copy-done | bytes 327704
  34.1 2.3 %ends.1 = (f32[2,3,48,16,128]{4,3,2,1,0:T(8,128)}, f32[2,1632,128]{2,1,0:T(8,128)S(1)}) custom-call(s32[2]{0:T(128)S(1)} %copy-done.6, s32[2,3]{1,0:T(2,128)S(1)} %copy-done.4, s32[2,3]{1,0:T(2,128)S(1)} %copy-done.5, f32[2,48]{1,0:T(2,128)S(1)} %copy-done.7, f32[8,64,128]{2,1,0:T(8,128)S(1)} %all-to-all-done.1.halo_ref, ...), custom_call_target="tpu_custom_call", output_to_operand_aliasing={{0}: (8, {})} | custom-call | tf_op jit(solution)/shard_map/ends/pallas_call | solution.py:611
  36.4 0.0 copy-done.9
  36.4 1.4 %close.1 = (f32[8,2,2,3,24,128]{5,4,3,2,1,0:T(8,128)S(1)}, f32[8,2,2,3,24,128]{5,4,3,2,1,0:T(8,128)S(1)}) custom-call(f32[1632,128]{1,0:T(8,128)S(1)} %get-tuple-element.35.part_0, f32[1632,128]{1,0:T(8,128)S(1)} %get-tuple-element.36.part_1, f32[2,1632,128]{2,1,0:T(8,128)S(1)} %get-tuple-element.37.xdone, f32[2,16]{1,0:T(2,128)S(1)} %copy-done.9), custom_call_target="tpu_custom_call" | custom-call | tf_op jit(solution)/shard_map/close/pallas_call | solution.py:626
  37.9 0.1 collective-permute-start
  38.0 2.8 %collective-permute-done = f32[8,2,2,3,24,128]{5,4,3,2,1,0:T(8,128)S(1)} collective-permute-done((f32[8,2,2,3,24,128]{5,4,3,2,1,0:T(8,128)S(1)}, f32[8,2,2,3,24,128]{5,4,3,2,1,0:T(8,128)S(1)}, u32[]{:S(2)}, u32[]{:S(2)}) %collective-permute-start) | collective-permute-done | bytes 1179680 | tf_op jit(solution)/shard_map/ppermute | solution.py:658
  40.8 0.2 shard_map.95
  41.0 1.5 %collective-permute-start.1 = (f32[4,2,72,128]{3,2,1,0:T(8,128)S(1)}, f32[4,2,72,128]{3,2,1,0:T(8,128)S(1)}, u32[]{:S(2)}, u32[]{:S(2)}) collective-permute-start(f32[4,2,72,128]{3,2,1,0:T(8,128)S(1)} %get-tuple-element.41), channel_id=1, source_target_pairs={{0,1},{1,0},{2,3},{3,2},{4,5},{5,4},{6,7},{7,6},{8,9},{9,8},{10,11... | collective-permute-start | bytes 884744 | tf_op jit(solution)/shard_map/ppermute | solution.py:658
  42.4 1.5 %collective-permute-start.2 = (f32[4,2,72,128]{3,2,1,0:T(8,128)S(1)}, f32[4,2,72,128]{3,2,1,0:T(8,128)S(1)}, u32[]{:S(2)}, u32[]{:S(2)}) collective-permute-start(f32[4,2,72,128]{3,2,1,0:T(8,128)S(1)} %get-tuple-element.43), channel_id=1, source_target_pairs={{0,16},{1,17},{2,18},{3,19},{4,20},{5,21},{6,22},{7,23},{8,24},{9,... | collective-permute-start | bytes 884744 | tf_op jit(solution)/shard_map/ppermute | solution.py:658
  43.9 6.1 %collective-permute-done.1.got_y = f32[4,2,72,128]{3,2,1,0:T(8,128)S(1)} collective-permute-done((f32[4,2,72,128]{3,2,1,0:T(8,128)S(1)}, f32[4,2,72,128]{3,2,1,0:T(8,128)S(1)}, u32[]{:S(2)}, u32[]{:S(2)}) %collective-permute-start.1) | collective-permute-done | bytes 294944 | tf_op jit(solution)/shard_map/ppermute | solution.py:658
  50.1 1.1 %collective-permute-done.2.got_x = f32[4,2,72,128]{3,2,1,0:T(8,128)S(1)} collective-permute-done((f32[4,2,72,128]{3,2,1,0:T(8,128)S(1)}, f32[4,2,72,128]{3,2,1,0:T(8,128)S(1)}, u32[]{:S(2)}, u32[]{:S(2)}) %collective-permute-start.2) | collective-permute-done | bytes 294944 | tf_op jit(solution)/shard_map/ppermute | solution.py:658
  51.2 0.1 shard_map.96
  51.3 1.6 %collective-permute-start.3 = (f32[4,72,128]{2,1,0:T(8,128)S(1)}, f32[4,72,128]{2,1,0:T(8,128)S(1)}, u32[]{:S(2)}, u32[]{:S(2)}) collective-permute-start(f32[4,72,128]{2,1,0:T(8,128)S(1)} %get-tuple-element.45), channel_id=1, source_target_pairs={{0,16},{1,17},{2,18},{3,19},{4,20},{5,21},{6,22},{7,23},{8,24},{9,... | collective-permute-start | bytes 442376 | tf_op jit(solution)/shard_map/ppermute | solution.py:658
  52.8 0.6 collective-permute-start.4
  53.4 3.1 %collective-permute-done.3.got_0 = f32[4,72,128]{2,1,0:T(8,128)S(1)} collective-permute-done((f32[4,72,128]{2,1,0:T(8,128)S(1)}, f32[4,72,128]{2,1,0:T(8,128)S(1)}, u32[]{:S(2)}, u32[]{:S(2)}) %collective-permute-start.3) | collective-permute-done | bytes 147488 | tf_op jit(solution)/shard_map/ppermute | solution.py:658
  56.5 1.5 %collective-permute-done.4.got_1 = f32[4,72,128]{2,1,0:T(8,128)S(1)} collective-permute-done((f32[4,72,128]{2,1,0:T(8,128)S(1)}, f32[4,72,128]{2,1,0:T(8,128)S(1)}, u32[]{:S(2)}, u32[]{:S(2)}) %collective-permute-start.4) | collective-permute-done | bytes 147488 | tf_op jit(solution)/shard_map/ppermute | solution.py:658
  58.0 0.8 %collective-permute-start.5 = (f32[2,72,128]{2,1,0:T(8,128)S(1)}, f32[2,72,128]{2,1,0:T(8,128)S(1)}, u32[]{:S(2)}, u32[]{:S(2)}) collective-permute-start(f32[2,72,128]{2,1,0:T(8,128)S(1)} %get-tuple-element.49), channel_id=1, source_target_pairs={{0,2},{1,3},{2,4},{3,5},{4,6},{5,7},{6,0},{7,1},{8,10},{9,11},{10,... | collective-permute-start | bytes 221192 | tf_op jit(solution)/shard_map/ppermute | solution.py:658
  58.8 2.2 %collective-permute-start.6 = (f32[2,72,128]{2,1,0:T(8,128)S(1)}, f32[2,72,128]{2,1,0:T(8,128)S(1)}, u32[]{:S(2)}, u32[]{:S(2)}) collective-permute-start(f32[2,72,128]{2,1,0:T(8,128)S(1)} %get-tuple-element.50), channel_id=1, source_target_pairs={{0,4},{1,5},{2,6},{3,7},{4,0},{5,1},{6,2},{7,3},{8,12},{9,13},{10,... | collective-permute-start | bytes 221192 | tf_op jit(solution)/shard_map/ppermute | solution.py:658
  61.0 1.6 %collective-permute-start.7 = (f32[2,72,128]{2,1,0:T(8,128)S(1)}, f32[2,72,128]{2,1,0:T(8,128)S(1)}, u32[]{:S(2)}, u32[]{:S(2)}) collective-permute-start(f32[2,72,128]{2,1,0:T(8,128)S(1)} %get-tuple-element.51), channel_id=1, source_target_pairs={{0,6},{1,7},{2,0},{3,1},{4,2},{5,3},{6,4},{7,5},{8,14},{9,15},{10,... | collective-permute-start | bytes 221192 | tf_op jit(solution)/shard_map/ppermute | solution.py:658
  62.6 1.7 %collective-permute-done.5.refs_1_ = f32[2,72,128]{2,1,0:T(8,128)S(1)} collective-permute-done((f32[2,72,128]{2,1,0:T(8,128)S(1)}, f32[2,72,128]{2,1,0:T(8,128)S(1)}, u32[]{:S(2)}, u32[]{:S(2)}) %collective-permute-start.5) | collective-permute-done | bytes 73760 | tf_op jit(solution)/shard_map/ppermute | solution.py:658
  64.3 1.4 %collective-permute-done.6.refs_2_ = f32[2,72,128]{2,1,0:T(8,128)S(1)} collective-permute-done((f32[2,72,128]{2,1,0:T(8,128)S(1)}, f32[2,72,128]{2,1,0:T(8,128)S(1)}, u32[]{:S(2)}, u32[]{:S(2)}) %collective-permute-start.6) | collective-permute-done | bytes 73760 | tf_op jit(solution)/shard_map/ppermute | solution.py:658
  65.7 0.2 collective-permute-done.7.refs_3_
  65.9 0.1 collective-permute-start.10
  66.0 0.4 collective-permute-start.9
  66.4 1.4 %collective-permute-start.8 = (f32[2,72,128]{2,1,0:T(8,128)S(1)}, f32[2,72,128]{2,1,0:T(8,128)S(1)}, u32[]{:S(2)}, u32[]{:S(2)}) collective-permute-start(f32[2,72,128]{2,1,0:T(8,128)S(1)} %shard_map.98), channel_id=1, source_target_pairs={{0,8},{1,9},{2,10},{3,11},{4,12},{5,13},{6,14},{7,15},{8,0},{9,1},... | collective-permute-start | bytes 221192 | tf_op jit(solution)/shard_map/ppermute | solution.py:658
  67.8 2.0 %collective-permute-done.10 = f32[2,72,128]{2,1,0:T(8,128)S(1)} collective-permute-done((f32[2,72,128]{2,1,0:T(8,128)S(1)}, f32[2,72,128]{2,1,0:T(8,128)S(1)}, u32[]{:S(2)}, u32[]{:S(2)}) %collective-permute-start.10) | collective-permute-done | bytes 73760 | tf_op jit(solution)/shard_map/ppermute | solution.py:658
  69.9 1.3 %collective-permute-done.9 = f32[2,72,128]{2,1,0:T(8,128)S(1)} collective-permute-done((f32[2,72,128]{2,1,0:T(8,128)S(1)}, f32[2,72,128]{2,1,0:T(8,128)S(1)}, u32[]{:S(2)}, u32[]{:S(2)}) %collective-permute-start.9) | collective-permute-done | bytes 73760 | tf_op jit(solution)/shard_map/ppermute | solution.py:658
  71.2 0.0 collective-permute-done.8
  71.2 1.3 %shard_map.99 = f32[12,6144]{1,0:T(8,128)} custom-call(f32[2,3,24,128]{3,2,1,0:T(8,128)S(1)} %bitcast.8, f32[2,3,24,128]{3,2,1,0:T(8,128)S(1)} %bitcast.11, f32[2,3,24,128]{3,2,1,0:T(8,128)S(1)} %bitcast.10, f32[2,3,24,128]{3,2,1,0:T(8,128)S(1)} %bitcast.9), custom_call_target="tpu_custom_call" | custom-call | tf_op jit(solution)/shard_map/pallas_call | solution.py:638
  (2 shorter events, 0.1 us)
Async XLA Ops:
  0.6 9.9 %copy-start.6 = (s32[2]{0:T(128)S(1)}, s32[2]{0:T(128)}, u32[]{:S(2)}) copy-start(s32[2]{0:T(128)} %len_ref.5) | copy-start | bytes 28
  0.6 9.9 %copy-start = (bf16[2,3,48,16,128]{4,3,2,1,0:T(8,128)(2,1)S(1)}, bf16[2,3,48,16,128]{4,3,2,1,0:T(8,128)(2,1)}, u32[]{:S(2)}) copy-start(bf16[2,3,48,16,128]{4,3,2,1,0:T(8,128)(2,1)} %seed_in.5) | copy-start | bytes 3538948
  0.7 9.9 %copy-start.1 = (f32[2,48,16,128]{3,2,1,0:T(8,128)S(1)}, f32[2,48,16,128]{3,2,1,0:T(8,128)}, u32[]{:S(2)}) copy-start(f32[2,48,16,128]{3,2,1,0:T(8,128)} %stiff_in.3) | copy-start | bytes 2359300
  0.7 9.9 %copy-start.8 = (f32[2,128]{1,0:T(2,128)S(1)}, f32[2,128]{1,0:T(2,128)}, u32[]{:S(2)}) copy-start(f32[2,128]{1,0:T(2,128)} %cz_ref.5) | copy-start | bytes 3076
  0.7 9.9 %copy-start.7 = (f32[2,48]{1,0:T(2,128)S(1)}, f32[2,48]{1,0:T(2,128)}, u32[]{:S(2)}) copy-start(f32[2,48]{1,0:T(2,128)} %cx_ref.5) | copy-start | bytes 1156
  3.2 16.9 %all-to-all-start = ((f32[8,72,128]{2,1,0:T(8,128)}), f32[8,72,128]{2,1,0:T(8,128)S(1)}, u32[]{:S(2)}, u32[]{:S(2)}) async-start(f32[8,72,128]{2,1,0:T(8,128)} %pack.1), calls=%async_computation | async-start | bytes 589824 | tf_op jit(solution)/shard_map/all_to_all | solution.py:562
  16.0 0.7 %copy-start.10 = (f32[48,16,128]{2,1,0:T(8,128)}, f32[48,16,128]{2,1,0:T(8,128)S(1)}, u32[]{:S(2)}) copy-start(f32[48,16,128]{2,1,0:T(8,128)S(1)} %get-tuple-element.30.stiff_in) | copy-start | bytes 1179652
  21.0 12.1 %all-to-all-start.1 = ((f32[8,64,128]{2,1,0:T(8,128)}), f32[8,64,128]{2,1,0:T(8,128)S(1)}, u32[]{:S(2)}, u32[]{:S(2)}) async-start(f32[8,64,128]{2,1,0:T(8,128)} %route.1), calls=%async_computation.1 | async-start | bytes 524288 | tf_op jit(solution)/shard_map/all_to_all | solution.py:606
  24.6 1.0 %copy-start.11 = (f32[48,16,128]{2,1,0:T(8,128)S(1)}, f32[48,16,128]{2,1,0:T(8,128)}, u32[]{:S(2)}) copy-start(f32[48,16,128]{2,1,0:T(8,128)} %copy-done.10) | copy-start | bytes 1179652
  25.6 7.5 %copy-start.4 = (s32[2,3]{1,0:T(2,128)S(1)}, s32[2,3]{1,0:T(2,128)}, u32[]{:S(2)}) copy-start(s32[2,3]{1,0:T(2,128)} %low_ref.1) | copy-start | bytes 76
  25.6 7.5 %copy-start.5 = (s32[2,3]{1,0:T(2,128)S(1)}, s32[2,3]{1,0:T(2,128)}, u32[]{:S(2)}) copy-start(s32[2,3]{1,0:T(2,128)} %up_ref.1) | copy-start | bytes 76
  31.0 0.7 %copy-start.2 = (f32[640,128]{1,0:T(8,128)}, f32[640,128]{1,0:T(8,128)S(1)}, u32[]{:S(2)}) copy-start(f32[640,128]{1,0:T(8,128)S(1)} %get-tuple-element.32.edge_1) | copy-start | bytes 983044
  31.7 4.7 %copy-start.9 = (f32[2,16]{1,0:T(2,128)S(1)}, f32[2,16]{1,0:T(2,128)}, u32[]{:S(2)}) copy-start(f32[2,16]{1,0:T(2,128)} %cy_ref.1) | copy-start | bytes 388
  33.1 1.0 %copy-start.3 = (f32[640,128]{1,0:T(8,128)S(1)}, f32[640,128]{1,0:T(8,128)}, u32[]{:S(2)}) copy-start(f32[640,128]{1,0:T(8,128)} %copy-done.2) | copy-start | bytes 983044
  37.9 2.9 %collective-permute-start = (f32[8,2,2,3,24,128]{5,4,3,2,1,0:T(8,128)S(1)}, f32[8,2,2,3,24,128]{5,4,3,2,1,0:T(8,128)S(1)}, u32[]{:S(2)}, u32[]{:S(2)}) collective-permute-start(f32[8,2,2,3,24,128]{5,4,3,2,1,0:T(8,128)S(1)} %get-tuple-element.39), channel_id=1, source_target_pairs={{0,8},{1,9},{2,10},{3,11},{4,12},{5,13},{6,14},{7,15},{8,0},{9,1},... | collective-permute-start | bytes 3538952 | tf_op jit(solution)/shard_map/ppermute | solution.py:658
  41.0 9.1 %collective-permute-start.1 = (f32[4,2,72,128]{3,2,1,0:T(8,128)S(1)}, f32[4,2,72,128]{3,2,1,0:T(8,128)S(1)}, u32[]{:S(2)}, u32[]{:S(2)}) collective-permute-start(f32[4,2,72,128]{3,2,1,0:T(8,128)S(1)} %get-tuple-element.41), channel_id=1, source_target_pairs={{0,1},{1,0},{2,3},{3,2},{4,5},{5,4},{6,7},{7,6},{8,9},{9,8},{10,11... | collective-permute-start | bytes 884744 | tf_op jit(solution)/shard_map/ppermute | solution.py:658
  42.4 8.8 %collective-permute-start.2 = (f32[4,2,72,128]{3,2,1,0:T(8,128)S(1)}, f32[4,2,72,128]{3,2,1,0:T(8,128)S(1)}, u32[]{:S(2)}, u32[]{:S(2)}) collective-permute-start(f32[4,2,72,128]{3,2,1,0:T(8,128)S(1)} %get-tuple-element.43), channel_id=1, source_target_pairs={{0,16},{1,17},{2,18},{3,19},{4,20},{5,21},{6,22},{7,23},{8,24},{9,... | collective-permute-start | bytes 884744 | tf_op jit(solution)/shard_map/ppermute | solution.py:658
  51.3 5.2 %collective-permute-start.3 = (f32[4,72,128]{2,1,0:T(8,128)S(1)}, f32[4,72,128]{2,1,0:T(8,128)S(1)}, u32[]{:S(2)}, u32[]{:S(2)}) collective-permute-start(f32[4,72,128]{2,1,0:T(8,128)S(1)} %get-tuple-element.45), channel_id=1, source_target_pairs={{0,16},{1,17},{2,18},{3,19},{4,20},{5,21},{6,22},{7,23},{8,24},{9,... | collective-permute-start | bytes 442376 | tf_op jit(solution)/shard_map/ppermute | solution.py:658
  52.8 5.1 %collective-permute-start.4 = (f32[4,72,128]{2,1,0:T(8,128)S(1)}, f32[4,72,128]{2,1,0:T(8,128)S(1)}, u32[]{:S(2)}, u32[]{:S(2)}) collective-permute-start(f32[4,72,128]{2,1,0:T(8,128)S(1)} %get-tuple-element.47), channel_id=1, source_target_pairs={{0,1},{1,0},{2,3},{3,2},{4,5},{5,4},{6,7},{7,6},{8,9},{9,8},{10,11... | collective-permute-start | bytes 442376 | tf_op jit(solution)/shard_map/ppermute | solution.py:658
  58.0 6.3 %collective-permute-start.5 = (f32[2,72,128]{2,1,0:T(8,128)S(1)}, f32[2,72,128]{2,1,0:T(8,128)S(1)}, u32[]{:S(2)}, u32[]{:S(2)}) collective-permute-start(f32[2,72,128]{2,1,0:T(8,128)S(1)} %get-tuple-element.49), channel_id=1, source_target_pairs={{0,2},{1,3},{2,4},{3,5},{4,6},{5,7},{6,0},{7,1},{8,10},{9,11},{10,... | collective-permute-start | bytes 221192 | tf_op jit(solution)/shard_map/ppermute | solution.py:658
  58.8 6.9 %collective-permute-start.6 = (f32[2,72,128]{2,1,0:T(8,128)S(1)}, f32[2,72,128]{2,1,0:T(8,128)S(1)}, u32[]{:S(2)}, u32[]{:S(2)}) collective-permute-start(f32[2,72,128]{2,1,0:T(8,128)S(1)} %get-tuple-element.50), channel_id=1, source_target_pairs={{0,4},{1,5},{2,6},{3,7},{4,0},{5,1},{6,2},{7,3},{8,12},{9,13},{10,... | collective-permute-start | bytes 221192 | tf_op jit(solution)/shard_map/ppermute | solution.py:658
  61.0 4.8 %collective-permute-start.7 = (f32[2,72,128]{2,1,0:T(8,128)S(1)}, f32[2,72,128]{2,1,0:T(8,128)S(1)}, u32[]{:S(2)}, u32[]{:S(2)}) collective-permute-start(f32[2,72,128]{2,1,0:T(8,128)S(1)} %get-tuple-element.51), channel_id=1, source_target_pairs={{0,6},{1,7},{2,0},{3,1},{4,2},{5,3},{6,4},{7,5},{8,14},{9,15},{10,... | collective-permute-start | bytes 221192 | tf_op jit(solution)/shard_map/ppermute | solution.py:658
  65.9 4.0 %collective-permute-start.10 = (f32[2,72,128]{2,1,0:T(8,128)S(1)}, f32[2,72,128]{2,1,0:T(8,128)S(1)}, u32[]{:S(2)}, u32[]{:S(2)}) collective-permute-start(f32[2,72,128]{2,1,0:T(8,128)S(1)} %shard_map.98), channel_id=1, source_target_pairs={{0,24},{1,25},{2,26},{3,27},{4,28},{5,29},{6,30},{7,31},{8,16},{9,... | collective-permute-start | bytes 221192 | tf_op jit(solution)/shard_map/ppermute | solution.py:658
  66.0 5.2 %collective-permute-start.9 = (f32[2,72,128]{2,1,0:T(8,128)S(1)}, f32[2,72,128]{2,1,0:T(8,128)S(1)}, u32[]{:S(2)}, u32[]{:S(2)}) collective-permute-start(f32[2,72,128]{2,1,0:T(8,128)S(1)} %shard_map.98), channel_id=1, source_target_pairs={{0,16},{1,17},{2,18},{3,19},{4,20},{5,21},{6,22},{7,23},{8,24},{9,... | collective-permute-start | bytes 221192 | tf_op jit(solution)/shard_map/ppermute | solution.py:658
  66.4 4.8 %collective-permute-start.8 = (f32[2,72,128]{2,1,0:T(8,128)S(1)}, f32[2,72,128]{2,1,0:T(8,128)S(1)}, u32[]{:S(2)}, u32[]{:S(2)}) collective-permute-start(f32[2,72,128]{2,1,0:T(8,128)S(1)} %shard_map.98), channel_id=1, source_target_pairs={{0,8},{1,9},{2,10},{3,11},{4,12},{5,13},{6,14},{7,15},{8,0},{9,1},... | collective-permute-start | bytes 221192 | tf_op jit(solution)/shard_map/ppermute | solution.py:658

commit v7 on v6

--- a/solution.py
+++ b/solution.py
@@ -422,7 +422,8 @@
         copy.wait()
 
 
-def close_kernel(fast, per, part_0, part_1, xdone, cy_ref, keep_ref, send_ref):
+def close_kernel(fast, per, part_0, part_1, xdone, cy_ref, edge_0, edge_1, keep_ref, send_ref):
+    del edge_0, edge_1
     slots, ny = cy_ref.shape
     pitch = ny + 1
     depth = per * slots * ny
@@ -626,11 +627,11 @@
     keep, send = pl.pallas_call(
         functools.partial(close_kernel, fast, per),
         out_shape=(half, half),
-        in_specs=[VMEM] * 4,
+        in_specs=[VMEM] * 4 + [ANY] * 2,
         out_specs=(VMEM, VMEM),
         compiler_params=params(12),
         name="close",
-    )(part_0, part_1, last, coord_y)
+    )(part_0, part_1, last, coord_y, edge_0, edge_1)
 
     scale = math.sqrt(LX * LY * LZ / (groups * devs * slots * nx * ny * nz))
 

time: 72.8 us -> 71.1 us (0.977)
  local copies, waits for them, and re-layouts: 3.46 us -> 2.07 us
    unnamed x24 -> x20, local copies, waits for them, and re-layouts: 3.46 us -> 2.07 us
    all_to_all x1, waiting for transfers between devices: 1.4 us -> 2.18 us  [on_device(): halos = lax.all_to_all(routed, 'dev', 0, 0)]
  transfers between devices with their start and end apart: 13 -> 13, of which waited for: 12 -> 11; matrix products, arithmetic and copies ran while one was open for 0% -> 0% of each run, Pallas kernels for 15% -> 15%
where the time goes in v7:
time: 71.1 us; the launch traced here: 70.7 us
  waiting for transfers between devices  26.3 us (37%)
  starting transfers between devices  22 us (31%)
  Pallas kernels  19.5 us (27%)
  local copies, waits for them, and re-layouts  2.07 us (3%)
  between operations  0.81 us (1%)
    ppermute x11, waiting for transfers between devices, move(): return lax.ppermute(value, ('group', 'dev'), links)  21.1 us
    ppermute x11, starting transfers between devices, move(): return lax.ppermute(value, ('group', 'dev'), links)  11.1 us
    pallas_call x2, Pallas kernels, one_block(): pl.pallas_call(functools.partial(block_kernel, b), out_shape=(shape(slots...  10.8 us
    all_to_all x1, starting transfers between devices, on_device(): spread = lax.all_to_all(packed, 'dev', 0, 0)  7.32 us
    all_to_all x1, starting transfers between devices, on_device(): halos = lax.all_to_all(routed, 'dev', 0, 0)  3.62 us
    all_to_all x1, waiting for transfers between devices, on_device(): spread = lax.all_to_all(packed, 'dev', 0, 0)  3.02 us
    pallas_call x1, Pallas kernels, on_device(): pl.pallas_call(functools.partial(pack_kernel, devs, slots, nx, ny, nz), o...  2.51 us
    pallas_call x1, Pallas kernels, on_device(): pl.pallas_call(ends_kernel, out_shape=(shape(slots, 3, nx, ny, nz), shape...  2.29 us
  transfers between devices with their start and end apart: 13, of which 11 were waited for; matrix products, arithmetic and copies ran while one was open for 0% of the time, Pallas kernels for 15%

profile of v7, /device:TPU:0, one launch (start us, length us, event | category | flops | bytes accessed | tf_op | source)
XLA Modules:
  0.0 70.7 jit_solution(6763173689289295277)
XLA Ops:
  0.6 0.0 copy-start.6
  0.6 0.0 copy-start
  0.7 0.0 copy-start.8
  0.7 0.0 copy-start.7
  0.7 2.5 %pack.1 = f32[8,72,128]{2,1,0:T(8,128)} custom-call(s32[2]{0:T(128)} %len_ref.5, s32[2,3]{1,0:T(2,128)} %low_ref.1, s32[2,3]{1,0:T(2,128)} %up_ref.1, bf16[2,3,48,16,128]{4,3,2,1,0:T(8,128)(2,1)} %seed_in.5, f32[2,48,16,128]{3,2,1,0:T(8,128)} %stiff_in.3), custom_call_target="tpu_custom_call" | custom-call | tf_op jit(solution)/shard_map/pack/pallas_call | solution.py:546
  3.2 7.3 %all-to-all-start = ((f32[8,72,128]{2,1,0:T(8,128)}), f32[8,72,128]{2,1,0:T(8,128)S(1)}, u32[]{:S(2)}, u32[]{:S(2)}) async-start(f32[8,72,128]{2,1,0:T(8,128)} %pack.1), calls=%async_computation | async-start | bytes 589824 | tf_op jit(solution)/shard_map/all_to_all | solution.py:563
  10.5 0.0 copy-done.6
  10.5 0.0 copy-done
  10.5 0.0 copy-done.8
  10.5 0.0 copy-done.7
  10.5 0.0 copy-start.3
  10.6 1.1 %copy-done.3 = f32[2,48,16,128]{3,2,1,0:T(8,128)S(1)} copy-done((f32[2,48,16,128]{3,2,1,0:T(8,128)S(1)}, f32[2,48,16,128]{3,2,1,0:T(8,128)}, u32[]{:S(2)}) %copy-start.3) | copy-done | bytes 786456
  11.7 5.4 %block_0.1 = (f32[2,3,48,16,128]{4,3,2,1,0:T(8,128)}, f32[1632,128]{1,0:T(8,128)S(1)}, f32[640,128]{1,0:T(8,128)S(1)}, f32[48,16,128]{2,1,0:T(8,128)S(1)}) custom-call(s32[2]{0:T(128)S(1)} %copy-done.6, bf16[2,3,48,16,128]{4,3,2,1,0:T(8,128)(2,1)S(1)} %copy-done, f32[2,48,16,128]{3,2,1,0:T(8,128)S(1)} %copy-done.3, f32[2,48]{1,0:T(2,128)S(1)} %copy-done.7, ...), custom_call_target="tpu_custom_call" | custom-call | flops 3000000000 | bytes 10000000 | tf_op jit(solution)/shard_map/block_0/pallas_call | solution.py:568
  17.1 3.0 %all-to-all-done.in_ref = f32[8,72,128]{2,1,0:T(8,128)S(1)} async-done(((f32[8,72,128]{2,1,0:T(8,128)}), f32[8,72,128]{2,1,0:T(8,128)S(1)}, u32[]{:S(2)}, u32[]{:S(2)}) %all-to-all-start) | async-done | bytes 294944 | tf_op jit(solution)/shard_map/all_to_all | solution.py:563
  20.1 0.8 %route.1 = f32[8,64,128]{2,1,0:T(8,128)} custom-call(f32[8,72,128]{2,1,0:T(8,128)S(1)} %all-to-all-done.in_ref), custom_call_target="tpu_custom_call" | custom-call | tf_op jit(solution)/shard_map/route/pallas_call | solution.py:598
  21.0 3.6 %all-to-all-start.1 = ((f32[8,64,128]{2,1,0:T(8,128)}), f32[8,64,128]{2,1,0:T(8,128)S(1)}, u32[]{:S(2)}, u32[]{:S(2)}) async-start(f32[8,64,128]{2,1,0:T(8,128)} %route.1), calls=%async_computation.1 | async-start | bytes 524288 | tf_op jit(solution)/shard_map/all_to_all | solution.py:607
  24.6 0.0 copy-start.4
  24.6 0.0 copy-start.5
  24.6 5.4 %block_1.1 = (f32[2,3,48,16,128]{4,3,2,1,0:T(8,128)}, f32[1632,128]{1,0:T(8,128)S(1)}, f32[640,128]{1,0:T(8,128)S(1)}) custom-call(s32[2]{0:T(128)S(1)} %copy-done.6, bf16[2,3,48,16,128]{4,3,2,1,0:T(8,128)(2,1)S(1)} %copy-done, f32[48,16,128]{2,1,0:T(8,128)S(1)} %get-tuple-element.30.stiff_in, ...), custom_call_target="tpu_custom_call", output_to_operand_aliasing={{0}: (5, {})} | custom-call | flops 3000000000 | bytes 10000000 | tf_op jit(solution)/shard_map/block_1/pallas_call | solution.py:568
  30.0 0.0 copy-start.1
  30.0 0.9 %copy-done.1 = f32[1632,128]{1,0:T(8,128)} copy-done((f32[1632,128]{1,0:T(8,128)}, f32[1632,128]{1,0:T(8,128)S(1)}, u32[]{:S(2)}) %copy-start.1) | copy-done | bytes 835608
  30.9 0.0 copy-start.9
  30.9 2.2 %all-to-all-done.1.halo_ref = f32[8,64,128]{2,1,0:T(8,128)S(1)} async-done(((f32[8,64,128]{2,1,0:T(8,128)}), f32[8,64,128]{2,1,0:T(8,128)S(1)}, u32[]{:S(2)}, u32[]{:S(2)}) %all-to-all-start.1) | async-done | bytes 262176 | tf_op jit(solution)/shard_map/all_to_all | solution.py:607
  33.1 0.0 copy-start.2
  33.1 0.0 copy-done.4
  33.1 0.0 copy-done.5
  33.1 2.3 %ends.1 = (f32[2,3,48,16,128]{4,3,2,1,0:T(8,128)}, f32[2,1632,128]{2,1,0:T(8,128)S(1)}) custom-call(s32[2]{0:T(128)S(1)} %copy-done.6, s32[2,3]{1,0:T(2,128)S(1)} %copy-done.4, s32[2,3]{1,0:T(2,128)S(1)} %copy-done.5, f32[2,48]{1,0:T(2,128)S(1)} %copy-done.7, f32[8,64,128]{2,1,0:T(8,128)S(1)} %all-to-all-done.1.halo_ref, ...), custom_call_target="tpu_custom_call", output_to_operand_aliasing={{0}: (8, {})} | custom-call | tf_op jit(solution)/shard_map/ends/pallas_call | solution.py:612
  35.4 0.0 copy-done.9
  35.4 0.0 copy-done.2
  35.4 1.4 %close.1 = (f32[8,2,2,3,24,128]{5,4,3,2,1,0:T(8,128)S(1)}, f32[8,2,2,3,24,128]{5,4,3,2,1,0:T(8,128)S(1)}) custom-call(f32[1632,128]{1,0:T(8,128)S(1)} %get-tuple-element.35.part_0, f32[1632,128]{1,0:T(8,128)S(1)} %copy-done.2, f32[2,1632,128]{2,1,0:T(8,128)S(1)} %get-tuple-element.37.xdone, f32[2,16]{1,0:T(2,128)S(1)} %copy-done.9, ...), custom_call_target="tpu_custom_call" | custom-call | tf_op jit(solution)/shard_map/close/pallas_call | solution.py:627
  36.9 0.1 collective-permute-start
  36.9 2.8 %collective-permute-done = f32[8,2,2,3,24,128]{5,4,3,2,1,0:T(8,128)S(1)} collective-permute-done((f32[8,2,2,3,24,128]{5,4,3,2,1,0:T(8,128)S(1)}, f32[8,2,2,3,24,128]{5,4,3,2,1,0:T(8,128)S(1)}, u32[]{:S(2)}, u32[]{:S(2)}) %collective-permute-start) | collective-permute-done | bytes 1179680 | tf_op jit(solution)/shard_map/ppermute | solution.py:659
  39.8 0.2 shard_map.95
  39.9 1.5 %collective-permute-start.1 = (f32[4,2,72,128]{3,2,1,0:T(8,128)S(1)}, f32[4,2,72,128]{3,2,1,0:T(8,128)S(1)}, u32[]{:S(2)}, u32[]{:S(2)}) collective-permute-start(f32[4,2,72,128]{3,2,1,0:T(8,128)S(1)} %get-tuple-element.41), channel_id=1, source_target_pairs={{0,1},{1,0},{2,3},{3,2},{4,5},{5,4},{6,7},{7,6},{8,9},{9,8},{10,11... | collective-permute-start | bytes 884744 | tf_op jit(solution)/shard_map/ppermute | solution.py:659
  41.4 1.5 %collective-permute-start.2 = (f32[4,2,72,128]{3,2,1,0:T(8,128)S(1)}, f32[4,2,72,128]{3,2,1,0:T(8,128)S(1)}, u32[]{:S(2)}, u32[]{:S(2)}) collective-permute-start(f32[4,2,72,128]{3,2,1,0:T(8,128)S(1)} %get-tuple-element.43), channel_id=1, source_target_pairs={{0,16},{1,17},{2,18},{3,19},{4,20},{5,21},{6,22},{7,23},{8,24},{9,... | collective-permute-start | bytes 884744 | tf_op jit(solution)/shard_map/ppermute | solution.py:659
  42.9 6.1 %collective-permute-done.1.got_y = f32[4,2,72,128]{3,2,1,0:T(8,128)S(1)} collective-permute-done((f32[4,2,72,128]{3,2,1,0:T(8,128)S(1)}, f32[4,2,72,128]{3,2,1,0:T(8,128)S(1)}, u32[]{:S(2)}, u32[]{:S(2)}) %collective-permute-start.1) | collective-permute-done | bytes 294944 | tf_op jit(solution)/shard_map/ppermute | solution.py:659
  49.1 1.1 %collective-permute-done.2.got_x = f32[4,2,72,128]{3,2,1,0:T(8,128)S(1)} collective-permute-done((f32[4,2,72,128]{3,2,1,0:T(8,128)S(1)}, f32[4,2,72,128]{3,2,1,0:T(8,128)S(1)}, u32[]{:S(2)}, u32[]{:S(2)}) %collective-permute-start.2) | collective-permute-done | bytes 294944 | tf_op jit(solution)/shard_map/ppermute | solution.py:659
  50.2 0.1 shard_map.96
  50.3 1.6 %collective-permute-start.3 = (f32[4,72,128]{2,1,0:T(8,128)S(1)}, f32[4,72,128]{2,1,0:T(8,128)S(1)}, u32[]{:S(2)}, u32[]{:S(2)}) collective-permute-start(f32[4,72,128]{2,1,0:T(8,128)S(1)} %get-tuple-element.45), channel_id=1, source_target_pairs={{0,16},{1,17},{2,18},{3,19},{4,20},{5,21},{6,22},{7,23},{8,24},{9,... | collective-permute-start | bytes 442376 | tf_op jit(solution)/shard_map/ppermute | solution.py:659
  51.8 0.6 collective-permute-start.4
  52.5 3.0 %collective-permute-done.3.got_0 = f32[4,72,128]{2,1,0:T(8,128)S(1)} collective-permute-done((f32[4,72,128]{2,1,0:T(8,128)S(1)}, f32[4,72,128]{2,1,0:T(8,128)S(1)}, u32[]{:S(2)}, u32[]{:S(2)}) %collective-permute-start.3) | collective-permute-done | bytes 147488 | tf_op jit(solution)/shard_map/ppermute | solution.py:659
  55.5 1.5 %collective-permute-done.4.got_1 = f32[4,72,128]{2,1,0:T(8,128)S(1)} collective-permute-done((f32[4,72,128]{2,1,0:T(8,128)S(1)}, f32[4,72,128]{2,1,0:T(8,128)S(1)}, u32[]{:S(2)}, u32[]{:S(2)}) %collective-permute-start.4) | collective-permute-done | bytes 147488 | tf_op jit(solution)/shard_map/ppermute | solution.py:659
  57.0 0.1 collective-permute-start.5
  57.2 2.1 %collective-permute-start.6 = (f32[2,72,128]{2,1,0:T(8,128)S(1)}, f32[2,72,128]{2,1,0:T(8,128)S(1)}, u32[]{:S(2)}, u32[]{:S(2)}) collective-permute-start(f32[2,72,128]{2,1,0:T(8,128)S(1)} %get-tuple-element.50), channel_id=1, source_target_pairs={{0,4},{1,5},{2,6},{3,7},{4,0},{5,1},{6,2},{7,3},{8,12},{9,13},{10,... | collective-permute-start | bytes 221192 | tf_op jit(solution)/shard_map/ppermute | solution.py:659
  59.2 1.7 %collective-permute-start.7 = (f32[2,72,128]{2,1,0:T(8,128)S(1)}, f32[2,72,128]{2,1,0:T(8,128)S(1)}, u32[]{:S(2)}, u32[]{:S(2)}) collective-permute-start(f32[2,72,128]{2,1,0:T(8,128)S(1)} %get-tuple-element.51), channel_id=1, source_target_pairs={{0,6},{1,7},{2,0},{3,1},{4,2},{5,3},{6,4},{7,5},{8,14},{9,15},{10,... | collective-permute-start | bytes 221192 | tf_op jit(solution)/shard_map/ppermute | solution.py:659
  60.9 2.4 %collective-permute-done.5.refs_1_ = f32[2,72,128]{2,1,0:T(8,128)S(1)} collective-permute-done((f32[2,72,128]{2,1,0:T(8,128)S(1)}, f32[2,72,128]{2,1,0:T(8,128)S(1)}, u32[]{:S(2)}, u32[]{:S(2)}) %collective-permute-start.5) | collective-permute-done | bytes 73760 | tf_op jit(solution)/shard_map/ppermute | solution.py:659
  63.3 0.0 collective-permute-done.6.refs_2_
  63.3 0.8 %collective-permute-done.7.refs_3_ = f32[2,72,128]{2,1,0:T(8,128)S(1)} collective-permute-done((f32[2,72,128]{2,1,0:T(8,128)S(1)}, f32[2,72,128]{2,1,0:T(8,128)S(1)}, u32[]{:S(2)}, u32[]{:S(2)}) %collective-permute-start.7) | collective-permute-done | bytes 73760 | tf_op jit(solution)/shard_map/ppermute | solution.py:659
  64.1 0.1 collective-permute-start.10
  64.2 0.5 collective-permute-start.9
  64.7 1.3 %collective-permute-start.8 = (f32[2,72,128]{2,1,0:T(8,128)S(1)}, f32[2,72,128]{2,1,0:T(8,128)S(1)}, u32[]{:S(2)}, u32[]{:S(2)}) collective-permute-start(f32[2,72,128]{2,1,0:T(8,128)S(1)} %shard_map.98), channel_id=1, source_target_pairs={{0,8},{1,9},{2,10},{3,11},{4,12},{5,13},{6,14},{7,15},{8,0},{9,1},... | collective-permute-start | bytes 221192 | tf_op jit(solution)/shard_map/ppermute | solution.py:659
  66.0 2.0 %collective-permute-done.10 = f32[2,72,128]{2,1,0:T(8,128)S(1)} collective-permute-done((f32[2,72,128]{2,1,0:T(8,128)S(1)}, f32[2,72,128]{2,1,0:T(8,128)S(1)}, u32[]{:S(2)}, u32[]{:S(2)}) %collective-permute-start.10) | collective-permute-done | bytes 73760 | tf_op jit(solution)/shard_map/ppermute | solution.py:659
  68.1 1.3 %collective-permute-done.9 = f32[2,72,128]{2,1,0:T(8,128)S(1)} collective-permute-done((f32[2,72,128]{2,1,0:T(8,128)S(1)}, f32[2,72,128]{2,1,0:T(8,128)S(1)}, u32[]{:S(2)}, u32[]{:S(2)}) %collective-permute-start.9) | collective-permute-done | bytes 73760 | tf_op jit(solution)/shard_map/ppermute | solution.py:659
  69.4 0.0 collective-permute-done.8
  69.4 1.3 %shard_map.99 = f32[12,6144]{1,0:T(8,128)} custom-call(f32[2,3,24,128]{3,2,1,0:T(8,128)S(1)} %bitcast.8, f32[2,3,24,128]{3,2,1,0:T(8,128)S(1)} %bitcast.11, f32[2,3,24,128]{3,2,1,0:T(8,128)S(1)} %bitcast.10, f32[2,3,24,128]{3,2,1,0:T(8,128)S(1)} %bitcast.9), custom_call_target="tpu_custom_call" | custom-call | tf_op jit(solution)/shard_map/pallas_call | solution.py:639
  (2 shorter events, 0.1 us)
Async XLA Ops:
  0.6 9.9 %copy-start.6 = (s32[2]{0:T(128)S(1)}, s32[2]{0:T(128)}, u32[]{:S(2)}) copy-start(s32[2]{0:T(128)} %len_ref.5) | copy-start | bytes 28
  0.6 9.9 %copy-start = (bf16[2,3,48,16,128]{4,3,2,1,0:T(8,128)(2,1)S(1)}, bf16[2,3,48,16,128]{4,3,2,1,0:T(8,128)(2,1)}, u32[]{:S(2)}) copy-start(bf16[2,3,48,16,128]{4,3,2,1,0:T(8,128)(2,1)} %seed_in.5) | copy-start | bytes 3538948
  0.7 9.9 %copy-start.8 = (f32[2,128]{1,0:T(2,128)S(1)}, f32[2,128]{1,0:T(2,128)}, u32[]{:S(2)}) copy-start(f32[2,128]{1,0:T(2,128)} %cz_ref.5) | copy-start | bytes 3076
  0.7 9.9 %copy-start.7 = (f32[2,48]{1,0:T(2,128)S(1)}, f32[2,48]{1,0:T(2,128)}, u32[]{:S(2)}) copy-start(f32[2,48]{1,0:T(2,128)} %cx_ref.5) | copy-start | bytes 1156
  3.2 16.9 %all-to-all-start = ((f32[8,72,128]{2,1,0:T(8,128)}), f32[8,72,128]{2,1,0:T(8,128)S(1)}, u32[]{:S(2)}, u32[]{:S(2)}) async-start(f32[8,72,128]{2,1,0:T(8,128)} %pack.1), calls=%async_computation | async-start | bytes 589824 | tf_op jit(solution)/shard_map/all_to_all | solution.py:563
  10.5 1.1 %copy-start.3 = (f32[2,48,16,128]{3,2,1,0:T(8,128)S(1)}, f32[2,48,16,128]{3,2,1,0:T(8,128)}, u32[]{:S(2)}) copy-start(f32[2,48,16,128]{3,2,1,0:T(8,128)} %stiff_in.3) | copy-start | bytes 2359300
  21.0 12.1 %all-to-all-start.1 = ((f32[8,64,128]{2,1,0:T(8,128)}), f32[8,64,128]{2,1,0:T(8,128)S(1)}, u32[]{:S(2)}, u32[]{:S(2)}) async-start(f32[8,64,128]{2,1,0:T(8,128)} %route.1), calls=%async_computation.1 | async-start | bytes 524288 | tf_op jit(solution)/shard_map/all_to_all | solution.py:607
  24.6 8.5 %copy-start.4 = (s32[2,3]{1,0:T(2,128)S(1)}, s32[2,3]{1,0:T(2,128)}, u32[]{:S(2)}) copy-start(s32[2,3]{1,0:T(2,128)} %low_ref.1) | copy-start | bytes 76
  24.6 8.5 %copy-start.5 = (s32[2,3]{1,0:T(2,128)S(1)}, s32[2,3]{1,0:T(2,128)}, u32[]{:S(2)}) copy-start(s32[2,3]{1,0:T(2,128)} %up_ref.1) | copy-start | bytes 76
  30.0 0.9 %copy-start.1 = (f32[1632,128]{1,0:T(8,128)}, f32[1632,128]{1,0:T(8,128)S(1)}, u32[]{:S(2)}) copy-start(f32[1632,128]{1,0:T(8,128)S(1)} %get-tuple-element.36.part_1) | copy-start | bytes 2506756
  30.9 4.5 %copy-start.9 = (f32[2,16]{1,0:T(2,128)S(1)}, f32[2,16]{1,0:T(2,128)}, u32[]{:S(2)}) copy-start(f32[2,16]{1,0:T(2,128)} %cy_ref.1) | copy-start | bytes 388
  33.1 2.3 %copy-start.2 = (f32[1632,128]{1,0:T(8,128)S(1)}, f32[1632,128]{1,0:T(8,128)}, u32[]{:S(2)}) copy-start(f32[1632,128]{1,0:T(8,128)} %copy-done.1) | copy-start | bytes 2506756
  36.9 2.9 %collective-permute-start = (f32[8,2,2,3,24,128]{5,4,3,2,1,0:T(8,128)S(1)}, f32[8,2,2,3,24,128]{5,4,3,2,1,0:T(8,128)S(1)}, u32[]{:S(2)}, u32[]{:S(2)}) collective-permute-start(f32[8,2,2,3,24,128]{5,4,3,2,1,0:T(8,128)S(1)} %get-tuple-element.39), channel_id=1, source_target_pairs={{0,8},{1,9},{2,10},{3,11},{4,12},{5,13},{6,14},{7,15},{8,0},{9,1},... | collective-permute-start | bytes 3538952 | tf_op jit(solution)/shard_map/ppermute | solution.py:659
  39.9 9.1 %collective-permute-start.1 = (f32[4,2,72,128]{3,2,1,0:T(8,128)S(1)}, f32[4,2,72,128]{3,2,1,0:T(8,128)S(1)}, u32[]{:S(2)}, u32[]{:S(2)}) collective-permute-start(f32[4,2,72,128]{3,2,1,0:T(8,128)S(1)} %get-tuple-element.41), channel_id=1, source_target_pairs={{0,1},{1,0},{2,3},{3,2},{4,5},{5,4},{6,7},{7,6},{8,9},{9,8},{10,11... | collective-permute-start | bytes 884744 | tf_op jit(solution)/shard_map/ppermute | solution.py:659
  41.4 8.8 %collective-permute-start.2 = (f32[4,2,72,128]{3,2,1,0:T(8,128)S(1)}, f32[4,2,72,128]{3,2,1,0:T(8,128)S(1)}, u32[]{:S(2)}, u32[]{:S(2)}) collective-permute-start(f32[4,2,72,128]{3,2,1,0:T(8,128)S(1)} %get-tuple-element.43), channel_id=1, source_target_pairs={{0,16},{1,17},{2,18},{3,19},{4,20},{5,21},{6,22},{7,23},{8,24},{9,... | collective-permute-start | bytes 884744 | tf_op jit(solution)/shard_map/ppermute | solution.py:659
  50.3 5.2 %collective-permute-start.3 = (f32[4,72,128]{2,1,0:T(8,128)S(1)}, f32[4,72,128]{2,1,0:T(8,128)S(1)}, u32[]{:S(2)}, u32[]{:S(2)}) collective-permute-start(f32[4,72,128]{2,1,0:T(8,128)S(1)} %get-tuple-element.45), channel_id=1, source_target_pairs={{0,16},{1,17},{2,18},{3,19},{4,20},{5,21},{6,22},{7,23},{8,24},{9,... | collective-permute-start | bytes 442376 | tf_op jit(solution)/shard_map/ppermute | solution.py:659
  51.8 5.1 %collective-permute-start.4 = (f32[4,72,128]{2,1,0:T(8,128)S(1)}, f32[4,72,128]{2,1,0:T(8,128)S(1)}, u32[]{:S(2)}, u32[]{:S(2)}) collective-permute-start(f32[4,72,128]{2,1,0:T(8,128)S(1)} %get-tuple-element.47), channel_id=1, source_target_pairs={{0,1},{1,0},{2,3},{3,2},{4,5},{5,4},{6,7},{7,6},{8,9},{9,8},{10,11... | collective-permute-start | bytes 442376 | tf_op jit(solution)/shard_map/ppermute | solution.py:659
  57.0 6.3 %collective-permute-start.5 = (f32[2,72,128]{2,1,0:T(8,128)S(1)}, f32[2,72,128]{2,1,0:T(8,128)S(1)}, u32[]{:S(2)}, u32[]{:S(2)}) collective-permute-start(f32[2,72,128]{2,1,0:T(8,128)S(1)} %get-tuple-element.49), channel_id=1, source_target_pairs={{0,2},{1,3},{2,4},{3,5},{4,6},{5,7},{6,0},{7,1},{8,10},{9,11},{10,... | collective-permute-start | bytes 221192 | tf_op jit(solution)/shard_map/ppermute | solution.py:659
  57.2 6.1 %collective-permute-start.6 = (f32[2,72,128]{2,1,0:T(8,128)S(1)}, f32[2,72,128]{2,1,0:T(8,128)S(1)}, u32[]{:S(2)}, u32[]{:S(2)}) collective-permute-start(f32[2,72,128]{2,1,0:T(8,128)S(1)} %get-tuple-element.50), channel_id=1, source_target_pairs={{0,4},{1,5},{2,6},{3,7},{4,0},{5,1},{6,2},{7,3},{8,12},{9,13},{10,... | collective-permute-start | bytes 221192 | tf_op jit(solution)/shard_map/ppermute | solution.py:659
  59.2 4.8 %collective-permute-start.7 = (f32[2,72,128]{2,1,0:T(8,128)S(1)}, f32[2,72,128]{2,1,0:T(8,128)S(1)}, u32[]{:S(2)}, u32[]{:S(2)}) collective-permute-start(f32[2,72,128]{2,1,0:T(8,128)S(1)} %get-tuple-element.51), channel_id=1, source_target_pairs={{0,6},{1,7},{2,0},{3,1},{4,2},{5,3},{6,4},{7,5},{8,14},{9,15},{10,... | collective-permute-start | bytes 221192 | tf_op jit(solution)/shard_map/ppermute | solution.py:659
  64.1 4.0 %collective-permute-start.10 = (f32[2,72,128]{2,1,0:T(8,128)S(1)}, f32[2,72,128]{2,1,0:T(8,128)S(1)}, u32[]{:S(2)}, u32[]{:S(2)}) collective-permute-start(f32[2,72,128]{2,1,0:T(8,128)S(1)} %shard_map.98), channel_id=1, source_target_pairs={{0,24},{1,25},{2,26},{3,27},{4,28},{5,29},{6,30},{7,31},{8,16},{9,... | collective-permute-start | bytes 221192 | tf_op jit(solution)/shard_map/ppermute | solution.py:659
  64.2 5.2 %collective-permute-start.9 = (f32[2,72,128]{2,1,0:T(8,128)S(1)}, f32[2,72,128]{2,1,0:T(8,128)S(1)}, u32[]{:S(2)}, u32[]{:S(2)}) collective-permute-start(f32[2,72,128]{2,1,0:T(8,128)S(1)} %shard_map.98), channel_id=1, source_target_pairs={{0,16},{1,17},{2,18},{3,19},{4,20},{5,21},{6,22},{7,23},{8,24},{9,... | collective-permute-start | bytes 221192 | tf_op jit(solution)/shard_map/ppermute | solution.py:659
  64.7 4.7 %collective-permute-start.8 = (f32[2,72,128]{2,1,0:T(8,128)S(1)}, f32[2,72,128]{2,1,0:T(8,128)S(1)}, u32[]{:S(2)}, u32[]{:S(2)}) collective-permute-start(f32[2,72,128]{2,1,0:T(8,128)S(1)} %shard_map.98), channel_id=1, source_target_pairs={{0,8},{1,9},{2,10},{3,11},{4,12},{5,13},{6,14},{7,15},{8,0},{9,1},... | collective-permute-start | bytes 221192 | tf_op jit(solution)/shard_map/ppermute | solution.py:659
